TPU v7x, 256 devices: a whole 4x4x8 slice. The times are simulated.
256 devices in a mesh: dof: 128 (over z_hi, x, y, core), mode: 2 (over z_lo).
Axes of the slice: x: 4, y: 4, z: 8 (z_hi: 4, z_lo: 2; z = z_hi * 2 + z_lo), core: 2. Of those that a mesh axis runs over, the one named last changes fastest.
Arguments:
- stiffness_tiles: bfloat16 [4096, 10, 128, 128], P('dof'), may hold values from -0.15625 to 0.15625
- tile_cols: int32 [4096, 10], P('dof'), may hold values from 0 to 47, as said below
- send_rows: int32 [256, 8], P('dof'), may hold values from 0 to 31, as said below
- block: bfloat16 [524288, 128], P('dof', 'mode'), may hold values from -51 to 51
- lower_bound: float32 [1], replicated, may hold values from -1.2 to -0.6
- upper_bound: float32 [1], replicated, may hold values from 0.4 to 0.9
Outputs:
- basis: bfloat16 [524288, 128], P('dof', 'mode')
- ritz: float32 [128, 128], replicated
Inputs may be any that keep to these rules, and one draw needn't show every extreme that they name: `tile_cols`: entry 0 of every tile row is that row's own local index; entry 1 is a code of the lower neighbour's upward list and entry 2 a code of the upper neighbour's downward list. A code below 32 is a tile row of the same partition; 32 + s is slot s of the lower neighbour's upward list; 40 + s is slot s of the upper neighbour's downward list. `send_rows`: rows 2 p and 2 p + 1 hold distinct local tile rows of partition p: its downward and upward send lists.
All inputs are finite; a program needn't handle non-finite values.
Results may differ from a plain program's by a relative error of at most 0.0086.
Values may be sent and summed in bfloat16 or wider, within the bound.
No kernel may reach another device: no remote copies, remote signals or barrier semaphores. Data moves between devices by JAX's collectives and lax.ppermute only.
A program may use at most 64 MiB of HBM per device.

v0:
```python
import functools

import jax
import jax.numpy as jnp
from jax import lax
from jax.sharding import Mesh
from jax.sharding import PartitionSpec as P

DOF = ("dof_0", "dof_1", "dof_2", "dof_3")
DOF_MODE = ("dof_0", "dof_1", "dof_2", "dof_3", "mode")


def shifted(block, axis, distance):
    devices = range(lax.axis_size(axis))
    route = [(i - distance, i) for i in devices if i - distance in devices]
    return lax.ppermute(block, axis, route)


def by_axis(shard, axes):
    return functools.reduce(lax.psum, axes, shard)


def reduce_factor(gram_matrix, projected):
    factor = jnp.linalg.cholesky(gram_matrix)
    identity = jnp.eye(gram_matrix.shape[0], dtype=jnp.float32)
    inverse = jax.scipy.linalg.solve_triangular(factor, identity, lower=True)
    ritz_matrix = jnp.dot(
        jnp.dot(inverse, projected, precision=lax.Precision.HIGHEST),
        inverse.T,
        precision=lax.Precision.HIGHEST,
    )
    return (ritz_matrix, inverse.T.astype(jnp.bfloat16))


def shards(stiffness_tiles, tile_cols, send_rows, block, lower_bound, upper_bound):
    row_count, mode_cols = block.shape
    row_tiles = stiffness_tiles.shape[0]
    tile_size = stiffness_tiles.shape[2]
    dof_total = row_count * lax.axis_size(DOF)
    center = (upper_bound[0] + lower_bound[0]) * 0.5
    half_width = (upper_bound[0] - lower_bound[0]) * 0.5

    def apply_stiffness(field):
        field_cube = field.reshape(row_tiles, tile_size, mode_cols)
        upward = field_cube[send_rows[1]]
        downward = field_cube[send_rows[0]]
        from_lower = shifted(upward, DOF, 1)
        from_upper = shifted(downward, DOF, -1)
        extended = jnp.concatenate([field_cube, from_lower, from_upper], axis=0)
        picked = extended[tile_cols]
        result = jnp.einsum(
            "rkij,rkjm->rim", stiffness_tiles, picked, preferred_element_type=jnp.float32
        )
        return result.reshape(row_count, mode_cols)

    previous = block
    current = ((apply_stiffness(block) - center * block.astype(jnp.float32)) / half_width).astype(
        jnp.bfloat16
    )
    following = (
        2.0 * (apply_stiffness(current) - center * current.astype(jnp.float32)) / half_width
        - previous.astype(jnp.float32)
    ).astype(jnp.bfloat16)
    previous, current = (current, following)
    image_block = apply_stiffness(current).astype(jnp.bfloat16)
    row_half, image_half = (
        lax.all_to_all(current, "mode", split_axis=0, concat_axis=1, tiled=True),
        lax.all_to_all(image_block, "mode", split_axis=0, concat_axis=1, tiled=True),
    )
    gram_part = jnp.dot(row_half.T, row_half, preferred_element_type=jnp.float32)
    proj_part = jnp.dot(row_half.T, image_half, preferred_element_type=jnp.float32)
    gram_matrix, projected = (by_axis(gram_part, DOF_MODE), by_axis(proj_part, DOF_MODE))
    ritz_matrix, right_factor = reduce_factor(gram_matrix / dof_total, projected / dof_total)
    basis_rows = jnp.dot(row_half, right_factor, preferred_element_type=jnp.float32).astype(
        jnp.bfloat16
    )
    basis_out = lax.all_to_all(basis_rows, "mode", split_axis=1, concat_axis=0, tiled=True)
    return (basis_out, ritz_matrix)


def solution(mesh):
    torus = Mesh(
        mesh.devices.reshape(4, 4, 4, 2, mesh.shape["mode"]),
        ("dof_0", "dof_1", "dof_2", "dof_3", "mode"),
    )
    return jax.shard_map(
        shards,
        mesh=torus,
        in_specs=(P(DOF, None, None, None), P(DOF, None), P(DOF, None), P(DOF, "mode"), P(), P()),
        out_specs=(P(DOF, "mode"), P()),
        check_vma=False,
    )
```

profile of v0, /device:TPU:1, one launch (start us, length us, event | category | flops | bytes accessed | tf_op | source)
XLA Modules:
  0.0 402.3 jit_solution(14474696328640916857)
XLA Ops:
  7.9 1.2 copy_bitcast_fusion.3
  9.7 4.6 %collective-permute-start = (bf16[8,128,64]{1,2,0:T(8,128)(2,1)S(1)}, bf16[8,128,64]{1,2,0:T(8,128)(2,1)S(1)}, u32[]{:S(2)}, u32[]{:S(2)}) collective-permute-start(bf16[8,128,64]{1,2,0:T(8,128)(2,1)S(1)} %gather_fusion), channel_id=1, source_target_pairs={{0,2},{2,4},{4,6},{6,8},{8,10},{10,12},{12,14},{14,16},{16,18},{18... | collective-permute-start | bytes 393224 | tf_op jit(solution)/shard_map/ppermute | solution.py:16
  14.9 1.9 collective-permute-start.1
  19.0 2.1 collective-permute-done.1
  21.3 13.3 %gather_fusion.2 = bf16[320,128,64]{1,2,0:T(8,128)(2,1)} fusion(bf16[48,128,64]{1,2,0:T(8,128)(2,1)S(1)} %pad_maximum_fusion, s32[1024]{0:T(1024)S(1)} %pad_clamp_fusion), kind=kCustom, calls=%fused_computation.2 | custom fusion | bytes 10487040 | tf_op jit(solution)/shard_map/gather | solution.py:50
  34.6 9.2 %convolution_bitcast_fusion.2 = f32[32,8,8,128]{3,2,1,0:T(8,128)S(1)} fusion(bf16[32,10,128,64]{2,3,1,0:T(8,128)(2,1)} %bitcast.99, bf16[32,10,128,128]{3,2,1,0:T(8,128)(2,1)} %param.6), kind=kOutput, calls=%fused_computation.12 | convolution fusion | flops 671088640 | bytes 16777216 | tf_op jit(solution)/shard_map/rkij,rkjm->rim/dot_general | solution.py:51
  45.4 1.9 collective-permute-start.2
  47.3 2.6 collective-permute-start.3
  49.9 3.7 collective-permute-done.3
  53.7 13.3 %gather_fusion.5 = bf16[320,128,64]{1,2,0:T(8,128)(2,1)} fusion(bf16[48,128,64]{1,2,0:T(8,128)(2,1)S(1)} %pad_maximum_fusion.1, s32[1024]{0:T(1024)S(1)} %pad_clamp_fusion), kind=kCustom, calls=%fused_computation.5 | custom fusion | bytes 10487040 | tf_op jit(solution)/shard_map/gather | solution.py:50
  67.0 9.2 %convolution_bitcast_fusion.1 = f32[32,8,8,128]{3,2,1,0:T(8,128)S(1)} fusion(bf16[32,10,128,64]{2,3,1,0:T(8,128)(2,1)} %bitcast.100, bf16[32,10,128,128]{3,2,1,0:T(8,128)(2,1)} %param.6), kind=kOutput, calls=%fused_computation.11 | convolution fusion | flops 671088640 | bytes 16777216 | tf_op jit(solution)/shard_map/rkij,rkjm->rim/dot_general | solution.py:51
  77.8 1.9 collective-permute-start.4
  79.7 2.4 collective-permute-start.5
  83.0 3.7 all-to-all-start
  86.8 13.3 %gather_fusion.8 = bf16[320,128,64]{1,2,0:T(8,128)(2,1)} fusion(bf16[48,128,64]{1,2,0:T(8,128)(2,1)S(1)} %pad_maximum_fusion.2, s32[1024]{0:T(1024)S(1)} %pad_clamp_fusion), kind=kCustom, calls=%fused_computation.8 | custom fusion | bytes 10487040 | tf_op jit(solution)/shard_map/gather | solution.py:50
  100.2 9.2 %fusion.1 = bf16[32,128,64]{1,2,0:T(8,128)(2,1)S(1)} fusion(bf16[32,10,128,64]{2,3,1,0:T(8,128)(2,1)} %bitcast.98, bf16[32,10,128,128]{3,2,1,0:T(8,128)(2,1)} %param.6), kind=kOutput, calls=%fused_computation.16 | convolution fusion | flops 671350784 | bytes 16252928 | tf_op jit(solution)/shard_map/rkij,rkjm->rim/dot_general | solution.py:51
  109.9 1.0 copy.59
  110.8 3.5 all-to-all-start.2
  114.4 0.9 fusion.19
  115.3 7.1 %all-to-all-done.2 = bf16[2,2048,64]{1,2,0:T(8,128)(2,1)S(1)} async-done(((bf16[2,2048,64]{1,2,0:T(8,128)(2,1)}), bf16[2,2048,64]{1,2,0:T(8,128)(2,1)S(1)}, u32[]{:S(2)}, u32[]{:S(2)}) %all-to-all-start.2) | async-done | bytes 524320 | tf_op jit(solution)/shard_map/all_to_all | solution.py:68
  122.4 0.9 fusion.20
  123.4 67.8 %all-reduce.15.cloned.1.call-done = (f32[128,128]{0,1:T(8,128)}, f32[128,128]{0,1:T(8,128)}) async-done(((f32[128,128]{0,1:T(8,128)}, f32[128,128]{0,1:T(8,128)}), (f32[128,128]{0,1:T(8,128)}, f32[128,128]{0,1:T(8,128)})) %all-reduce.15.cloned.1.call-update) | async-done | bytes 131088 | tf_op jit(solution)/shard_map/psum | solution.py:20
  191.3 47.6 %all-reduce.13.cloned.1.call-done = (f32[128,128]{0,1:T(8,128)}, f32[128,128]{0,1:T(8,128)}) async-done(((f32[128,128]{0,1:T(8,128)}, f32[128,128]{0,1:T(8,128)}), (f32[128,128]{0,1:T(8,128)}, f32[128,128]{0,1:T(8,128)})) %all-reduce.13.cloned.1.call-update) | async-done | bytes 131088 | tf_op jit(solution)/shard_map/psum | solution.py:20
  239.0 49.3 %all-reduce.11.cloned.1.call-done = (f32[128,128]{0,1:T(8,128)}, f32[128,128]{0,1:T(8,128)}) async-done(((f32[128,128]{0,1:T(8,128)}, f32[128,128]{0,1:T(8,128)}), (f32[128,128]{0,1:T(8,128)}, f32[128,128]{0,1:T(8,128)})) %all-reduce.11.cloned.1.call-update) | async-done | bytes 131088 | tf_op jit(solution)/shard_map/psum | solution.py:20
  288.5 34.3 %all-reduce.19.cloned.1.call-done = (f32[128,128]{0,1:T(8,128)}, f32[128,128]{0,1:T(8,128)}) async-done(((f32[128,128]{0,1:T(8,128)}, f32[128,128]{0,1:T(8,128)}), (f32[128,128]{0,1:T(8,128)}, f32[128,128]{0,1:T(8,128)})) %all-reduce.19.cloned.1.call-update) | async-done | bytes 131088 | tf_op jit(solution)/shard_map/psum | solution.py:20
  322.9 35.6 %all-reduce.17.cloned.1.call-done = (f32[128,128]{0,1:T(8,128)}, f32[128,128]{0,1:T(8,128)}) async-done(((f32[128,128]{0,1:T(8,128)}, f32[128,128]{0,1:T(8,128)}), (f32[128,128]{0,1:T(8,128)}, f32[128,128]{0,1:T(8,128)})) %all-reduce.17.cloned.1.call-update) | async-done | bytes 131088 | tf_op jit(solution)/shard_map/psum | solution.py:20
  360.3 11.7 %cholesky.17 = f32[128,128]{1,0:T(8,128)S(1)} custom-call(f32[128,128]{1,0:T(8,128)S(1)} %fusion.11), custom_call_target="Cholesky" | custom-call | tf_op jit(solution)/shard_map/jit(cholesky)/cholesky | solution.py:24
  373.4 9.8 %custom-call.7 = f32[1,128,128]{1,2,0:T(8,128)S(1)} custom-call(f32[1,128,128]{2,1,0:T(8,128)S(1)} %fusion.8), custom_call_target="InvertDiagBlocksLowerTriangular" | custom-call | tf_op jit(solution)/shard_map/jit(_solve_triangular)/triangular_solve | solution.py:26
  383.5 1.1 convolution_convert_fusion
  384.5 3.5 all-to-all-start.1
  388.0 1.1 fusion.12
  390.1 4.8 %all-to-all-done.1 = bf16[2048,2,64]{0,2,1:T(8,128)(2,1)S(1)} async-done(((bf16[2048,2,64]{0,2,1:T(8,128)(2,1)}), bf16[2048,2,64]{0,2,1:T(8,128)(2,1)S(1)}, u32[]{:S(2)}, u32[]{:S(2)}) %all-to-all-start.1) | async-done | bytes 524320 | tf_op jit(solution)/shard_map/all_to_all | solution.py:77
  (49 shorter events, 13.1 us)
Async XLA Ops:
  9.7 9.3 %collective-permute-start = (bf16[8,128,64]{1,2,0:T(8,128)(2,1)S(1)}, bf16[8,128,64]{1,2,0:T(8,128)(2,1)S(1)}, u32[]{:S(2)}, u32[]{:S(2)}) collective-permute-start(bf16[8,128,64]{1,2,0:T(8,128)(2,1)S(1)} %gather_fusion), channel_id=1, source_target_pairs={{0,2},{2,4},{4,6},{6,8},{8,10},{10,12},{12,14},{14,16},{16,18},{18... | collective-permute-start | bytes 393224 | tf_op jit(solution)/shard_map/ppermute | solution.py:16
  14.9 6.3 %collective-permute-start.1 = (bf16[8,128,64]{1,2,0:T(8,128)(2,1)S(1)}, bf16[8,128,64]{1,2,0:T(8,128)(2,1)S(1)}, u32[]{:S(2)}, u32[]{:S(2)}) collective-permute-start(bf16[8,128,64]{1,2,0:T(8,128)(2,1)S(1)} %gather_fusion.1), channel_id=1, source_target_pairs={{2,0},{4,2},{6,4},{8,6},{10,8},{12,10},{14,12},{16,14},{18,16},{20... | collective-permute-start | bytes 393224 | tf_op jit(solution)/shard_map/ppermute | solution.py:16
  34.6 9.3 %copy-start = (bf16[4096,64]{0,1:T(8,128)(2,1)S(1)}, bf16[4096,64]{0,1:T(8,128)(2,1)}, u32[]{:S(2)}) copy-start(bf16[4096,64]{0,1:T(8,128)(2,1)} %param.9) | copy-start | bytes 1572868
  45.4 4.5 %collective-permute-start.2 = (bf16[8,128,64]{1,2,0:T(8,128)(2,1)S(1)}, bf16[8,128,64]{1,2,0:T(8,128)(2,1)S(1)}, u32[]{:S(2)}, u32[]{:S(2)}) collective-permute-start(bf16[8,128,64]{1,2,0:T(8,128)(2,1)S(1)} %gather_fusion.3), channel_id=1, source_target_pairs={{0,2},{2,4},{4,6},{6,8},{8,10},{10,12},{12,14},{14,16},{16,18},{18... | collective-permute-start | bytes 393224 | tf_op jit(solution)/shard_map/ppermute | solution.py:16
  47.3 6.3 %collective-permute-start.3 = (bf16[8,128,64]{1,2,0:T(8,128)(2,1)S(1)}, bf16[8,128,64]{1,2,0:T(8,128)(2,1)S(1)}, u32[]{:S(2)}, u32[]{:S(2)}) collective-permute-start(bf16[8,128,64]{1,2,0:T(8,128)(2,1)S(1)} %gather_fusion.4), channel_id=1, source_target_pairs={{2,0},{4,2},{6,4},{8,6},{10,8},{12,10},{14,12},{16,14},{18,16},{20... | collective-permute-start | bytes 393224 | tf_op jit(solution)/shard_map/ppermute | solution.py:16
  77.8 8.9 %collective-permute-start.4 = (bf16[8,128,64]{1,2,0:T(8,128)(2,1)S(1)}, bf16[8,128,64]{1,2,0:T(8,128)(2,1)S(1)}, u32[]{:S(2)}, u32[]{:S(2)}) collective-permute-start(bf16[8,128,64]{1,2,0:T(8,128)(2,1)S(1)} %gather_fusion.6), channel_id=1, source_target_pairs={{0,2},{2,4},{4,6},{6,8},{8,10},{10,12},{12,14},{14,16},{16,18},{18... | collective-permute-start | bytes 393224 | tf_op jit(solution)/shard_map/ppermute | solution.py:16
  79.7 7.0 %collective-permute-start.5 = (bf16[8,128,64]{1,2,0:T(8,128)(2,1)S(1)}, bf16[8,128,64]{1,2,0:T(8,128)(2,1)S(1)}, u32[]{:S(2)}, u32[]{:S(2)}) collective-permute-start(bf16[8,128,64]{1,2,0:T(8,128)(2,1)S(1)} %gather_fusion.7), channel_id=1, source_target_pairs={{2,0},{4,2},{6,4},{8,6},{10,8},{12,10},{14,12},{16,14},{18,16},{20... | collective-permute-start | bytes 393224 | tf_op jit(solution)/shard_map/ppermute | solution.py:16
  83.0 27.9 %all-to-all-start = ((bf16[2,2048,64]{1,2,0:T(8,128)(2,1)}), bf16[2,2048,64]{1,2,0:T(8,128)(2,1)S(1)}, u32[]{:S(2)}, u32[]{:S(2)}) async-start(bf16[2,2048,64]{1,2,0:T(8,128)(2,1)} %bitcast.97), calls=%async_computation | async-start | bytes 1048576 | tf_op jit(solution)/shard_map/all_to_all | solution.py:67
  110.8 11.6 %all-to-all-start.2 = ((bf16[2,2048,64]{1,2,0:T(8,128)(2,1)}), bf16[2,2048,64]{1,2,0:T(8,128)(2,1)S(1)}, u32[]{:S(2)}, u32[]{:S(2)}) async-start(bf16[2,2048,64]{1,2,0:T(8,128)(2,1)} %copy.59), calls=%async_computation.2 | async-start | bytes 1048576 | tf_op jit(solution)/shard_map/all_to_all | solution.py:68
  114.3 76.9 %all-reduce.15.cloned.1.call-start = ((), (), s32[]{:S(2)}) async-start(), calls=%async_computation.5 | async-start | bytes 262144 | tf_op jit(solution)/shard_map/psum | solution.py:20
  123.4 115.5 %all-reduce.13.cloned.1.call-start = ((), (), s32[]{:S(2)}) async-start(), calls=%async_computation.4 | async-start | bytes 262144 | tf_op jit(solution)/shard_map/psum | solution.py:20
  191.3 96.9 %all-reduce.11.cloned.1.call-start = ((), (), s32[]{:S(2)}) async-start(), calls=%async_computation.3 | async-start | bytes 262144 | tf_op jit(solution)/shard_map/psum | solution.py:20
  238.9 84.0 %all-reduce.19.cloned.1.call-start = ((), (), s32[]{:S(2)}) async-start(), calls=%async_computation.7 | async-start | bytes 262144 | tf_op jit(solution)/shard_map/psum | solution.py:20
  288.2 70.3 %all-reduce.17.cloned.1.call-start = ((), (), s32[]{:S(2)}) async-start(), calls=%async_computation.6 | async-start | bytes 262144 | tf_op jit(solution)/shard_map/psum | solution.py:20
  384.5 10.3 %all-to-all-start.1 = ((bf16[2048,2,64]{0,2,1:T(8,128)(2,1)}), bf16[2048,2,64]{0,2,1:T(8,128)(2,1)S(1)}, u32[]{:S(2)}, u32[]{:S(2)}) async-start(bf16[2048,2,64]{0,2,1:T(8,128)(2,1)} %bitcast.20), calls=%async_computation.1 | async-start | bytes 1048576 | tf_op jit(solution)/shard_map/all_to_all | solution.py:77
Sparse Core Ops, SparseCore 0:
  123.5 67.7 all-reduce.14
  193.8 45.0 all-reduce.12
  241.3 46.8 all-reduce.10
  290.8 31.9 all-reduce.18
  325.5 32.9 all-reduce.16
where the time goes:
time: 404 us; the launch traced here: 402 us
  waiting for transfers between devices  252 us (62%)
  local copies, waits for them, and re-layouts  48.2 us (12%)
  matrix products  32.9 us (8%)
  other arithmetic  26.7 us (7%)
  starting transfers between devices  26.5 us (7%)
  between operations  15.4 us (4%)
    psum x5, waiting for transfers between devices, by_axis(): return functools.reduce(lax.psum, axes, shard)  235 us
    gather x3, local copies, waits for them, and re-layouts, apply_stiffness(): picked = extended[tile_cols]  40 us
    dot_general x3, matrix products, apply_stiffness(): jnp.einsum('rkij,rkjm->rim', stiffness_tiles, picked, preferred_element_t...  27.7 us
    ppermute x6, starting transfers between devices, shifted(): return lax.ppermute(block, axis, route)  15.4 us
    another operation x3, other arithmetic, reduce_factor(): factor = jnp.linalg.cholesky(gram_matrix)  12.4 us
    another operation x2, other arithmetic, reduce_factor(): inverse = jax.scipy.linalg.solve_triangular(factor, identity, lower=True)  10.5 us
  transfers between devices with their start and end apart: 14, of which 9 were waited for; matrix products, arithmetic and copies ran while one was open for 7% of the time, Pallas kernels for 0%

commit v1 on v0

v1 whole, which is shorter than its diff:
```python
import functools

import jax
import jax.numpy as jnp
from jax import lax
from jax.experimental import pallas as pl
from jax.experimental.pallas import tpu as pltpu
from jax.sharding import Mesh
from jax.sharding import PartitionSpec as P

Z, X, Y, C, M = "dof_z", "dof_x", "dof_y", "dof_c", "mode"
DOF = (Z, X, Y, C)
VMEM = pl.BlockSpec(memory_space=pltpu.VMEM)
SMEM = pl.BlockSpec(memory_space=pltpu.SMEM)
NT = (((1,), (1,)), ((), ()))


def shifted(block, axis, distance):
    devices = range(lax.axis_size(axis))
    route = [(i - distance, i) for i in devices if i - distance in devices]
    return lax.ppermute(block, axis, route)


def flipped(block, axis, bits):
    return lax.ppermute(block, axis, [(i, i ^ bits) for i in range(lax.axis_size(axis))])


def copy_lists(send, field, up, down, tile):
    count = up.shape[1] // tile
    for slot in range(count):
        here = slice(slot * tile, (slot + 1) * tile)
        low = pl.multiple_of(send[slot] * tile, tile)
        high = pl.multiple_of(send[count + slot] * tile, tile)
        down[:, here] = field[:, pl.ds(low, tile)]
        up[:, here] = field[:, pl.ds(high, tile)]


def pick_lists(send_rows, field, tile):
    modes = field.shape[0]
    count = send_rows.shape[0] // 2
    part = jax.ShapeDtypeStruct((modes, count * tile), field.dtype)

    def kernel(send, field_ref, up, down):
        copy_lists(send, field_ref, up, down, tile)

    return pl.pallas_call(
        kernel,
        out_shape=(part, part),
        in_specs=[SMEM, VMEM],
        out_specs=(VMEM, VMEM),
        compiler_params=pltpu.CompilerParams(vmem_limit_bytes=8 << 20),
        name="pick_lists",
    )(send_rows, field)


def apply_operator(level, tiles, codes, send_rows, scales, field, previous, from_lower, from_upper):
    rows, nnz, tile, _ = tiles.shape
    modes, width = field.shape
    ghost = from_lower.shape[1]
    step_rows = 4
    lists = level < 3

    def kernel(*refs):
        codes, send, scales, tiles, field, *rest = refs
        if level == 2:
            previous, *rest = rest
        lower, upper, out, *rest = rest
        if lists:
            up, down, *rest = rest
        (extended,) = rest
        step = pl.program_id(0)

        @pl.when(step == 0)
        def _():
            extended[:, :width] = field[...]
            extended[:, width : width + ghost] = lower[...]
            extended[:, width + ghost :] = upper[...]

        center, factor = scales[0], scales[1]
        for sub in range(step_rows):
            row = step * step_rows + sub
            total = None
            for k in range(0, nnz, 2):
                sources = [
                    extended[:, pl.ds(pl.multiple_of(codes[row * nnz + k + i] * tile, tile), tile)]
                    for i in range(2)
                ]
                product = lax.dot_general(
                    jnp.concatenate(sources, axis=1),
                    jnp.concatenate([tiles[sub, k], tiles[sub, k + 1]], axis=1),
                    NT,
                    preferred_element_type=jnp.float32,
                )
                total = product if total is None else total + product
            here = pl.ds(pl.multiple_of(row * tile, tile), tile)
            if level < 3:
                total = (total - center * field[:, here].astype(jnp.float32)) * factor
            if level == 2:
                total = 2.0 * total - previous[:, here].astype(jnp.float32)
            out[:, here] = total.astype(out.dtype)

        if lists:

            @pl.when(step == pl.num_programs(0) - 1)
            def _():
                copy_lists(send, out, up, down, tile)

    operands = [codes, send_rows, scales, tiles, field]
    specs = [SMEM, SMEM, SMEM, pl.BlockSpec((step_rows, nnz, tile, tile), lambda i: (i, 0, 0, 0)), VMEM]
    if level == 2:
        operands.append(previous)
        specs.append(VMEM)
    operands += [from_lower, from_upper]
    specs += [VMEM, VMEM]
    shapes = [jax.ShapeDtypeStruct(field.shape, field.dtype)]
    if lists:
        shapes += [jax.ShapeDtypeStruct(from_lower.shape, field.dtype)] * 2
    return pl.pallas_call(
        kernel,
        grid=(rows // step_rows,),
        out_shape=shapes,
        in_specs=specs,
        out_specs=[VMEM] * len(shapes),
        scratch_shapes=[pltpu.VMEM((modes, width + 2 * ghost), field.dtype)],
        compiler_params=pltpu.CompilerParams(vmem_limit_bytes=16 << 20),
        cost_estimate=pl.CostEstimate(
            flops=2 * tiles.size * modes, bytes_accessed=tiles.size * 2, transcendentals=0
        ),
        name=f"apply_{level}",
    )(*operands)


def partial_sums(place, own, partner, image):
    modes, width = own.shape
    product = jax.ShapeDtypeStruct((modes, 2 * modes), jnp.float32)

    def kernel(place, own, partner, image, keep, send, both, left):
        mode, core = place[0], place[1]
        both[pl.ds(pl.multiple_of(mode * modes, modes), modes), :] = own[...]
        both[pl.ds(pl.multiple_of((1 - mode) * modes, modes), modes), :] = partner[...]
        left[pl.ds(pl.multiple_of(core * modes, modes), modes), :] = own[...]
        left[pl.ds(pl.multiple_of((1 - core) * modes, modes), modes), :] = image[...]
        sums = lax.dot_general(left[...], both[...], NT, preferred_element_type=jnp.float32)
        keep[...] = sums[:modes]
        send[...] = sums[modes:]

    return pl.pallas_call(
        kernel,
        out_shape=(product, product, jax.ShapeDtypeStruct((2 * modes, width), own.dtype)),
        in_specs=[SMEM, VMEM, VMEM, VMEM],
        out_specs=(VMEM, VMEM, VMEM),
        scratch_shapes=[pltpu.VMEM((2 * modes, width), own.dtype)],
        compiler_params=pltpu.CompilerParams(vmem_limit_bytes=16 << 20),
        name="partial_sums",
    )(place, own, partner, image)


def sum_over_chips(value):
    for axis in (X, Y, Z):
        others = [flipped(value, axis, bits) for bits in (1, 2, 3)]
        value = (value + others[0]) + (others[1] + others[2])
    return value


def reduce_factor(gram_matrix, projected):
    factor = jnp.linalg.cholesky(gram_matrix)
    identity = jnp.eye(gram_matrix.shape[0], dtype=jnp.float32)
    inverse = jax.scipy.linalg.solve_triangular(factor, identity, lower=True)
    ritz_matrix = jnp.dot(
        jnp.dot(inverse, projected, precision=lax.Precision.HIGHEST),
        inverse.T,
        precision=lax.Precision.HIGHEST,
    )
    return (ritz_matrix, inverse)


def shards(stiffness_tiles, tile_cols, send_rows, block, lower_bound, upper_bound):
    row_count, mode_cols = block.shape
    tile = stiffness_tiles.shape[2]
    dof_total = row_count * lax.axis_size(DOF)
    center = (upper_bound[0] + lower_bound[0]) * 0.5
    half_width = (upper_bound[0] - lower_bound[0]) * 0.5
    scales = jnp.stack([center, 1.0 / half_width])
    codes = tile_cols.reshape(-1)
    send = send_rows.reshape(-1)
    mode, core = lax.axis_index(M), lax.axis_index(C)
    place = jnp.stack([mode, core])

    def exchange(up, down):
        return shifted(up, DOF, 1), shifted(down, DOF, -1)

    apply = functools.partial(apply_operator, tiles=stiffness_tiles, codes=codes, send_rows=send, scales=scales)
    level_0 = block.T
    lower, upper = exchange(*pick_lists(send, level_0, tile))
    level_1, up, down = apply(1, field=level_0, previous=None, from_lower=lower, from_upper=upper)
    lower, upper = exchange(up, down)
    filtered, up, down = apply(2, field=level_1, previous=level_0, from_lower=lower, from_upper=upper)
    lower, upper = exchange(up, down)
    partner = flipped(filtered, M, 1)
    (image,) = apply(3, field=filtered, previous=None, from_lower=lower, from_upper=upper)
    keep, send_half, both = partial_sums(place, filtered, partner, image)
    half = sum_over_chips(keep + flipped(send_half, C, 1))
    others = [flipped(half, C, 1), flipped(half, M, 1), flipped(half, (C, M), 3)]
    same, swapped = (half, others[1]), (others[0], others[2])
    gram_rows = [jnp.where(core == 0, a, b) for a, b in zip(same, swapped)]
    proj_rows = [jnp.where(core == 0, b, a) for a, b in zip(same, swapped)]

    def in_order(rows):
        return jnp.where(mode == 0, jnp.concatenate(rows), jnp.concatenate(rows[::-1]))

    ritz_matrix, inverse = reduce_factor(in_order(gram_rows) / dof_total, in_order(proj_rows).T / dof_total)
    left = lax.dynamic_slice_in_dim(inverse, mode * mode_cols, mode_cols, 0).astype(jnp.bfloat16)
    basis = jnp.dot(left, both, preferred_element_type=jnp.float32).astype(jnp.bfloat16)
    return (basis.T, ritz_matrix)


def solution(mesh):
    torus = Mesh(mesh.devices.reshape(4, 4, 4, 2, mesh.shape["mode"]), DOF + (M,))
    return jax.shard_map(
        shards,
        mesh=torus,
        in_specs=(P(DOF, None, None, None), P(DOF, None), P(DOF, None), P(DOF, M), P(), P()),
        out_specs=(P(DOF, M), P()),
        check_vma=False,
    )
```

time: 404 us -> 147 us (0.36)
  waiting for transfers between devices: 252 us -> 26.8 us
  local copies, waits for them, and re-layouts: 48.2 us -> 11.9 us
  starting transfers between devices: 26.5 us -> 61.4 us
  matrix products: 32.9 us -> 2.53 us
  Pallas kernels: 0 us -> 18 us
  between operations: 15.4 us -> 2.2 us
    psum x5 -> x0, waiting for transfers between devices: 235 us -> none  [by_axis(): return functools.reduce(lax.psum, axes, shard)]
    ppermute x0 -> x14, starting transfers between devices: none -> 46.2 us  [flipped(): lax.ppermute(block, axis, [(i, i ^ bits) for i in range(lax.axis_size(axi...]
    gather x9 -> x0, local copies, waits for them, and re-layouts: 43.4 us -> none  [the longest x3 40 us: apply_stiffness(): picked = extended[tile_cols]]
    dot_general x6 -> x1, matrix products: 30.6 us -> 1.09 us  [shards(): jnp.dot(left, both, preferred_element_type=jnp.float32).astype(jnp.bfloat16)]
    pallas_call x0 -> x5, Pallas kernels: none -> 18 us  [the longest x3 16.3 us: apply_operator(): pl.pallas_call(kernel, grid=(rows // step_rows,), out_shape=shapes, in_sp...]
    ppermute x0 -> x14, waiting for transfers between devices: none -> 16.7 us  [flipped(): lax.ppermute(block, axis, [(i, i ^ bits) for i in range(lax.axis_size(axi...]
    all_to_all x3 -> x0, waiting for transfers between devices: 11.9 us -> none  [the longest x1 7.09 us: shards(): lax.all_to_all(image_block, 'mode', split_axis=0, concat_axis=1, tiled=True)]
    unnamed x2 -> x9, local copies, waits for them, and re-layouts: 0.01 us -> 10.8 us
  transfers between devices with their start and end apart: 14 -> 20, of which waited for: 9 -> 12; matrix products, arithmetic and copies ran while one was open for 7% -> 1% of each run, Pallas kernels for 0% -> 4%
where the time goes in v1:
time: 147 us; the launch traced here: 146 us
  starting transfers between devices  61.4 us (42%)
  waiting for transfers between devices  26.8 us (18%)
  other arithmetic  23.2 us (16%)
  Pallas kernels  18 us (12%)
  local copies, waits for them, and re-layouts  11.9 us (8%)
  matrix products  2.53 us (2%)
  between operations  2.2 us (1%)
    ppermute x14, starting transfers between devices, flipped(): lax.ppermute(block, axis, [(i, i ^ bits) for i in range(lax.axis_size(axi...  46.2 us
    ppermute x14, waiting for transfers between devices, flipped(): lax.ppermute(block, axis, [(i, i ^ bits) for i in range(lax.axis_size(axi...  16.7 us
    pallas_call x3, Pallas kernels, apply_operator(): pl.pallas_call(kernel, grid=(rows // step_rows,), out_shape=shapes, in_sp...  16.3 us
    ppermute x6, starting transfers between devices, shifted(): return lax.ppermute(block, axis, route)  15.2 us
    another operation x3, other arithmetic, reduce_factor(): factor = jnp.linalg.cholesky(gram_matrix)  12.4 us
    unnamed x9, local copies, waits for them, and re-layouts  10.8 us
    another operation x2, other arithmetic, reduce_factor(): inverse = jax.scipy.linalg.solve_triangular(factor, identity, lower=True)  10.5 us
    ppermute x6, waiting for transfers between devices, shifted(): return lax.ppermute(block, axis, route)  10.1 us
  transfers between devices with their start and end apart: 20, of which 12 were waited for; matrix products, arithmetic and copies ran while one was open for 1% of the time, Pallas kernels for 4%

profile of v1, /device:TPU:1, one launch (start us, length us, event | category | flops | bytes accessed | tf_op | source)
XLA Modules:
  0.0 146.1 jit_solution(13236063036709257093)
XLA Ops:
  3.1 4.6 %collective-permute-start = (bf16[64,1024]{1,0:T(8,128)(2,1)S(1)}, bf16[64,1024]{1,0:T(8,128)(2,1)S(1)}, u32[]{:S(2)}, u32[]{:S(2)}) collective-permute-start(bf16[64,1024]{1,0:T(8,128)(2,1)S(1)} %get-tuple-element.13), channel_id=1, source_target_pairs={{0,2},{2,4},{4,6},{6,8},{8,10},{10,12},{12,14},{14,16},{16,18},{18... | collective-permute-start | bytes 393224 | tf_op jit(solution)/shard_map/ppermute | solution.py:21
  7.7 1.9 %collective-permute-start.1 = (bf16[64,1024]{1,0:T(8,128)(2,1)S(1)}, bf16[64,1024]{1,0:T(8,128)(2,1)S(1)}, u32[]{:S(2)}, u32[]{:S(2)}) collective-permute-start(bf16[64,1024]{1,0:T(8,128)(2,1)S(1)} %get-tuple-element.14), channel_id=1, source_target_pairs={{2,0},{4,2},{6,4},{8,6},{10,8},{12,10},{14,12},{16,14},{18,16},{20... | collective-permute-start | bytes 393224 | tf_op jit(solution)/shard_map/ppermute | solution.py:21
  11.9 2.0 %collective-permute-done.1.refs_6_ = bf16[64,1024]{1,0:T(8,128)(2,1)S(1)} collective-permute-done((bf16[64,1024]{1,0:T(8,128)(2,1)S(1)}, bf16[64,1024]{1,0:T(8,128)(2,1)S(1)}, u32[]{:S(2)}, u32[]{:S(2)}) %collective-permute-start.1) | collective-permute-done | bytes 131104 | tf_op jit(solution)/shard_map/ppermute | solution.py:21
  13.9 4.0 %copy-done = bf16[32,10,128,128]{3,2,1,0:T(8,128)(2,1)S(1)} copy-done((bf16[32,10,128,128]{3,2,1,0:T(8,128)(2,1)S(1)}, bf16[32,10,128,128]{3,2,1,0:T(8,128)(2,1)}, u32[]{:S(2)}) %copy-start) | copy-done | bytes 10485784
  19.0 5.5 %apply_1.1 = (bf16[64,4096]{1,0:T(8,128)(2,1)S(1)}, bf16[64,1024]{1,0:T(8,128)(2,1)S(1)}, bf16[64,1024]{1,0:T(8,128)(2,1)S(1)}) custom-call(s32[320]{0:T(512)S(1)} %reshape.30.refs_0_, s32[16]{0:T(128)S(1)} %reshape.31.send.refs_1_, f32[2]{0:T(128)S(1)} %pad_maximum_fusion.refs_2_, bf16[32,10,128,128]{3,2,1,0:T(8,128)(2,1)S(1)} %copy-done, ...), custom_call_target="tpu_custom_call" | custom-call | flops 671088640 | bytes 10485760 | tf_op jit(solution)/shard_map/apply_1/pallas_call | solution.py:118
  24.5 1.9 %collective-permute-start.2 = (bf16[64,1024]{1,0:T(8,128)(2,1)S(1)}, bf16[64,1024]{1,0:T(8,128)(2,1)S(1)}, u32[]{:S(2)}, u32[]{:S(2)}) collective-permute-start(bf16[64,1024]{1,0:T(8,128)(2,1)S(1)} %get-tuple-element.16), channel_id=1, source_target_pairs={{0,2},{2,4},{4,6},{6,8},{8,10},{10,12},{12,14},{14,16},{16,18},{18... | collective-permute-start | bytes 393224 | tf_op jit(solution)/shard_map/ppermute | solution.py:21
  26.4 2.4 %collective-permute-start.3 = (bf16[64,1024]{1,0:T(8,128)(2,1)S(1)}, bf16[64,1024]{1,0:T(8,128)(2,1)S(1)}, u32[]{:S(2)}, u32[]{:S(2)}) collective-permute-start(bf16[64,1024]{1,0:T(8,128)(2,1)S(1)} %get-tuple-element.17), channel_id=1, source_target_pairs={{2,0},{4,2},{6,4},{8,6},{10,8},{12,10},{14,12},{16,14},{18,16},{20... | collective-permute-start | bytes 393224 | tf_op jit(solution)/shard_map/ppermute | solution.py:21
  28.8 3.9 %collective-permute-done.3.refs_7_ = bf16[64,1024]{1,0:T(8,128)(2,1)S(1)} collective-permute-done((bf16[64,1024]{1,0:T(8,128)(2,1)S(1)}, bf16[64,1024]{1,0:T(8,128)(2,1)S(1)}, u32[]{:S(2)}, u32[]{:S(2)}) %collective-permute-start.3) | collective-permute-done | bytes 131104 | tf_op jit(solution)/shard_map/ppermute | solution.py:21
  32.7 5.5 %apply_2.1 = (bf16[64,4096]{1,0:T(8,128)(2,1)S(1)}, bf16[64,1024]{1,0:T(8,128)(2,1)S(1)}, bf16[64,1024]{1,0:T(8,128)(2,1)S(1)}) custom-call(s32[320]{0:T(512)S(1)} %reshape.30.refs_0_, s32[16]{0:T(128)S(1)} %reshape.31.send.refs_1_, f32[2]{0:T(128)S(1)} %pad_maximum_fusion.refs_2_, bf16[32,10,128,128]{3,2,1,0:T(8,128)(2,1)S(1)} %copy-done, ...), custom_call_target="tpu_custom_call" | custom-call | flops 671088640 | bytes 10485760 | tf_op jit(solution)/shard_map/apply_2/pallas_call | solution.py:118
  38.2 1.7 %collective-permute-start.4 = (bf16[64,4096]{1,0:T(8,128)(2,1)S(1)}, bf16[64,4096]{1,0:T(8,128)(2,1)S(1)}, u32[]{:S(2)}, u32[]{:S(2)}) collective-permute-start(bf16[64,4096]{1,0:T(8,128)(2,1)S(1)} %get-tuple-element.18.refs_4_.own), channel_id=1, source_target_pairs={{0,1},{1,0},{2,3},{3,2},{4,5},{5,4},{6,7},{7,6},{8,9},{9,8},{10,11... | collective-permute-start | bytes 1572872 | tf_op jit(solution)/shard_map/ppermute | solution.py:25
  39.9 2.1 %collective-permute-start.5 = (bf16[64,1024]{1,0:T(8,128)(2,1)S(1)}, bf16[64,1024]{1,0:T(8,128)(2,1)S(1)}, u32[]{:S(2)}, u32[]{:S(2)}) collective-permute-start(bf16[64,1024]{1,0:T(8,128)(2,1)S(1)} %get-tuple-element.19), channel_id=1, source_target_pairs={{0,2},{2,4},{4,6},{6,8},{8,10},{10,12},{12,14},{14,16},{16,18},{18... | collective-permute-start | bytes 393224 | tf_op jit(solution)/shard_map/ppermute | solution.py:21
  42.0 2.3 %collective-permute-start.6 = (bf16[64,1024]{1,0:T(8,128)(2,1)S(1)}, bf16[64,1024]{1,0:T(8,128)(2,1)S(1)}, u32[]{:S(2)}, u32[]{:S(2)}) collective-permute-start(bf16[64,1024]{1,0:T(8,128)(2,1)S(1)} %get-tuple-element.20), channel_id=1, source_target_pairs={{2,0},{4,2},{6,4},{8,6},{10,8},{12,10},{14,12},{16,14},{18,16},{20... | collective-permute-start | bytes 393224 | tf_op jit(solution)/shard_map/ppermute | solution.py:21
  44.3 4.2 %collective-permute-done.6.refs_6_ = bf16[64,1024]{1,0:T(8,128)(2,1)S(1)} collective-permute-done((bf16[64,1024]{1,0:T(8,128)(2,1)S(1)}, bf16[64,1024]{1,0:T(8,128)(2,1)S(1)}, u32[]{:S(2)}, u32[]{:S(2)}) %collective-permute-start.6) | collective-permute-done | bytes 131104 | tf_op jit(solution)/shard_map/ppermute | solution.py:21
  48.5 4.0 %copy-done.1 = bf16[32,10,128,128]{3,2,1,0:T(8,128)(2,1)S(1)} copy-done((bf16[32,10,128,128]{3,2,1,0:T(8,128)(2,1)S(1)}, bf16[32,10,128,128]{3,2,1,0:T(8,128)(2,1)}, u32[]{:S(2)}) %copy-start.1) | copy-done | bytes 10485784
  52.5 5.4 %apply_3.1.image = bf16[64,4096]{1,0:T(8,128)(2,1)S(1)} custom-call(s32[320]{0:T(512)S(1)} %reshape.30.refs_0_, s32[16]{0:T(128)S(1)} %reshape.31.send.refs_1_, f32[2]{0:T(128)S(1)} %pad_maximum_fusion.refs_2_, bf16[32,10,128,128]{3,2,1,0:T(8,128)(2,1)S(1)} %copy-done.1, bf16[64,4096]{1,0:T(8,128)(2,1)S(1)} %get-tuple-element.18.refs_4_.own, ...), custom_call_target="tpu_custom_call" | custom-call | flops 671088640 | bytes 10485760 | tf_op jit(solution)/shard_map/apply_3/pallas_call | solution.py:118
  59.3 1.1 collective-permute-done.7
  60.4 6.9 %collective-permute-start.10 = (f32[64,128]{0,1:T(8,128)S(1)}, f32[64,128]{0,1:T(8,128)S(1)}, u32[]{:S(2)}, u32[]{:S(2)}) collective-permute-start(f32[64,128]{0,1:T(8,128)S(1)} %add.50), channel_id=1, source_target_pairs={{0,48},{16,32},{32,16},{48,0},{1,49},{17,33},{33,17},{49,1},{2,50}... | collective-permute-start | bytes 98312 | tf_op jit(solution)/shard_map/ppermute | solution.py:25
  67.4 1.3 collective-permute-start.9
  70.5 1.5 %collective-permute-done.9 = f32[64,128]{0,1:T(8,128)S(1)} collective-permute-done((f32[64,128]{0,1:T(8,128)S(1)}, f32[64,128]{0,1:T(8,128)S(1)}, u32[]{:S(2)}, u32[]{:S(2)}) %collective-permute-start.9) | collective-permute-done | bytes 32800 | tf_op jit(solution)/shard_map/ppermute | solution.py:25
  72.0 2.6 %collective-permute-start.11 = (f32[64,128]{0,1:T(8,128)S(1)}, f32[64,128]{0,1:T(8,128)S(1)}, u32[]{:S(2)}, u32[]{:S(2)}) collective-permute-start(f32[64,128]{0,1:T(8,128)S(1)} %add_add_fusion.2), channel_id=1, source_target_pairs={{0,4},{4,0},{8,12},{12,8},{1,5},{5,1},{9,13},{13,9},{2,6},{6,2},{1... | collective-permute-start | bytes 98312 | tf_op jit(solution)/shard_map/ppermute | solution.py:25
  74.6 15.8 %collective-permute-start.12 = (f32[64,128]{0,1:T(8,128)S(1)}, f32[64,128]{0,1:T(8,128)S(1)}, u32[]{:S(2)}, u32[]{:S(2)}) collective-permute-start(f32[64,128]{0,1:T(8,128)S(1)} %add_add_fusion.2), channel_id=1, source_target_pairs={{0,8},{4,12},{8,0},{12,4},{1,9},{5,13},{9,1},{13,5},{2,10},{6,14},... | collective-permute-start | bytes 98312 | tf_op jit(solution)/shard_map/ppermute | solution.py:25
  90.4 2.3 %collective-permute-done.12 = f32[64,128]{0,1:T(8,128)S(1)} collective-permute-done((f32[64,128]{0,1:T(8,128)S(1)}, f32[64,128]{0,1:T(8,128)S(1)}, u32[]{:S(2)}, u32[]{:S(2)}) %collective-permute-start.12) | collective-permute-done | bytes 32800 | tf_op jit(solution)/shard_map/ppermute | solution.py:25
  92.7 2.7 %collective-permute-done.13 = f32[64,128]{0,1:T(8,128)S(1)} collective-permute-done((f32[64,128]{0,1:T(8,128)S(1)}, f32[64,128]{0,1:T(8,128)S(1)}, u32[]{:S(2)}, u32[]{:S(2)}) %collective-permute-start.13) | collective-permute-done | bytes 32800 | tf_op jit(solution)/shard_map/ppermute | solution.py:25
  95.4 8.6 %collective-permute-start.14 = (f32[64,128]{0,1:T(8,128)S(1)}, f32[64,128]{0,1:T(8,128)S(1)}, u32[]{:S(2)}, u32[]{:S(2)}) collective-permute-start(f32[64,128]{0,1:T(8,128)S(1)} %add_add_fusion.1), channel_id=1, source_target_pairs={{0,64},{64,0},{128,192},{192,128},{1,65},{65,1},{129,193},{193,129... | collective-permute-start | bytes 98312 | tf_op jit(solution)/shard_map/ppermute | solution.py:25
  104.1 3.4 %collective-permute-start.16 = (f32[64,128]{0,1:T(8,128)S(1)}, f32[64,128]{0,1:T(8,128)S(1)}, u32[]{:S(2)}, u32[]{:S(2)}) collective-permute-start(f32[64,128]{0,1:T(8,128)S(1)} %add_add_fusion.1), channel_id=1, source_target_pairs={{0,192},{64,128},{128,64},{192,0},{1,193},{65,129},{129,65},{193,1... | collective-permute-start | bytes 98312 | tf_op jit(solution)/shard_map/ppermute | solution.py:25
  107.4 3.6 %collective-permute-done.15 = f32[64,128]{0,1:T(8,128)S(1)} collective-permute-done((f32[64,128]{0,1:T(8,128)S(1)}, f32[64,128]{0,1:T(8,128)S(1)}, u32[]{:S(2)}, u32[]{:S(2)}) %collective-permute-start.15) | collective-permute-done | bytes 32800 | tf_op jit(solution)/shard_map/ppermute | solution.py:25
  111.1 4.1 %collective-permute-start.17 = (f32[64,128]{0,1:T(8,128)S(1)}, f32[64,128]{0,1:T(8,128)S(1)}, u32[]{:S(2)}, u32[]{:S(2)}) collective-permute-start(f32[64,128]{0,1:T(8,128)S(1)} %add_add_fusion), channel_id=1, source_target_pairs={{0,2},{2,0},{1,3},{3,1},{4,6},{6,4},{5,7},{7,5},{8,10},{10,8},{9,1... | collective-permute-start | bytes 98312 | tf_op jit(solution)/shard_map/ppermute | solution.py:25
  115.2 1.7 %collective-permute-start.19 = (f32[64,128]{0,1:T(8,128)S(1)}, f32[64,128]{0,1:T(8,128)S(1)}, u32[]{:S(2)}, u32[]{:S(2)}) collective-permute-start(f32[64,128]{0,1:T(8,128)S(1)} %add_add_fusion), channel_id=1, source_target_pairs={{0,3},{1,2},{2,1},{3,0},{4,7},{5,6},{6,5},{7,4},{8,11},{9,10},{10,... | collective-permute-start | bytes 98312 | tf_op jit(solution)/shard_map/ppermute | solution.py:25
  117.0 1.9 %collective-permute-done.18 = f32[64,128]{0,1:T(8,128)S(1)} collective-permute-done((f32[64,128]{0,1:T(8,128)S(1)}, f32[64,128]{0,1:T(8,128)S(1)}, u32[]{:S(2)}, u32[]{:S(2)}) %collective-permute-start.18) | collective-permute-done | bytes 32800 | tf_op jit(solution)/shard_map/ppermute | solution.py:25
  118.9 1.6 %collective-permute-done.19 = f32[64,128]{0,1:T(8,128)S(1)} collective-permute-done((f32[64,128]{0,1:T(8,128)S(1)}, f32[64,128]{0,1:T(8,128)S(1)}, u32[]{:S(2)}, u32[]{:S(2)}) %collective-permute-start.19) | collective-permute-done | bytes 32800 | tf_op jit(solution)/shard_map/ppermute | solution.py:25
  120.7 11.7 %cholesky.17 = f32[128,128]{1,0:T(8,128)S(1)} custom-call(f32[128,128]{1,0:T(8,128)S(1)} %fusion.12), custom_call_target="Cholesky" | custom-call | tf_op jit(solution)/shard_map/jit(cholesky)/cholesky | solution.py:166
  133.8 9.8 %custom-call.7 = f32[1,128,128]{1,2,0:T(8,128)S(1)} custom-call(f32[1,128,128]{2,1,0:T(8,128)S(1)} %fusion), custom_call_target="InvertDiagBlocksLowerTriangular" | custom-call | tf_op jit(solution)/shard_map/jit(_solve_triangular)/triangular_solve | solution.py:168
  (46 shorter events, 11.9 us)
Async XLA Ops:
  1.4 1.0 copy-start.2
  3.1 8.8 %collective-permute-start = (bf16[64,1024]{1,0:T(8,128)(2,1)S(1)}, bf16[64,1024]{1,0:T(8,128)(2,1)S(1)}, u32[]{:S(2)}, u32[]{:S(2)}) collective-permute-start(bf16[64,1024]{1,0:T(8,128)(2,1)S(1)} %get-tuple-element.13), channel_id=1, source_target_pairs={{0,2},{2,4},{4,6},{6,8},{8,10},{10,12},{12,14},{14,16},{16,18},{18... | collective-permute-start | bytes 393224 | tf_op jit(solution)/shard_map/ppermute | solution.py:21
  7.7 6.3 %collective-permute-start.1 = (bf16[64,1024]{1,0:T(8,128)(2,1)S(1)}, bf16[64,1024]{1,0:T(8,128)(2,1)S(1)}, u32[]{:S(2)}, u32[]{:S(2)}) collective-permute-start(bf16[64,1024]{1,0:T(8,128)(2,1)S(1)} %get-tuple-element.14), channel_id=1, source_target_pairs={{2,0},{4,2},{6,4},{8,6},{10,8},{12,10},{14,12},{16,14},{18,16},{20... | collective-permute-start | bytes 393224 | tf_op jit(solution)/shard_map/ppermute | solution.py:21
  13.9 4.0 %copy-start = (bf16[32,10,128,128]{3,2,1,0:T(8,128)(2,1)S(1)}, bf16[32,10,128,128]{3,2,1,0:T(8,128)(2,1)}, u32[]{:S(2)}) copy-start(bf16[32,10,128,128]{3,2,1,0:T(8,128)(2,1)} %refs_3_.5) | copy-start | bytes 31457284
  17.9 1.0 copy-start.3
  24.5 4.3 %collective-permute-start.2 = (bf16[64,1024]{1,0:T(8,128)(2,1)S(1)}, bf16[64,1024]{1,0:T(8,128)(2,1)S(1)}, u32[]{:S(2)}, u32[]{:S(2)}) collective-permute-start(bf16[64,1024]{1,0:T(8,128)(2,1)S(1)} %get-tuple-element.16), channel_id=1, source_target_pairs={{0,2},{2,4},{4,6},{6,8},{8,10},{10,12},{12,14},{14,16},{16,18},{18... | collective-permute-start | bytes 393224 | tf_op jit(solution)/shard_map/ppermute | solution.py:21
  26.4 6.3 %collective-permute-start.3 = (bf16[64,1024]{1,0:T(8,128)(2,1)S(1)}, bf16[64,1024]{1,0:T(8,128)(2,1)S(1)}, u32[]{:S(2)}, u32[]{:S(2)}) collective-permute-start(bf16[64,1024]{1,0:T(8,128)(2,1)S(1)} %get-tuple-element.17), channel_id=1, source_target_pairs={{2,0},{4,2},{6,4},{8,6},{10,8},{12,10},{14,12},{16,14},{18,16},{20... | collective-permute-start | bytes 393224 | tf_op jit(solution)/shard_map/ppermute | solution.py:21
  38.2 19.7 %collective-permute-start.4 = (bf16[64,4096]{1,0:T(8,128)(2,1)S(1)}, bf16[64,4096]{1,0:T(8,128)(2,1)S(1)}, u32[]{:S(2)}, u32[]{:S(2)}) collective-permute-start(bf16[64,4096]{1,0:T(8,128)(2,1)S(1)} %get-tuple-element.18.refs_4_.own), channel_id=1, source_target_pairs={{0,1},{1,0},{2,3},{3,2},{4,5},{5,4},{6,7},{7,6},{8,9},{9,8},{10,11... | collective-permute-start | bytes 1572872 | tf_op jit(solution)/shard_map/ppermute | solution.py:25
  39.9 4.4 %collective-permute-start.5 = (bf16[64,1024]{1,0:T(8,128)(2,1)S(1)}, bf16[64,1024]{1,0:T(8,128)(2,1)S(1)}, u32[]{:S(2)}, u32[]{:S(2)}) collective-permute-start(bf16[64,1024]{1,0:T(8,128)(2,1)S(1)} %get-tuple-element.19), channel_id=1, source_target_pairs={{0,2},{2,4},{4,6},{6,8},{8,10},{10,12},{12,14},{14,16},{16,18},{18... | collective-permute-start | bytes 393224 | tf_op jit(solution)/shard_map/ppermute | solution.py:21
  42.0 6.6 %collective-permute-start.6 = (bf16[64,1024]{1,0:T(8,128)(2,1)S(1)}, bf16[64,1024]{1,0:T(8,128)(2,1)S(1)}, u32[]{:S(2)}, u32[]{:S(2)}) collective-permute-start(bf16[64,1024]{1,0:T(8,128)(2,1)S(1)} %get-tuple-element.20), channel_id=1, source_target_pairs={{2,0},{4,2},{6,4},{8,6},{10,8},{12,10},{14,12},{16,14},{18,16},{20... | collective-permute-start | bytes 393224 | tf_op jit(solution)/shard_map/ppermute | solution.py:21
  48.5 4.0 %copy-start.1 = (bf16[32,10,128,128]{3,2,1,0:T(8,128)(2,1)S(1)}, bf16[32,10,128,128]{3,2,1,0:T(8,128)(2,1)}, u32[]{:S(2)}) copy-start(bf16[32,10,128,128]{3,2,1,0:T(8,128)(2,1)} %refs_3_.5) | copy-start | bytes 31457284
  59.1 1.3 collective-permute-start.7
  60.4 9.1 %collective-permute-start.10 = (f32[64,128]{0,1:T(8,128)S(1)}, f32[64,128]{0,1:T(8,128)S(1)}, u32[]{:S(2)}, u32[]{:S(2)}) collective-permute-start(f32[64,128]{0,1:T(8,128)S(1)} %add.50), channel_id=1, source_target_pairs={{0,48},{16,32},{32,16},{48,0},{1,49},{17,33},{33,17},{49,1},{2,50}... | collective-permute-start | bytes 98312 | tf_op jit(solution)/shard_map/ppermute | solution.py:25
  67.4 3.1 %collective-permute-start.8 = (f32[64,128]{0,1:T(8,128)S(1)}, f32[64,128]{0,1:T(8,128)S(1)}, u32[]{:S(2)}, u32[]{:S(2)}) collective-permute-start(f32[64,128]{0,1:T(8,128)S(1)} %add.50), channel_id=1, source_target_pairs={{0,16},{16,0},{32,48},{48,32},{1,17},{17,1},{33,49},{49,33},{2,18}... | collective-permute-start | bytes 98312 | tf_op jit(solution)/shard_map/ppermute | solution.py:25
  67.4 4.6 %collective-permute-start.9 = (f32[64,128]{0,1:T(8,128)S(1)}, f32[64,128]{0,1:T(8,128)S(1)}, u32[]{:S(2)}, u32[]{:S(2)}) collective-permute-start(f32[64,128]{0,1:T(8,128)S(1)} %add.50), channel_id=1, source_target_pairs={{0,32},{16,48},{32,0},{48,16},{1,33},{17,49},{33,1},{49,17},{2,34}... | collective-permute-start | bytes 98312 | tf_op jit(solution)/shard_map/ppermute | solution.py:25
  72.0 18.4 %collective-permute-start.11 = (f32[64,128]{0,1:T(8,128)S(1)}, f32[64,128]{0,1:T(8,128)S(1)}, u32[]{:S(2)}, u32[]{:S(2)}) collective-permute-start(f32[64,128]{0,1:T(8,128)S(1)} %add_add_fusion.2), channel_id=1, source_target_pairs={{0,4},{4,0},{8,12},{12,8},{1,5},{5,1},{9,13},{13,9},{2,6},{6,2},{1... | collective-permute-start | bytes 98312 | tf_op jit(solution)/shard_map/ppermute | solution.py:25
  74.6 18.1 %collective-permute-start.12 = (f32[64,128]{0,1:T(8,128)S(1)}, f32[64,128]{0,1:T(8,128)S(1)}, u32[]{:S(2)}, u32[]{:S(2)}) collective-permute-start(f32[64,128]{0,1:T(8,128)S(1)} %add_add_fusion.2), channel_id=1, source_target_pairs={{0,8},{4,12},{8,0},{12,4},{1,9},{5,13},{9,1},{13,5},{2,10},{6,14},... | collective-permute-start | bytes 98312 | tf_op jit(solution)/shard_map/ppermute | solution.py:25
  90.4 5.0 %collective-permute-start.13 = (f32[64,128]{0,1:T(8,128)S(1)}, f32[64,128]{0,1:T(8,128)S(1)}, u32[]{:S(2)}, u32[]{:S(2)}) collective-permute-start(f32[64,128]{0,1:T(8,128)S(1)} %add_add_fusion.2), channel_id=1, source_target_pairs={{0,12},{4,8},{8,4},{12,0},{1,13},{5,9},{9,5},{13,1},{2,14},{6,10},... | collective-permute-start | bytes 98312 | tf_op jit(solution)/shard_map/ppermute | solution.py:25
  95.4 12.0 %collective-permute-start.14 = (f32[64,128]{0,1:T(8,128)S(1)}, f32[64,128]{0,1:T(8,128)S(1)}, u32[]{:S(2)}, u32[]{:S(2)}) collective-permute-start(f32[64,128]{0,1:T(8,128)S(1)} %add_add_fusion.1), channel_id=1, source_target_pairs={{0,64},{64,0},{128,192},{192,128},{1,65},{65,1},{129,193},{193,129... | collective-permute-start | bytes 98312 | tf_op jit(solution)/shard_map/ppermute | solution.py:25
  104.1 7.0 %collective-permute-start.15 = (f32[64,128]{0,1:T(8,128)S(1)}, f32[64,128]{0,1:T(8,128)S(1)}, u32[]{:S(2)}, u32[]{:S(2)}) collective-permute-start(f32[64,128]{0,1:T(8,128)S(1)} %add_add_fusion.1), channel_id=1, source_target_pairs={{0,128},{64,192},{128,0},{192,64},{1,129},{65,193},{129,1},{193,65... | collective-permute-start | bytes 98312 | tf_op jit(solution)/shard_map/ppermute | solution.py:25
  104.1 7.0 %collective-permute-start.16 = (f32[64,128]{0,1:T(8,128)S(1)}, f32[64,128]{0,1:T(8,128)S(1)}, u32[]{:S(2)}, u32[]{:S(2)}) collective-permute-start(f32[64,128]{0,1:T(8,128)S(1)} %add_add_fusion.1), channel_id=1, source_target_pairs={{0,192},{64,128},{128,64},{192,0},{1,193},{65,129},{129,65},{193,1... | collective-permute-start | bytes 98312 | tf_op jit(solution)/shard_map/ppermute | solution.py:25
  111.1 5.8 %collective-permute-start.17 = (f32[64,128]{0,1:T(8,128)S(1)}, f32[64,128]{0,1:T(8,128)S(1)}, u32[]{:S(2)}, u32[]{:S(2)}) collective-permute-start(f32[64,128]{0,1:T(8,128)S(1)} %add_add_fusion), channel_id=1, source_target_pairs={{0,2},{2,0},{1,3},{3,1},{4,6},{6,4},{5,7},{7,5},{8,10},{10,8},{9,1... | collective-permute-start | bytes 98312 | tf_op jit(solution)/shard_map/ppermute | solution.py:25
  115.2 3.7 %collective-permute-start.18 = (f32[64,128]{0,1:T(8,128)S(1)}, f32[64,128]{0,1:T(8,128)S(1)}, u32[]{:S(2)}, u32[]{:S(2)}) collective-permute-start(f32[64,128]{0,1:T(8,128)S(1)} %add_add_fusion), channel_id=1, source_target_pairs={{0,1},{1,0},{2,3},{3,2},{4,5},{5,4},{6,7},{7,6},{8,9},{9,8},{10,11... | collective-permute-start | bytes 98312 | tf_op jit(solution)/shard_map/ppermute | solution.py:25
  115.2 5.2 %collective-permute-start.19 = (f32[64,128]{0,1:T(8,128)S(1)}, f32[64,128]{0,1:T(8,128)S(1)}, u32[]{:S(2)}, u32[]{:S(2)}) collective-permute-start(f32[64,128]{0,1:T(8,128)S(1)} %add_add_fusion), channel_id=1, source_target_pairs={{0,3},{1,2},{2,1},{3,0},{4,7},{5,6},{6,5},{7,4},{8,11},{9,10},{10,... | collective-permute-start | bytes 98312 | tf_op jit(solution)/shard_map/ppermute | solution.py:25

commit v2 on v0

v2 whole, which is shorter than its diff:
```python
import jax
import jax.numpy as jnp
from jax import lax
from jax.experimental import pallas as pl
from jax.experimental.pallas import tpu as pltpu
from jax.sharding import Mesh
from jax.sharding import PartitionSpec as P

Z, X, Y, C, M = "dof_z", "dof_x", "dof_y", "dof_c", "mode"
DOF = (Z, X, Y, C)
VMEM = pl.BlockSpec(memory_space=pltpu.VMEM)
SMEM = pl.BlockSpec(memory_space=pltpu.SMEM)
HBM = pl.BlockSpec(memory_space=pltpu.HBM)
NT = (((1,), (1,)), ((), ()))
GROUP = 8


def params(mib):
    return pltpu.CompilerParams(vmem_limit_bytes=mib << 20)


def shape(dims, dtype):
    return jax.ShapeDtypeStruct(dims, dtype)


def flipped(block, axis, bits):
    return lax.ppermute(block, axis, [(i, i ^ bits) for i in range(lax.axis_size(axis))])


def swapped_between_chips(block):
    count = lax.axis_size(DOF)
    pairs = [(i, i + 1) for i in range(1, count - 1, 2)]
    return lax.ppermute(block, DOF, pairs + [(b, a) for a, b in pairs])


def exchange(near, far):
    from_far = swapped_between_chips(far)
    from_near = flipped(near, C, 1)
    return from_near, from_far


def columns(index, tile):
    return pl.ds(pl.multiple_of(index * tile, tile), tile)


def copy_lists(place, send, field, near, far, tile):
    core = place[1]
    for slot in range(near.shape[1] // tile):
        here = slice(slot * tile, (slot + 1) * tile)
        near[:, here] = field[:, columns(send[1 - core, slot], tile)]
        far[:, here] = field[:, columns(send[core, slot], tile)]


def pick_lists(place, send_rows, field, tile):
    modes = field.shape[0]
    count = send_rows.shape[1]
    part = shape((modes, count * tile), field.dtype)

    def kernel(place, send, field, near, far, sems):
        core = place[1]
        copies = []
        for slot in range(count):
            here = slice(slot * tile, (slot + 1) * tile)
            for out, row, which in ((far, core, 0), (near, 1 - core, 1)):
                source = field.at[:, columns(send[row, slot], tile)]
                copies.append(pltpu.make_async_copy(source, out.at[:, here], sems.at[which, slot]))
        for copy in copies:
            copy.start()
        for copy in copies:
            copy.wait()

    return pl.pallas_call(
        kernel,
        out_shape=(part, part),
        in_specs=[SMEM, SMEM, HBM],
        out_specs=(VMEM, VMEM),
        scratch_shapes=[pltpu.SemaphoreType.DMA((2, count))],
        compiler_params=params(4),
        name="pick_lists",
    )(place, send_rows, pltpu.with_memory_space_constraint(field, pltpu.HBM))


class Plan:
    def __init__(self, rows, nnz):
        self.pairs = rows * ((nnz + 1) // 2) + GROUP
        self.tiles = 2 * self.pairs + 16
        self.rows = 2 * self.tiles
        self.groups = self.rows + self.pairs + 16
        self.size = self.groups + 8


def stage(tile_cols, tiles, ghosts):
    nnz, rows = tile_cols.shape
    plan = Plan(rows, nnz)
    chunks = 8
    per_chunk = rows * nnz // chunks

    def kernel(cols, tiles, staged, local, ghost, sems):
        copies = [
            pltpu.make_async_copy(
                tiles.at[pl.ds(i * per_chunk, per_chunk)], staged.at[pl.ds(i * per_chunk, per_chunk)], sems.at[i]
            )
            for i in range(chunks)
        ]
        for copy in copies:
            copy.start()

        lists = ((local, rows), (ghost, ghosts))

        def put(row, counts):
            starts = counts
            for k in range(nnz):
                code = cols[k, row]
                is_local = (code < rows).astype(jnp.int32)
                took = (is_local, 1 - is_local)
                for (out, _), at, shift in zip(lists, counts, (0, rows)):
                    out[at] = code - shift
                    out[plan.tiles + at] = row * nnz + k
                counts = tuple(at + one for at, one in zip(counts, took))
            for (out, zero), at, start in zip(lists, counts, starts):
                out[at] = jnp.int32(zero)
                out[plan.tiles + at] = row * nnz
                for i in range((nnz + 1) // 2):
                    out[plan.rows + (start >> 1) + i] = row
            return tuple(at + (at & 1) for at in counts)

        counts = lax.fori_loop(0, rows, put, (jnp.int32(0), jnp.int32(0)))
        for (out, zero), at in zip(lists, counts):
            for i in range(GROUP):
                for j in range(2):
                    out[at + 2 * i + j] = jnp.int32(zero)
                    out[plan.tiles + at + 2 * i + j] = jnp.int32(0)
                out[plan.rows + (at >> 1) + i] = jnp.int32(rows)
            out[plan.groups] = ((at >> 1) + GROUP - 1) // GROUP
        for copy in copies:
            copy.wait()

    return pl.pallas_call(
        kernel,
        out_shape=(shape(tiles.shape, tiles.dtype), shape((plan.size,), jnp.int32), shape((plan.size,), jnp.int32)),
        in_specs=[SMEM, HBM],
        out_specs=(VMEM, SMEM, SMEM),
        scratch_shapes=[pltpu.SemaphoreType.DMA((chunks,))],
        compiler_params=params(4),
        cost_estimate=pl.CostEstimate(flops=0, bytes_accessed=2 * tiles.size, transcendentals=0),
        name="stage",
    )(tile_cols, pltpu.with_memory_space_constraint(tiles, pltpu.HBM))


def add_pairs(layout, plan, tiles, sources, total):
    tile = tiles.shape[1]

    def step(group, carry):
        for u in range(GROUP):
            pair = group * GROUP + u
            source = [sources[:, columns(plan[2 * pair + i], tile)] for i in range(2)]
            stored = [tiles[plan[layout.tiles + 2 * pair + i]] for i in range(2)]
            product = lax.dot_general(
                jnp.concatenate(source, axis=1),
                jnp.concatenate(stored, axis=1),
                NT,
                preferred_element_type=jnp.float32,
            )
            here = columns(plan[layout.rows + pair], tile)
            total[:, here] = total[:, here] + product
        return carry

    lax.fori_loop(0, plan[layout.groups], step, 0)


def local_sums(level, layout, plan, tiles, field):
    modes, width = field.shape
    tile = tiles.shape[1]

    def kernel(plan, tiles, field, total, sources):
        sources[:, :width] = field[...]
        sources[:, width:] = jnp.zeros((modes, tile), field.dtype)
        total[...] = jnp.zeros(total.shape, total.dtype)
        add_pairs(layout, plan, tiles, sources, total)

    return pl.pallas_call(
        kernel,
        out_shape=shape((modes, width + tile), jnp.float32),
        in_specs=[SMEM, VMEM, VMEM],
        out_specs=VMEM,
        scratch_shapes=[pltpu.VMEM((modes, width + tile), field.dtype)],
        compiler_params=params(8),
        cost_estimate=pl.CostEstimate(flops=tiles.size * modes, bytes_accessed=2 * tiles.size, transcendentals=0),
        name=f"local_sums_{level}",
    )(plan, tiles, field)


def add_ghosts(layout, place, plan, tiles, near, far, ghosts, total):
    tile = tiles.shape[1]
    width = near.shape[1]
    core = place[1]
    ghosts[:, pl.ds(pl.multiple_of((1 - core) * width, width), width)] = near[...]
    ghosts[:, pl.ds(pl.multiple_of(core * width, width), width)] = far[...]
    ghosts[:, 2 * width :] = jnp.zeros((near.shape[0], tile), near.dtype)
    add_pairs(layout, plan, tiles, ghosts, total)


def next_level(level, layout, place, plan, send_rows, bounds, tiles, total, near, far, field, previous):
    modes, width = field.shape
    tile = tiles.shape[1]
    part = 4 * tile

    def kernel(place, plan, send, lower, upper, tiles, _, near, far, field, *rest):
        if level == 2:
            previous, *rest = rest
        total, out, near_out, far_out, ghosts = rest
        add_ghosts(layout, place, plan, tiles, near, far, ghosts, total)
        center = (upper[0] + lower[0]) * 0.5
        factor = 1.0 / jnp.full((modes, part), (upper[0] - lower[0]) * 0.5, jnp.float32)

        def finish(i, carry):
            here = columns(i, part)
            value = (total[:, here] - center * field[:, here].astype(jnp.float32)) * factor
            if level == 2:
                value = 2.0 * value - previous[:, here].astype(jnp.float32)
            out[:, here] = value.astype(out.dtype)
            return carry

        lax.fori_loop(0, width // part, finish, 0)
        copy_lists(place, send, out, near_out, far_out, tile)

    operands = [place, plan, send_rows, *bounds, tiles, total, near, far, field]
    specs = [SMEM] * 5 + [VMEM] * 5
    if level == 2:
        operands.append(previous)
        specs.append(VMEM)
    return pl.pallas_call(
        kernel,
        out_shape=(
            shape(total.shape, total.dtype),
            shape(field.shape, field.dtype),
            shape(near.shape, near.dtype),
            shape(near.shape, near.dtype),
        ),
        in_specs=specs,
        out_specs=(VMEM,) * 4,
        scratch_shapes=[pltpu.VMEM((modes, 2 * near.shape[1] + tile), near.dtype)],
        input_output_aliases={6: 0},
        compiler_params=params(8),
        name=f"next_level_{level}",
    )(*operands)[1:]


def partial_sums(layout, place, plan, tiles, total, near, far, own, partner):
    modes, width = own.shape
    tile = tiles.shape[1]
    product = shape((modes, 2 * modes), jnp.float32)

    def kernel(place, plan, tiles, _, near, far, own, partner, total, keep, send, both, ghosts, left):
        add_ghosts(layout, place, plan, tiles, near, far, ghosts, total)
        mode, core = place[0], place[1]
        both[columns(mode, modes), :] = own[...]
        both[columns(1 - mode, modes), :] = partner[...]
        left[columns(core, modes), :] = own[...]
        left[columns(1 - core, modes), :] = total[:, :width].astype(own.dtype)
        sums = lax.dot_general(left[...], both[...], NT, preferred_element_type=jnp.float32)
        keep[...] = sums[:modes]
        send[...] = sums[modes:]

    return pl.pallas_call(
        kernel,
        out_shape=(shape(total.shape, total.dtype), product, product, shape((2 * modes, width), own.dtype)),
        in_specs=[SMEM] * 2 + [VMEM] * 6,
        out_specs=(VMEM,) * 4,
        scratch_shapes=[
            pltpu.VMEM((modes, 2 * near.shape[1] + tile), near.dtype),
            pltpu.VMEM((2 * modes, width), own.dtype),
        ],
        input_output_aliases={3: 0},
        compiler_params=params(12),
        name="partial_sums",
    )(place, plan, tiles, total, near, far, own, partner)[1:]


def sum_over_chips(value):
    for axis in (X, Y, Z):
        others = [flipped(value, axis, bits) for bits in (1, 2, 3)]
        value = (value + others[0]) + (others[1] + others[2])
    return value


def spread(block, lane):
    return jnp.broadcast_to(block[:, lane : lane + 1], block.shape)


def eliminated(blocks):
    rows, size = blocks[0].shape
    sub = lax.broadcasted_iota(jnp.int32, (rows, size), 0)
    lane = lax.broadcasted_iota(jnp.int32, (rows, size), 1)
    blocks = list(blocks)
    for b in range(len(blocks)):
        first = rows * b
        row = [jnp.broadcast_to(blocks[b][s : s + 1, :], (rows, size)) for s in range(rows)]
        d = {(t, s): spread(row[t], first + s) for t in range(rows) for s in range(t + 1)}
        unit = [row[s] + (lane == first + s).astype(jnp.float32) for s in range(rows)]
        ratio, reciprocal = {}, []
        for s in range(rows):
            reciprocal.append(1.0 / d[s, s])
            for t in range(s + 1, rows):
                ratio[t, s] = d[t, s] * reciprocal[s]
            for t in range(s + 1, rows):
                for q in range(s + 1, t + 1):
                    d[t, q] = d[t, q] - ratio[t, s] * d[q, s]
                unit[t] = unit[t] - ratio[t, s] * unit[s]
        solved = [None] * rows
        for s in reversed(range(rows)):
            value = unit[s] * reciprocal[s]
            for t in range(s + 1, rows):
                value = value - ratio[t, s] * solved[t]
            solved[s] = value
        for k in range(b + 1, len(blocks)):
            value = blocks[k]
            for s in range(rows):
                value = value - spread(blocks[k], first + s) * solved[s]
            blocks[k] = value
        value = blocks[b]
        for s in range(rows):
            value = jnp.where(sub == s, unit[s] - (lane == first + s).astype(jnp.float32), value)
        blocks[b] = value
    return blocks


def factor_and_project(place, quarters, both, dof_total):
    modes, width = both.shape[0] // 2, both.shape[1]
    size = 2 * modes

    def kernel(place, own, other_core, other_mode, last, both, basis, ritz, sums, inverse):
        mode, core = place[0], place[1]
        for part, c, m in (
            (own, core, mode),
            (other_core, 1 - core, mode),
            (other_mode, core, 1 - mode),
            (last, 1 - core, 1 - mode),
        ):
            sums[columns(2 * c + m, modes), :] = part[...] / dof_total
        blocks = eliminated([sums[i : i + 8, :] for i in range(0, size, 8)])
        matrix = jnp.concatenate(blocks, axis=0)
        sub = lax.broadcasted_iota(jnp.int32, (size, size), 0)
        lane = lax.broadcasted_iota(jnp.int32, (size, size), 1)
        pivots = jnp.sum(jnp.where(sub == lane, matrix, 0.0), axis=1, keepdims=True)
        lower = jnp.where(lane < sub, matrix, jnp.where(lane == sub, 1.0, 0.0)) * lax.rsqrt(pivots)
        inverse[...] = lower
        left = inverse[columns(mode, modes), :].astype(both.dtype)
        basis[...] = jnp.dot(left, both[...], preferred_element_type=jnp.float32).astype(basis.dtype)
        half = lax.dot_general(
            lower, sums[size:, :], NT, precision=lax.Precision.HIGHEST, preferred_element_type=jnp.float32
        )
        ritz[...] = lax.dot_general(
            half, lower, NT, precision=lax.Precision.HIGHEST, preferred_element_type=jnp.float32
        )

    return pl.pallas_call(
        kernel,
        out_shape=(shape((modes, width), both.dtype), shape((size, size), jnp.float32)),
        in_specs=[SMEM] + [VMEM] * 5,
        out_specs=(VMEM, VMEM),
        scratch_shapes=[pltpu.VMEM((2 * size, size), jnp.float32), pltpu.VMEM((size, size), jnp.float32)],
        compiler_params=params(12),
        name="factor_and_project",
    )(place, *quarters, both)


def shards(stiffness_tiles, tile_cols, send_rows, block, lower_bound, upper_bound):
    rows, nnz, tile, _ = stiffness_tiles.shape
    dof_total = block.shape[0] * lax.axis_size(DOF)
    ghosts = 2 * send_rows.shape[1]
    place = jnp.stack([lax.axis_index(M), lax.axis_index(C)]).astype(jnp.int32)
    layout = Plan(rows, nnz)
    bounds = (lower_bound, upper_bound)
    level_0 = block.T

    near, far = exchange(*pick_lists(place, send_rows, level_0, tile))
    tiles, local, ghost = stage(tile_cols.T, stiffness_tiles.reshape(rows * nnz, tile, tile), ghosts)

    def level(index, total, near, far, field, previous=None):
        return next_level(
            index, layout, place, ghost, send_rows, bounds, tiles, total, near, far, field, previous
        )

    total = local_sums(1, layout, local, tiles, level_0)
    level_1, near, far = level(1, total, near, far, level_0)
    near, far = exchange(near, far)
    total = local_sums(2, layout, local, tiles, level_1)
    filtered, near, far = level(2, total, near, far, level_1, level_0)
    near, far = exchange(near, far)
    partner = flipped(filtered, M, 1)
    total = local_sums(3, layout, local, tiles, filtered)
    keep, send, both = partial_sums(layout, place, ghost, tiles, total, near, far, filtered, partner)
    quarter = sum_over_chips(keep + flipped(send, C, 1))
    quarters = (quarter, flipped(quarter, C, 1), flipped(quarter, M, 1), flipped(quarter, (C, M), 3))
    basis, ritz = factor_and_project(place, quarters, both, dof_total)
    return (basis.T, ritz)


def solution(mesh):
    torus = Mesh(mesh.devices.reshape(4, 4, 4, 2, mesh.shape["mode"]), DOF + (M,))
    return jax.shard_map(
        shards,
        mesh=torus,
        in_specs=(P(DOF, None, None, None), P(DOF, None), P(DOF, None), P(DOF, M), P(), P()),
        out_specs=(P(DOF, M), P()),
        check_vma=False,
    )
```

time: 404 us -> 106 us (0.26)
  waiting for transfers between devices: 252 us -> 18 us
  local copies, waits for them, and re-layouts: 48.2 us -> 1.38 us
  Pallas kernels: 0 us -> 41.9 us
  matrix products: 32.9 us -> 0 us
  other arithmetic: 26.7 us -> 0.11 us
  starting transfers between devices: 26.5 us -> 41.9 us
  between operations: 15.4 us -> 2.13 us
    psum x5 -> x0, waiting for transfers between devices: 235 us -> none  [by_axis(): return functools.reduce(lax.psum, axes, shard)]
    gather x9 -> x0, local copies, waits for them, and re-layouts: 43.4 us -> none  [the longest x3 40 us: apply_stiffness(): picked = extended[tile_cols]]
    pallas_call x0 -> x9, Pallas kernels: none -> 41.9 us  [the longest x3 14.1 us: local_sums(): pl.pallas_call(kernel, out_shape=shape((modes, width + tile), jnp.float32...]
    dot_general x8 -> x0, matrix products: 32.6 us -> none  [the longest x3 27.7 us: apply_stiffness(): jnp.einsum('rkij,rkjm->rim', stiffness_tiles, picked, preferred_element_t...]
    ppermute x6 -> x20, starting transfers between devices: 15.4 us -> 41.9 us  [the longest x17 33.1 us: flipped(): lax.ppermute(block, axis, [(i, i ^ bits) for i in range(lax.axis_size(axi...]
    another operation x5 -> x1, other arithmetic: 22.9 us -> 0.08 us  [shards(): place = jnp.stack([lax.axis_index(M), lax.axis_index(C)]).astype(jnp.int32)]
    ppermute x6 -> x20, waiting for transfers between devices: 5.83 us -> 18 us  [the longest x17 18 us: flipped(): lax.ppermute(block, axis, [(i, i ^ bits) for i in range(lax.axis_size(axi...]
    all_to_all x3 -> x0, waiting for transfers between devices: 11.9 us -> none  [the longest x1 7.09 us: shards(): lax.all_to_all(image_block, 'mode', split_axis=0, concat_axis=1, tiled=True)]
  transfers between devices with their start and end apart: 14 -> 20, of which waited for: 9 -> 9; matrix products, arithmetic and copies ran while one was open for 7% -> 0% of each run, Pallas kernels for 0% -> 19%
where the time goes in v2:
time: 106 us; the launch traced here: 105 us
  Pallas kernels  41.9 us (40%)
  starting transfers between devices  41.9 us (40%)
  waiting for transfers between devices  18 us (17%)
  between operations  2.13 us (2%)
  local copies, waits for them, and re-layouts  1.38 us (1%)
    ppermute x17, starting transfers between devices, flipped(): lax.ppermute(block, axis, [(i, i ^ bits) for i in range(lax.axis_size(axi...  33.1 us
    ppermute x17, waiting for transfers between devices, flipped(): lax.ppermute(block, axis, [(i, i ^ bits) for i in range(lax.axis_size(axi...  18 us
    pallas_call x3, Pallas kernels, local_sums(): pl.pallas_call(kernel, out_shape=shape((modes, width + tile), jnp.float32...  14.1 us
    ppermute x3, starting transfers between devices, swapped_between_chips(): return lax.ppermute(block, DOF, pairs + [(b, a) for a, b in pairs])  8.81 us
    pallas_call x1, Pallas kernels, factor_and_project(): pl.pallas_call(kernel, out_shape=(shape((modes, width), both.dtype), shap...  8.31 us
    pallas_call x2, Pallas kernels, next_level(): pl.pallas_call(kernel, out_shape=(shape(total.shape, total.dtype), shape(...  8.14 us
    pallas_call x1, Pallas kernels, stage(): pl.pallas_call(kernel, out_shape=(shape(tiles.shape, tiles.dtype), shape(...  5.45 us
    pallas_call x1, Pallas kernels, partial_sums(): pl.pallas_call(kernel, out_shape=(shape(total.shape, total.dtype), produc...  4.26 us
  transfers between devices with their start and end apart: 20, of which 9 were waited for; matrix products, arithmetic and copies ran while one was open for 0% of the time, Pallas kernels for 19%

profile of v2, /device:TPU:1, one launch (start us, length us, event | category | flops | bytes accessed | tf_op | source)
XLA Modules:
  0.0 105.4 jit_solution(17294761156528653550)
XLA Ops:
  0.7 0.7 copy-done.1
  1.4 1.6 %pick_lists.1 = (bf16[64,1024]{1,0:T(8,128)(2,1)S(1)}, bf16[64,1024]{1,0:T(8,128)(2,1)S(1)}) custom-call(s32[2]{0:T(128)S(1)} %pad_add_fusion.place, s32[2,8]{1,0:T(2,128)S(1)} %copy-done.1, bf16[64,4096]{1,0:T(8,128)(2,1)} %bitcast.6), custom_call_target="tpu_custom_call" | custom-call | tf_op jit(solution)/shard_map/pick_lists/pallas_call | solution.py:72
  3.0 3.4 %collective-permute-start = (bf16[64,1024]{1,0:T(8,128)(2,1)S(1)}, bf16[64,1024]{1,0:T(8,128)(2,1)S(1)}, u32[]{:S(2)}, u32[]{:S(2)}) collective-permute-start(bf16[64,1024]{1,0:T(8,128)(2,1)S(1)} %get-tuple-element.21), channel_id=1, source_target_pairs={{0,2},{2,0},{1,3},{3,1},{4,6},{6,4},{5,7},{7,5},{8,10},{10,8},{9,1... | collective-permute-start | bytes 393224 | tf_op jit(solution)/shard_map/ppermute | solution.py:27
  6.4 1.9 %collective-permute-start.1 = (bf16[64,1024]{1,0:T(8,128)(2,1)S(1)}, bf16[64,1024]{1,0:T(8,128)(2,1)S(1)}, u32[]{:S(2)}, u32[]{:S(2)}) collective-permute-start(bf16[64,1024]{1,0:T(8,128)(2,1)S(1)} %get-tuple-element.22), channel_id=1, source_target_pairs={{2,4},{6,8},{10,12},{14,16},{18,20},{22,24},{26,28},{30,32},{34,36... | collective-permute-start | bytes 393224 | tf_op jit(solution)/shard_map/ppermute | solution.py:33
  9.6 0.7 copy-done.3
  10.3 5.5 %stage.1 = (bf16[320,128,128]{2,1,0:T(8,128)(2,1)S(1)}, s32[896]{0:T(1024)S(1)}, s32[896]{0:T(1024)S(1)}) custom-call(s32[10,32]{1,0:T(8,128)S(1)} %bitcast.10, bf16[320,128,128]{2,1,0:T(8,128)(2,1)} %bitcast.11), custom_call_target="tpu_custom_call" | custom-call | bytes 10485760 | tf_op jit(solution)/shard_map/stage/pallas_call | solution.py:138
  15.8 4.7 %local_sums_1.1._ = f32[64,4224]{1,0:T(8,128)S(1)} custom-call(s32[896]{0:T(1024)S(1)} %get-tuple-element.20.plan, bf16[320,128,128]{2,1,0:T(8,128)(2,1)S(1)} %get-tuple-element.19.tiles, bf16[64,4096]{1,0:T(8,128)(2,1)S(1)} %bitcast.7), custom_call_target="tpu_custom_call" | custom-call | flops 335544320 | bytes 10485760 | tf_op jit(solution)/shard_map/local_sums_1/pallas_call | solution.py:181
  20.5 4.0 %next_level_1.1 = (f32[64,4224]{1,0:T(8,128)S(1)}, bf16[64,4096]{1,0:T(8,128)(2,1)S(1)}, bf16[64,1024]{1,0:T(8,128)(2,1)S(1)}, bf16[64,1024]{1,0:T(8,128)(2,1)S(1)}) custom-call(s32[2]{0:T(128)S(1)} %pad_add_fusion.place, s32[896]{0:T(1024)S(1)} %get-tuple-element.18.plan, s32[2,8]{1,0:T(2,128)S(1)} %copy-done.2, ...), custom_call_target="tpu_custom_call", output_to_operand_aliasing={{0}: (6, {})} | custom-call | tf_op jit(solution)/shard_map/next_level_1/pallas_call | solution.py:232
  24.6 3.6 %collective-permute-start.3 = (bf16[64,1024]{1,0:T(8,128)(2,1)S(1)}, bf16[64,1024]{1,0:T(8,128)(2,1)S(1)}, u32[]{:S(2)}, u32[]{:S(2)}) collective-permute-start(bf16[64,1024]{1,0:T(8,128)(2,1)S(1)} %get-tuple-element.25), channel_id=1, source_target_pairs={{2,4},{6,8},{10,12},{14,16},{18,20},{22,24},{26,28},{30,32},{34,36... | collective-permute-start | bytes 393224 | tf_op jit(solution)/shard_map/ppermute | solution.py:33
  28.3 4.7 %local_sums_2.1._ = f32[64,4224]{1,0:T(8,128)S(1)} custom-call(s32[896]{0:T(1024)S(1)} %get-tuple-element.20.plan, bf16[320,128,128]{2,1,0:T(8,128)(2,1)S(1)} %get-tuple-element.19.tiles, bf16[64,4096]{1,0:T(8,128)(2,1)S(1)} %get-tuple-element.23.field), custom_call_target="tpu_custom_call" | custom-call | flops 335544320 | bytes 10485760 | tf_op jit(solution)/shard_map/local_sums_2/pallas_call | solution.py:181
  33.0 4.1 %next_level_2.1 = (f32[64,4224]{1,0:T(8,128)S(1)}, bf16[64,4096]{1,0:T(8,128)(2,1)S(1)}, bf16[64,1024]{1,0:T(8,128)(2,1)S(1)}, bf16[64,1024]{1,0:T(8,128)(2,1)S(1)}) custom-call(s32[2]{0:T(128)S(1)} %pad_add_fusion.place, s32[896]{0:T(1024)S(1)} %get-tuple-element.18.plan, s32[2,8]{1,0:T(2,128)S(1)} %copy-done.2, ...), custom_call_target="tpu_custom_call", output_to_operand_aliasing={{0}: (6, {})} | custom-call | tf_op jit(solution)/shard_map/next_level_2/pallas_call | solution.py:232
  37.1 1.1 %collective-permute-start.6 = (bf16[64,4096]{1,0:T(8,128)(2,1)S(1)}, bf16[64,4096]{1,0:T(8,128)(2,1)S(1)}, u32[]{:S(2)}, u32[]{:S(2)}) collective-permute-start(bf16[64,4096]{1,0:T(8,128)(2,1)S(1)} %get-tuple-element.26.field.own), channel_id=1, source_target_pairs={{0,1},{1,0},{2,3},{3,2},{4,5},{5,4},{6,7},{7,6},{8,9},{9,8},{10,11... | collective-permute-start | bytes 1572872 | tf_op jit(solution)/shard_map/ppermute | solution.py:27
  38.2 3.3 %collective-permute-start.5 = (bf16[64,1024]{1,0:T(8,128)(2,1)S(1)}, bf16[64,1024]{1,0:T(8,128)(2,1)S(1)}, u32[]{:S(2)}, u32[]{:S(2)}) collective-permute-start(bf16[64,1024]{1,0:T(8,128)(2,1)S(1)} %get-tuple-element.28), channel_id=1, source_target_pairs={{2,4},{6,8},{10,12},{14,16},{18,20},{22,24},{26,28},{30,32},{34,36... | collective-permute-start | bytes 393224 | tf_op jit(solution)/shard_map/ppermute | solution.py:33
  41.5 4.7 %local_sums_3.1._ = f32[64,4224]{1,0:T(8,128)S(1)} custom-call(s32[896]{0:T(1024)S(1)} %get-tuple-element.20.plan, bf16[320,128,128]{2,1,0:T(8,128)(2,1)S(1)} %get-tuple-element.19.tiles, bf16[64,4096]{1,0:T(8,128)(2,1)S(1)} %get-tuple-element.26.field.own), custom_call_target="tpu_custom_call" | custom-call | flops 335544320 | bytes 10485760 | tf_op jit(solution)/shard_map/local_sums_3/pallas_call | solution.py:181
  46.2 2.6 %collective-permute-done.6.partner = bf16[64,4096]{1,0:T(8,128)(2,1)S(1)} collective-permute-done((bf16[64,4096]{1,0:T(8,128)(2,1)S(1)}, bf16[64,4096]{1,0:T(8,128)(2,1)S(1)}, u32[]{:S(2)}, u32[]{:S(2)}) %collective-permute-start.6) | collective-permute-done | bytes 524320 | tf_op jit(solution)/shard_map/ppermute | solution.py:27
  48.9 4.3 %partial_sums.1 = (f32[64,4224]{1,0:T(8,128)S(1)}, f32[64,128]{1,0:T(8,128)S(1)}, f32[64,128]{1,0:T(8,128)S(1)}, bf16[128,4096]{1,0:T(8,128)(2,1)S(1)}) custom-call(s32[2]{0:T(128)S(1)} %pad_add_fusion.place, s32[896]{0:T(1024)S(1)} %get-tuple-element.18.plan, bf16[320,128,128]{2,1,0:T(8,128)(2,1)S(1)} %get-tuple-element.19.tiles, ...), custom_call_target="tpu_custom_call", output_to_operand_aliasing={{0}: (3, {})} | custom-call | tf_op jit(solution)/shard_map/partial_sums/pallas_call | solution.py:265
  53.2 1.2 %collective-permute-done.7 = f32[64,128]{1,0:T(8,128)S(1)} collective-permute-done((f32[64,128]{1,0:T(8,128)S(1)}, f32[64,128]{1,0:T(8,128)S(1)}, u32[]{:S(2)}, u32[]{:S(2)}) %collective-permute-start.7) | collective-permute-done | bytes 32800 | tf_op jit(solution)/shard_map/ppermute | solution.py:27
  54.4 4.3 %collective-permute-start.10 = (f32[64,128]{1,0:T(8,128)S(1)}, f32[64,128]{1,0:T(8,128)S(1)}, u32[]{:S(2)}, u32[]{:S(2)}) collective-permute-start(f32[64,128]{1,0:T(8,128)S(1)} %add.30), channel_id=1, source_target_pairs={{0,48},{16,32},{32,16},{48,0},{1,49},{17,33},{33,17},{49,1},{2,50}... | collective-permute-start | bytes 98312 | tf_op jit(solution)/shard_map/ppermute | solution.py:27
  59.4 0.6 collective-permute-done.10
  60.0 3.0 %collective-permute-done.9 = f32[64,128]{1,0:T(8,128)S(1)} collective-permute-done((f32[64,128]{1,0:T(8,128)S(1)}, f32[64,128]{1,0:T(8,128)S(1)}, u32[]{:S(2)}, u32[]{:S(2)}) %collective-permute-start.9) | collective-permute-done | bytes 32800 | tf_op jit(solution)/shard_map/ppermute | solution.py:27
  63.0 6.4 %collective-permute-start.13 = (f32[64,128]{1,0:T(8,128)S(1)}, f32[64,128]{1,0:T(8,128)S(1)}, u32[]{:S(2)}, u32[]{:S(2)}) collective-permute-start(f32[64,128]{1,0:T(8,128)S(1)} %add_add_fusion.2), channel_id=1, source_target_pairs={{0,12},{4,8},{8,4},{12,0},{1,13},{5,9},{9,5},{13,1},{2,14},{6,10},... | collective-permute-start | bytes 98312 | tf_op jit(solution)/shard_map/ppermute | solution.py:27
  69.4 0.7 collective-permute-start.11
  70.1 0.6 collective-permute-done.13
  70.7 3.0 %collective-permute-done.12 = f32[64,128]{1,0:T(8,128)S(1)} collective-permute-done((f32[64,128]{1,0:T(8,128)S(1)}, f32[64,128]{1,0:T(8,128)S(1)}, u32[]{:S(2)}, u32[]{:S(2)}) %collective-permute-start.12) | collective-permute-done | bytes 32800 | tf_op jit(solution)/shard_map/ppermute | solution.py:27
  73.7 7.9 %collective-permute-start.16 = (f32[64,128]{1,0:T(8,128)S(1)}, f32[64,128]{1,0:T(8,128)S(1)}, u32[]{:S(2)}, u32[]{:S(2)}) collective-permute-start(f32[64,128]{1,0:T(8,128)S(1)} %add_add_fusion.1), channel_id=1, source_target_pairs={{0,192},{64,128},{128,64},{192,0},{1,193},{65,129},{129,65},{193,1... | collective-permute-start | bytes 98312 | tf_op jit(solution)/shard_map/ppermute | solution.py:27
  81.6 1.6 %collective-permute-start.15 = (f32[64,128]{1,0:T(8,128)S(1)}, f32[64,128]{1,0:T(8,128)S(1)}, u32[]{:S(2)}, u32[]{:S(2)}) collective-permute-start(f32[64,128]{1,0:T(8,128)S(1)} %add_add_fusion.1), channel_id=1, source_target_pairs={{0,128},{64,192},{128,0},{192,64},{1,129},{65,193},{129,1},{193,65... | collective-permute-start | bytes 98312 | tf_op jit(solution)/shard_map/ppermute | solution.py:27
  83.2 0.6 collective-permute-start.14
  83.8 4.7 %collective-permute-done.15 = f32[64,128]{1,0:T(8,128)S(1)} collective-permute-done((f32[64,128]{1,0:T(8,128)S(1)}, f32[64,128]{1,0:T(8,128)S(1)}, u32[]{:S(2)}, u32[]{:S(2)}) %collective-permute-start.15) | collective-permute-done | bytes 32800 | tf_op jit(solution)/shard_map/ppermute | solution.py:27
  88.5 5.8 %collective-permute-start.19 = (f32[64,128]{1,0:T(8,128)S(1)}, f32[64,128]{1,0:T(8,128)S(1)}, u32[]{:S(2)}, u32[]{:S(2)}) collective-permute-start(f32[64,128]{1,0:T(8,128)S(1)} %add_add_fusion.own), channel_id=1, source_target_pairs={{0,3},{1,2},{2,1},{3,0},{4,7},{5,6},{6,5},{7,4},{8,11},{9,10},{10,... | collective-permute-start | bytes 98312 | tf_op jit(solution)/shard_map/ppermute | solution.py:27
  94.8 1.1 %collective-permute-done.19.last = f32[64,128]{1,0:T(8,128)S(1)} collective-permute-done((f32[64,128]{1,0:T(8,128)S(1)}, f32[64,128]{1,0:T(8,128)S(1)}, u32[]{:S(2)}, u32[]{:S(2)}) %collective-permute-start.19) | collective-permute-done | bytes 32800 | tf_op jit(solution)/shard_map/ppermute | solution.py:27
  95.9 1.2 %collective-permute-done.18.other_mode = f32[64,128]{1,0:T(8,128)S(1)} collective-permute-done((f32[64,128]{1,0:T(8,128)S(1)}, f32[64,128]{1,0:T(8,128)S(1)}, u32[]{:S(2)}, u32[]{:S(2)}) %collective-permute-start.18) | collective-permute-done | bytes 32800 | tf_op jit(solution)/shard_map/ppermute | solution.py:27
  97.1 8.3 %factor_and_project.1 = (bf16[64,4096]{1,0:T(8,128)(2,1)}, f32[128,128]{1,0:T(8,128)}) custom-call(s32[2]{0:T(128)S(1)} %pad_add_fusion.place, f32[64,128]{1,0:T(8,128)S(1)} %add_add_fusion.own, f32[64,128]{1,0:T(8,128)S(1)} %collective-permute-done.17.other_core, f32[64,128]{1,0:T(8,128)S(1)} %collective-permute-done.18.other_mode, ...), custom_call_target="tpu_custom_call" | custom-call | tf_op jit(solution)/shard_map/factor_and_project/pallas_call | solution.py:357
  (30 shorter events, 1.5 us)
Async XLA Ops:
  0.7 0.7 copy-start.1
  3.0 17.5 %collective-permute-start = (bf16[64,1024]{1,0:T(8,128)(2,1)S(1)}, bf16[64,1024]{1,0:T(8,128)(2,1)S(1)}, u32[]{:S(2)}, u32[]{:S(2)}) collective-permute-start(bf16[64,1024]{1,0:T(8,128)(2,1)S(1)} %get-tuple-element.21), channel_id=1, source_target_pairs={{0,2},{2,0},{1,3},{3,1},{4,6},{6,4},{5,7},{7,5},{8,10},{10,8},{9,1... | collective-permute-start | bytes 393224 | tf_op jit(solution)/shard_map/ppermute | solution.py:27
  6.4 14.1 %collective-permute-start.1 = (bf16[64,1024]{1,0:T(8,128)(2,1)S(1)}, bf16[64,1024]{1,0:T(8,128)(2,1)S(1)}, u32[]{:S(2)}, u32[]{:S(2)}) collective-permute-start(bf16[64,1024]{1,0:T(8,128)(2,1)S(1)} %get-tuple-element.22), channel_id=1, source_target_pairs={{2,4},{6,8},{10,12},{14,16},{18,20},{22,24},{26,28},{30,32},{34,36... | collective-permute-start | bytes 393224 | tf_op jit(solution)/shard_map/ppermute | solution.py:33
  9.6 0.7 copy-start.3
  10.3 5.5 %copy-start = (bf16[4096,64]{0,1:T(8,128)(2,1)S(1)}, bf16[4096,64]{0,1:T(8,128)(2,1)}, u32[]{:S(2)}) copy-start(bf16[4096,64]{0,1:T(8,128)(2,1)} %param.9) | copy-start | bytes 1572868
  15.7 4.7 %copy-start.2 = (s32[2,8]{1,0:T(2,128)S(1)}, s32[2,8]{1,0:T(2,128)}, u32[]{:S(2)}) copy-start(s32[2,8]{1,0:T(2,128)} %send.5) | copy-start | bytes 196
  24.5 8.5 %collective-permute-start.2 = (bf16[64,1024]{1,0:T(8,128)(2,1)S(1)}, bf16[64,1024]{1,0:T(8,128)(2,1)S(1)}, u32[]{:S(2)}, u32[]{:S(2)}) collective-permute-start(bf16[64,1024]{1,0:T(8,128)(2,1)S(1)} %get-tuple-element.24), channel_id=1, source_target_pairs={{0,2},{2,0},{1,3},{3,1},{4,6},{6,4},{5,7},{7,5},{8,10},{10,8},{9,1... | collective-permute-start | bytes 393224 | tf_op jit(solution)/shard_map/ppermute | solution.py:27
  24.6 8.4 %collective-permute-start.3 = (bf16[64,1024]{1,0:T(8,128)(2,1)S(1)}, bf16[64,1024]{1,0:T(8,128)(2,1)S(1)}, u32[]{:S(2)}, u32[]{:S(2)}) collective-permute-start(bf16[64,1024]{1,0:T(8,128)(2,1)S(1)} %get-tuple-element.25), channel_id=1, source_target_pairs={{2,4},{6,8},{10,12},{14,16},{18,20},{22,24},{26,28},{30,32},{34,36... | collective-permute-start | bytes 393224 | tf_op jit(solution)/shard_map/ppermute | solution.py:33
  37.1 11.8 %collective-permute-start.6 = (bf16[64,4096]{1,0:T(8,128)(2,1)S(1)}, bf16[64,4096]{1,0:T(8,128)(2,1)S(1)}, u32[]{:S(2)}, u32[]{:S(2)}) collective-permute-start(bf16[64,4096]{1,0:T(8,128)(2,1)S(1)} %get-tuple-element.26.field.own), channel_id=1, source_target_pairs={{0,1},{1,0},{2,3},{3,2},{4,5},{5,4},{6,7},{7,6},{8,9},{9,8},{10,11... | collective-permute-start | bytes 1572872 | tf_op jit(solution)/shard_map/ppermute | solution.py:27
  38.2 8.0 %collective-permute-start.4 = (bf16[64,1024]{1,0:T(8,128)(2,1)S(1)}, bf16[64,1024]{1,0:T(8,128)(2,1)S(1)}, u32[]{:S(2)}, u32[]{:S(2)}) collective-permute-start(bf16[64,1024]{1,0:T(8,128)(2,1)S(1)} %get-tuple-element.27), channel_id=1, source_target_pairs={{0,2},{2,0},{1,3},{3,1},{4,6},{6,4},{5,7},{7,5},{8,10},{10,8},{9,1... | collective-permute-start | bytes 393224 | tf_op jit(solution)/shard_map/ppermute | solution.py:27
  38.2 8.0 %collective-permute-start.5 = (bf16[64,1024]{1,0:T(8,128)(2,1)S(1)}, bf16[64,1024]{1,0:T(8,128)(2,1)S(1)}, u32[]{:S(2)}, u32[]{:S(2)}) collective-permute-start(bf16[64,1024]{1,0:T(8,128)(2,1)S(1)} %get-tuple-element.28), channel_id=1, source_target_pairs={{2,4},{6,8},{10,12},{14,16},{18,20},{22,24},{26,28},{30,32},{34,36... | collective-permute-start | bytes 393224 | tf_op jit(solution)/shard_map/ppermute | solution.py:33
  53.1 1.3 %collective-permute-start.7 = (f32[64,128]{1,0:T(8,128)S(1)}, f32[64,128]{1,0:T(8,128)S(1)}, u32[]{:S(2)}, u32[]{:S(2)}) collective-permute-start(f32[64,128]{1,0:T(8,128)S(1)} %get-tuple-element.30), channel_id=1, source_target_pairs={{0,2},{2,0},{1,3},{3,1},{4,6},{6,4},{5,7},{7,5},{8,10},{10,8},{9,1... | collective-permute-start | bytes 98312 | tf_op jit(solution)/shard_map/ppermute | solution.py:27
  54.4 5.6 %collective-permute-start.10 = (f32[64,128]{1,0:T(8,128)S(1)}, f32[64,128]{1,0:T(8,128)S(1)}, u32[]{:S(2)}, u32[]{:S(2)}) collective-permute-start(f32[64,128]{1,0:T(8,128)S(1)} %add.30), channel_id=1, source_target_pairs={{0,48},{16,32},{32,16},{48,0},{1,49},{17,33},{33,17},{49,1},{2,50}... | collective-permute-start | bytes 98312 | tf_op jit(solution)/shard_map/ppermute | solution.py:27
  58.7 4.3 %collective-permute-start.9 = (f32[64,128]{1,0:T(8,128)S(1)}, f32[64,128]{1,0:T(8,128)S(1)}, u32[]{:S(2)}, u32[]{:S(2)}) collective-permute-start(f32[64,128]{1,0:T(8,128)S(1)} %add.30), channel_id=1, source_target_pairs={{0,32},{16,48},{32,0},{48,16},{1,33},{17,49},{33,1},{49,17},{2,34}... | collective-permute-start | bytes 98312 | tf_op jit(solution)/shard_map/ppermute | solution.py:27
  59.1 3.9 %collective-permute-start.8 = (f32[64,128]{1,0:T(8,128)S(1)}, f32[64,128]{1,0:T(8,128)S(1)}, u32[]{:S(2)}, u32[]{:S(2)}) collective-permute-start(f32[64,128]{1,0:T(8,128)S(1)} %add.30), channel_id=1, source_target_pairs={{0,16},{16,0},{32,48},{48,32},{1,17},{17,1},{33,49},{49,33},{2,18}... | collective-permute-start | bytes 98312 | tf_op jit(solution)/shard_map/ppermute | solution.py:27
  63.0 7.7 %collective-permute-start.13 = (f32[64,128]{1,0:T(8,128)S(1)}, f32[64,128]{1,0:T(8,128)S(1)}, u32[]{:S(2)}, u32[]{:S(2)}) collective-permute-start(f32[64,128]{1,0:T(8,128)S(1)} %add_add_fusion.2), channel_id=1, source_target_pairs={{0,12},{4,8},{8,4},{12,0},{1,13},{5,9},{9,5},{13,1},{2,14},{6,10},... | collective-permute-start | bytes 98312 | tf_op jit(solution)/shard_map/ppermute | solution.py:27
  69.4 4.3 %collective-permute-start.12 = (f32[64,128]{1,0:T(8,128)S(1)}, f32[64,128]{1,0:T(8,128)S(1)}, u32[]{:S(2)}, u32[]{:S(2)}) collective-permute-start(f32[64,128]{1,0:T(8,128)S(1)} %add_add_fusion.2), channel_id=1, source_target_pairs={{0,8},{4,12},{8,0},{12,4},{1,9},{5,13},{9,1},{13,5},{2,10},{6,14},... | collective-permute-start | bytes 98312 | tf_op jit(solution)/shard_map/ppermute | solution.py:27
  69.4 4.3 %collective-permute-start.11 = (f32[64,128]{1,0:T(8,128)S(1)}, f32[64,128]{1,0:T(8,128)S(1)}, u32[]{:S(2)}, u32[]{:S(2)}) collective-permute-start(f32[64,128]{1,0:T(8,128)S(1)} %add_add_fusion.2), channel_id=1, source_target_pairs={{0,4},{4,0},{8,12},{12,8},{1,5},{5,1},{9,13},{13,9},{2,6},{6,2},{1... | collective-permute-start | bytes 98312 | tf_op jit(solution)/shard_map/ppermute | solution.py:27
  73.7 10.0 %collective-permute-start.16 = (f32[64,128]{1,0:T(8,128)S(1)}, f32[64,128]{1,0:T(8,128)S(1)}, u32[]{:S(2)}, u32[]{:S(2)}) collective-permute-start(f32[64,128]{1,0:T(8,128)S(1)} %add_add_fusion.1), channel_id=1, source_target_pairs={{0,192},{64,128},{128,64},{192,0},{1,193},{65,129},{129,65},{193,1... | collective-permute-start | bytes 98312 | tf_op jit(solution)/shard_map/ppermute | solution.py:27
  81.6 6.9 %collective-permute-start.15 = (f32[64,128]{1,0:T(8,128)S(1)}, f32[64,128]{1,0:T(8,128)S(1)}, u32[]{:S(2)}, u32[]{:S(2)}) collective-permute-start(f32[64,128]{1,0:T(8,128)S(1)} %add_add_fusion.1), channel_id=1, source_target_pairs={{0,128},{64,192},{128,0},{192,64},{1,129},{65,193},{129,1},{193,65... | collective-permute-start | bytes 98312 | tf_op jit(solution)/shard_map/ppermute | solution.py:27
  83.2 5.3 %collective-permute-start.14 = (f32[64,128]{1,0:T(8,128)S(1)}, f32[64,128]{1,0:T(8,128)S(1)}, u32[]{:S(2)}, u32[]{:S(2)}) collective-permute-start(f32[64,128]{1,0:T(8,128)S(1)} %add_add_fusion.1), channel_id=1, source_target_pairs={{0,64},{64,0},{128,192},{192,128},{1,65},{65,1},{129,193},{193,129... | collective-permute-start | bytes 98312 | tf_op jit(solution)/shard_map/ppermute | solution.py:27
  88.5 7.4 %collective-permute-start.19 = (f32[64,128]{1,0:T(8,128)S(1)}, f32[64,128]{1,0:T(8,128)S(1)}, u32[]{:S(2)}, u32[]{:S(2)}) collective-permute-start(f32[64,128]{1,0:T(8,128)S(1)} %add_add_fusion.own), channel_id=1, source_target_pairs={{0,3},{1,2},{2,1},{3,0},{4,7},{5,6},{6,5},{7,4},{8,11},{9,10},{10,... | collective-permute-start | bytes 98312 | tf_op jit(solution)/shard_map/ppermute | solution.py:27
  94.3 2.8 %collective-permute-start.18 = (f32[64,128]{1,0:T(8,128)S(1)}, f32[64,128]{1,0:T(8,128)S(1)}, u32[]{:S(2)}, u32[]{:S(2)}) collective-permute-start(f32[64,128]{1,0:T(8,128)S(1)} %add_add_fusion.own), channel_id=1, source_target_pairs={{0,1},{1,0},{2,3},{3,2},{4,5},{5,4},{6,7},{7,6},{8,9},{9,8},{10,11... | collective-permute-start | bytes 98312 | tf_op jit(solution)/shard_map/ppermute | solution.py:27
  94.3 2.8 %collective-permute-start.17 = (f32[64,128]{1,0:T(8,128)S(1)}, f32[64,128]{1,0:T(8,128)S(1)}, u32[]{:S(2)}, u32[]{:S(2)}) collective-permute-start(f32[64,128]{1,0:T(8,128)S(1)} %add_add_fusion.own), channel_id=1, source_target_pairs={{0,2},{2,0},{1,3},{3,1},{4,6},{6,4},{5,7},{7,5},{8,10},{10,8},{9,1... | collective-permute-start | bytes 98312 | tf_op jit(solution)/shard_map/ppermute | solution.py:27

commit v3 on v2

v3 whole, which is shorter than its diff:
```python
import jax
import jax.numpy as jnp
from jax import lax
from jax.experimental import pallas as pl
from jax.experimental.pallas import tpu as pltpu
from jax.sharding import Mesh
from jax.sharding import PartitionSpec as P

Z, X, Y, C, M = "dof_z", "dof_x", "dof_y", "dof_c", "mode"
DOF = (Z, X, Y, C)
VMEM = pl.BlockSpec(memory_space=pltpu.VMEM)
SMEM = pl.BlockSpec(memory_space=pltpu.SMEM)
HBM = pl.BlockSpec(memory_space=pltpu.HBM)
NT = (((1,), (1,)), ((), ()))
GROUP = 8


def params(mib):
    return pltpu.CompilerParams(vmem_limit_bytes=mib << 20)


def shape(dims, dtype):
    return jax.ShapeDtypeStruct(dims, dtype)


def flipped(block, axis, bits):
    return lax.ppermute(block, axis, [(i, i ^ bits) for i in range(lax.axis_size(axis))])


def swapped_between_chips(block):
    count = lax.axis_size(DOF)
    pairs = [(i, i + 1) for i in range(1, count - 1, 2)]
    return lax.ppermute(block, DOF, pairs + [(b, a) for a, b in pairs])


def columns(index, tile):
    return pl.ds(pl.multiple_of(index * tile, tile), tile)


def pick_lists(place, send_rows, field, tile):
    modes, width = field.shape
    count = send_rows.shape[1]
    part = shape((modes, count * tile), field.dtype)

    def kernel(place, send, field, held, far, near, rows, sems):
        copies = [
            pltpu.make_async_copy(send, rows, sems.at[0]),
            pltpu.make_async_copy(field, held, sems.at[1]),
        ]
        for copy in copies:
            copy.start()
        for copy in copies:
            copy.wait()
        core = place[1]
        for slot in range(count):
            here = slice(slot * tile, (slot + 1) * tile)
            far[:, here] = held[:, columns(rows[core, slot], tile)]
            near[:, here] = held[:, columns(rows[1 - core, slot], tile)]

    return pl.pallas_call(
        kernel,
        out_shape=(shape(field.shape, field.dtype), part, part),
        in_specs=[SMEM, HBM, HBM],
        out_specs=(VMEM,) * 3,
        scratch_shapes=[pltpu.SMEM(send_rows.shape, jnp.int32), pltpu.SemaphoreType.DMA((2,))],
        compiler_params=params(4),
        name="pick_lists",
    )(
        place,
        pltpu.with_memory_space_constraint(send_rows, pltpu.HBM),
        pltpu.with_memory_space_constraint(field, pltpu.HBM),
    )


def make_plan(place, send_rows, tile_cols, ghosts):
    nnz, rows = tile_cols.shape
    count = send_rows.shape[1]

    def kernel(place, send, cols, table, order, taken):
        code = [cols[k : k + 1, :] for k in range(nnz)]
        local = [(one < rows).astype(jnp.int32) for one in code]
        locals_before, total = [], jnp.zeros_like(code[0])
        for one in local:
            locals_before.append(total)
            total = total + one
        position = [
            jnp.where(local[k] == 1, locals_before[k], total + k - locals_before[k]) for k in range(nnz)
        ]
        for p in range(nnz):
            source, entry = jnp.zeros_like(total), jnp.zeros_like(total)
            for k in range(nnz):
                source = jnp.where(position[k] == p, code[k], source)
                entry = jnp.where(position[k] == p, k, entry)
            table[p : p + 1, :] = jnp.where(p < total, source, rows)
            table[nnz + p : nnz + p + 1, :] = jnp.where(p < total, ghosts, source - rows)
            table[2 * nnz + p : 2 * nnz + p + 1, :] = entry
        table[3 * nnz : 3 * nnz + 1, :] = nnz // 2 - (total >> 1)

        core = place[1]
        for row in range(rows):
            taken[row] = 0
        for slot in range(count):
            for start, which in ((0, core), (count, 1 - core)):
                row = send[which, slot]
                taken[row] = 1
                order[start + slot] = row
        at = jnp.int32(2 * count)
        for row in range(rows):
            order[at] = row
            at = at + 1 - taken[row]
        for i in range(GROUP):
            order[at + i] = order[0]
        order[2 * rows] = (at + GROUP - 1) // GROUP

    return pl.pallas_call(
        kernel,
        out_shape=(shape((3 * nnz + 2, rows), jnp.int32), shape((2 * rows + 8,), jnp.int32)),
        in_specs=[SMEM, SMEM, VMEM],
        out_specs=(VMEM, SMEM),
        scratch_shapes=[pltpu.SMEM((rows,), jnp.int32)],
        compiler_params=params(4),
        name="make_plan",
    )(place, send_rows, tile_cols)


def local_rows(table, tiles, sources, total, step, nnz):
    tile = tiles.shape[1]
    for u in range(GROUP):
        row = step * GROUP + u
        source = [sources[:, columns(table[p, row], tile)] for p in range(nnz - 2)]
        stored = [tiles[row * nnz + table[2 * nnz + p, row]] for p in range(nnz - 2)]
        total[:, columns(row, tile)] = lax.dot_general(
            jnp.concatenate(source, axis=1), jnp.concatenate(stored, axis=1), NT, preferred_element_type=jnp.float32
        )


def fill_sources(field, sources):
    width = field.shape[1]
    sources[:, :width] = field[...]
    sources[:, width:] = jnp.zeros((field.shape[0], sources.shape[1] - width), sources.dtype)


def stage_and_sum(table, tiles, field, rows, nnz):
    modes, width = field.shape
    tile = tiles.shape[1]
    per_chunk = GROUP // 2 * nnz
    chunks = rows * nnz // per_chunk

    def kernel(table, tiles, field, staged, total, sources, sems):
        def chunk(i):
            here = pl.ds(i * per_chunk, per_chunk)
            return pltpu.make_async_copy(tiles.at[here], staged.at[here], sems.at[i])

        for i in range(chunks):
            chunk(i).start()
        fill_sources(field, sources)

        def step(i, carry):
            chunk(2 * i).wait()
            chunk(2 * i + 1).wait()
            local_rows(table, staged, sources, total, i, nnz)
            return carry

        lax.fori_loop(0, rows // GROUP, step, 0)

    return pl.pallas_call(
        kernel,
        out_shape=(shape(tiles.shape, tiles.dtype), shape((modes, width), jnp.float32)),
        in_specs=[SMEM, HBM, VMEM],
        out_specs=(VMEM, VMEM),
        scratch_shapes=[pltpu.VMEM((modes, width + tile), field.dtype), pltpu.SemaphoreType.DMA((chunks,))],
        compiler_params=params(8),
        cost_estimate=pl.CostEstimate(flops=2 * tiles.size * modes, bytes_accessed=2 * tiles.size, transcendentals=0),
        name="stage_and_sum",
    )(table, pltpu.with_memory_space_constraint(tiles, pltpu.HBM), field)


def local_sums(level, table, tiles, field, rows, nnz):
    modes, width = field.shape
    tile = tiles.shape[1]

    def kernel(table, tiles, field, total, sources):
        fill_sources(field, sources)

        def step(i, carry):
            local_rows(table, tiles, sources, total, i, nnz)
            return carry

        lax.fori_loop(0, rows // GROUP, step, 0)

    return pl.pallas_call(
        kernel,
        out_shape=shape((modes, width), jnp.float32),
        in_specs=[SMEM, VMEM, VMEM],
        out_specs=VMEM,
        scratch_shapes=[pltpu.VMEM((modes, width + tile), field.dtype)],
        compiler_params=params(8),
        cost_estimate=pl.CostEstimate(flops=tiles.size * modes // 8, bytes_accessed=0, transcendentals=0),
        name=f"local_sums_{level}",
    )(table, tiles, field)


def fill_ghosts(core, near, far, ghosts):
    width = near.shape[1]
    ghosts[:, columns(1 - core, width)] = near[...]
    ghosts[:, columns(core, width)] = far[...]
    ghosts[:, 2 * width :] = jnp.zeros((near.shape[0], ghosts.shape[1] - 2 * width), ghosts.dtype)


def ghost_rows(table, order, tiles, ghosts, partial, first, nnz):
    tile = tiles.shape[1]
    rows = [first + u if order is None else order[first + u] for u in range(GROUP)]
    most = table[3 * nnz, rows[0]]
    for row in rows[1:]:
        most = jnp.maximum(most, table[3 * nnz, row])

    def add(q):
        for u, row in enumerate(rows):
            source = [ghosts[:, columns(table[nnz + 2 * q + i, row], tile)] for i in range(2)]
            stored = [tiles[row * nnz + table[2 * nnz + 2 * q + i, row]] for i in range(2)]
            product = lax.dot_general(
                jnp.concatenate(source, axis=1),
                jnp.concatenate(stored, axis=1),
                NT,
                preferred_element_type=jnp.float32,
            )
            here = slice(u * tile, (u + 1) * tile)
            partial[:, here] = product if q == nnz // 2 - 1 else partial[:, here] + product

    for q in reversed(range(nnz // 2)):
        if q == nnz // 2 - 1:
            add(q)
        else:
            pl.when(most >= nnz // 2 - q)(lambda q=q: add(q))
    return rows


def level_rows(level, bounds, rows, total, partial, field, previous, store):
    lower, upper = bounds
    modes, tile = field.shape[0], partial.shape[1] // GROUP
    center = (upper[0] + lower[0]) * 0.5
    factor = 1.0 / jnp.full((modes, tile), (upper[0] - lower[0]) * 0.5, jnp.float32)
    for u, row in enumerate(rows):
        here = columns(row, tile)
        value = total[:, here] + partial[:, u * tile : (u + 1) * tile]
        value = (value - center * field[:, here].astype(jnp.float32)) * factor
        if level == 2:
            value = 2.0 * value - previous[:, here].astype(jnp.float32)
        store(u, row, value.astype(field.dtype))


def next_lists(level, nnz, place, table, order, bounds, tiles, total, near, far, field, previous):
    tile = tiles.shape[1]

    def kernel(place, table, order, lower, upper, tiles, total, near, far, field, *rest):
        if level == 2:
            previous, *rest = rest
        else:
            previous = None
        new_far, new_near, ghosts, partial = rest
        fill_ghosts(place[1], near, far, ghosts)
        for out, first in ((new_far, 0), (new_near, GROUP)):
            rows = ghost_rows(table, order, tiles, ghosts, partial, first, nnz)

            def store(u, row, value, out=out):
                out[:, u * tile : (u + 1) * tile] = value

            level_rows(level, (lower, upper), rows, total, partial, field, previous, store)

    operands = [place, table, order, *bounds, tiles, total, near, far, field] + [previous] * (level == 2)
    return pl.pallas_call(
        kernel,
        out_shape=(shape(far.shape, far.dtype),) * 2,
        in_specs=[SMEM] * 5 + [VMEM] * (len(operands) - 5),
        out_specs=(VMEM,) * 2,
        scratch_shapes=[
            pltpu.VMEM((far.shape[0], 2 * far.shape[1] + tile), far.dtype),
            pltpu.VMEM((far.shape[0], GROUP * tile), jnp.float32),
        ],
        compiler_params=params(8),
        name=f"next_lists_{level}",
    )(*operands)


def next_level(level, nnz, place, table, order, bounds, tiles, total, near, far, field, previous, new_far, new_near):
    modes, width = field.shape
    tile = tiles.shape[1]

    def kernel(place, table, order, lower, upper, tiles, total, near, far, field, new_far, new_near, *rest):
        if level == 2:
            previous, *rest = rest
        else:
            previous = None
        out, ghosts, partial = rest
        fill_ghosts(place[1], near, far, ghosts)
        for held, first in ((new_far, 0), (new_near, GROUP)):
            for u in range(GROUP):
                out[:, columns(order[first + u], tile)] = held[:, u * tile : (u + 1) * tile]

        def store(u, row, value):
            out[:, columns(row, tile)] = value

        def step(i, carry):
            rows = ghost_rows(table, order, tiles, ghosts, partial, i * GROUP, nnz)
            level_rows(level, (lower, upper), rows, total, partial, field, previous, store)
            return carry

        lax.fori_loop(2, order[2 * width // tile], step, 0)

    operands = [place, table, order, *bounds, tiles, total, near, far, field, new_far, new_near]
    operands += [previous] * (level == 2)
    return pl.pallas_call(
        kernel,
        out_shape=shape(field.shape, field.dtype),
        in_specs=[SMEM] * 5 + [VMEM] * (len(operands) - 5),
        out_specs=VMEM,
        scratch_shapes=[
            pltpu.VMEM((modes, 2 * far.shape[1] + tile), far.dtype),
            pltpu.VMEM((modes, GROUP * tile), jnp.float32),
        ],
        compiler_params=params(8),
        cost_estimate=pl.CostEstimate(flops=tiles.size * modes, bytes_accessed=2 * tiles.size, transcendentals=0),
        name=f"next_level_{level}",
    )(*operands)


def image_rows(nnz, place, table, tiles, total, near, far):
    modes, width = total.shape
    tile = tiles.shape[1]

    def kernel(place, table, tiles, total, near, far, out, ghosts, partial):
        fill_ghosts(place[1], near, far, ghosts)

        def step(i, carry):
            rows = ghost_rows(table, None, tiles, ghosts, partial, i * GROUP, nnz)
            for u, row in enumerate(rows):
                here = columns(row, tile)
                out[:, here] = (total[:, here] + partial[:, u * tile : (u + 1) * tile]).astype(out.dtype)
            return carry

        lax.fori_loop(0, width // tile // GROUP, step, 0)

    return pl.pallas_call(
        kernel,
        out_shape=shape((modes, width), near.dtype),
        in_specs=[SMEM] * 2 + [VMEM] * 4,
        out_specs=VMEM,
        scratch_shapes=[
            pltpu.VMEM((modes, 2 * near.shape[1] + tile), near.dtype),
            pltpu.VMEM((modes, GROUP * tile), jnp.float32),
        ],
        compiler_params=params(8),
        cost_estimate=pl.CostEstimate(flops=20 * tiles.size * modes, bytes_accessed=2 * tiles.size, transcendentals=0),
        name="image_rows",
    )(place, table, tiles, total, near, far)


def partial_sums(place, own, partner, image):
    modes, width = own.shape
    product = shape((modes, 2 * modes), jnp.float32)

    def kernel(place, own, partner, image, keep, send, both, left):
        mode, core = place[0], place[1]
        both[columns(mode, modes), :] = own[...]
        both[columns(1 - mode, modes), :] = partner[...]
        left[columns(core, modes), :] = own[...]
        left[columns(1 - core, modes), :] = image[...]
        sums = lax.dot_general(left[...], both[...], NT, preferred_element_type=jnp.float32)
        keep[...] = sums[:modes]
        send[...] = sums[modes:]

    return pl.pallas_call(
        kernel,
        out_shape=(product, product, shape((2 * modes, width), own.dtype)),
        in_specs=[SMEM] + [VMEM] * 3,
        out_specs=(VMEM,) * 3,
        scratch_shapes=[pltpu.VMEM((2 * modes, width), own.dtype)],
        compiler_params=params(12),
        name="partial_sums",
    )(place, own, partner, image)


def sum_over_chips(value):
    for axis in (X, Y, Z):
        others = [flipped(value, axis, bits) for bits in (1, 2, 3)]
        value = (value + others[0]) + (others[1] + others[2])
    return value


def spread(block, lane):
    return jnp.broadcast_to(block[:, lane : lane + 1], block.shape)


def eliminated(blocks):
    rows, size = blocks[0].shape
    sub = lax.broadcasted_iota(jnp.int32, (rows, size), 0)
    lane = lax.broadcasted_iota(jnp.int32, (rows, size), 1)
    blocks = list(blocks)
    for b in range(len(blocks)):
        first = rows * b
        row = [jnp.broadcast_to(blocks[b][s : s + 1, :], (rows, size)) for s in range(rows)]
        d = {(t, s): spread(row[t], first + s) for t in range(rows) for s in range(t + 1)}
        unit = [row[s] + (lane == first + s).astype(jnp.float32) for s in range(rows)]
        ratio, reciprocal = {}, []
        for s in range(rows):
            reciprocal.append(1.0 / d[s, s])
            for t in range(s + 1, rows):
                ratio[t, s] = d[t, s] * reciprocal[s]
            for t in range(s + 1, rows):
                for q in range(s + 1, t + 1):
                    d[t, q] = d[t, q] - ratio[t, s] * d[q, s]
                unit[t] = unit[t] - ratio[t, s] * unit[s]
        solved = [None] * rows
        for s in reversed(range(rows)):
            value = unit[s] * reciprocal[s]
            for t in range(s + 1, rows):
                value = value - ratio[t, s] * solved[t]
            solved[s] = value
        for k in range(b + 1, len(blocks)):
            value = blocks[k]
            for s in range(rows):
                value = value - spread(blocks[k], first + s) * solved[s]
            blocks[k] = value
        value = blocks[b]
        for s in range(rows):
            value = jnp.where(sub == s, unit[s] - (lane == first + s).astype(jnp.float32), value)
        blocks[b] = value
    return blocks


def factor_and_project(place, quarters, both, dof_total):
    modes, width = both.shape[0] // 2, both.shape[1]
    size = 2 * modes

    def kernel(place, own, other_core, other_mode, last, both, basis, ritz, sums, inverse):
        mode, core = place[0], place[1]
        for part, c, m in (
            (own, core, mode),
            (other_core, 1 - core, mode),
            (other_mode, core, 1 - mode),
            (last, 1 - core, 1 - mode),
        ):
            sums[columns(2 * c + m, modes), :] = part[...] / dof_total
        blocks = eliminated([sums[i : i + 8, :] for i in range(0, size, 8)])
        matrix = jnp.concatenate(blocks, axis=0)
        sub = lax.broadcasted_iota(jnp.int32, (size, size), 0)
        lane = lax.broadcasted_iota(jnp.int32, (size, size), 1)
        pivots = jnp.sum(jnp.where(sub == lane, matrix, 0.0), axis=1, keepdims=True)
        lower = jnp.where(lane < sub, matrix, jnp.where(lane == sub, 1.0, 0.0)) * lax.rsqrt(pivots)
        inverse[...] = lower
        left = inverse[columns(mode, modes), :].astype(both.dtype)
        basis[...] = jnp.dot(left, both[...], preferred_element_type=jnp.float32).astype(basis.dtype)
        half = lax.dot_general(
            lower, sums[size:, :], NT, precision=lax.Precision.HIGHEST, preferred_element_type=jnp.float32
        )
        ritz[...] = lax.dot_general(
            half, lower, NT, precision=lax.Precision.HIGHEST, preferred_element_type=jnp.float32
        )

    return pl.pallas_call(
        kernel,
        out_shape=(shape((modes, width), both.dtype), shape((size, size), jnp.float32)),
        in_specs=[SMEM] + [VMEM] * 5,
        out_specs=(VMEM, VMEM),
        scratch_shapes=[pltpu.VMEM((2 * size, size), jnp.float32), pltpu.VMEM((size, size), jnp.float32)],
        compiler_params=params(12),
        name="factor_and_project",
    )(place, *quarters, both)


def shards(stiffness_tiles, tile_cols, send_rows, block, lower_bound, upper_bound):
    rows, nnz, tile, _ = stiffness_tiles.shape
    dof_total = block.shape[0] * lax.axis_size(DOF)
    ghosts = 2 * send_rows.shape[1]
    place = jnp.stack([lax.axis_index(M), lax.axis_index(C)]).astype(jnp.int32)
    bounds = (lower_bound, upper_bound)

    level_0, far, near = pick_lists(place, send_rows, block.T, tile)
    far, near = swapped_between_chips(far), flipped(near, C, 1)
    table, order = make_plan(place, send_rows, tile_cols.T, ghosts)
    tiles, total = stage_and_sum(table, stiffness_tiles.reshape(rows * nnz, tile, tile), level_0, rows, nnz)

    def level(index, total, near, far, field, previous=None):
        known = (nnz, place, table, order, bounds, tiles, total, near, far, field, previous)
        new_far, new_near = next_lists(index, *known)
        arrived = flipped(new_near, C, 1), swapped_between_chips(new_far)
        field = next_level(index, *known, new_far, new_near)
        return field, *arrived, local_sums(index + 1, table, tiles, field, rows, nnz)

    level_1, near, far, total = level(1, total, near, far, level_0)
    filtered, near, far, total = level(2, total, near, far, level_1, level_0)
    partner = flipped(filtered, M, 1)
    image = image_rows(nnz, place, table, tiles, total, near, far)
    keep, send, both = partial_sums(place, filtered, partner, image)
    quarter = sum_over_chips(keep + flipped(send, C, 1))
    quarters = (quarter, flipped(quarter, C, 1), flipped(quarter, M, 1), flipped(quarter, (C, M), 3))
    basis, ritz = factor_and_project(place, quarters, both, dof_total)
    return (basis.T, ritz)


def solution(mesh):
    torus = Mesh(mesh.devices.reshape(4, 4, 4, 2, mesh.shape["mode"]), DOF + (M,))
    return jax.shard_map(
        shards,
        mesh=torus,
        in_specs=(P(DOF, None, None, None), P(DOF, None), P(DOF, None), P(DOF, M), P(), P()),
        out_specs=(P(DOF, M), P()),
        check_vma=False,
    )
```

time: 106 us -> 108 us (1.019); the launches traced: 105 us -> 109 us
  Pallas kernels: 41.9 us -> 44.4 us
    pallas_call x8 -> x11, Pallas kernels: 33.5 us -> 36.1 us  [the longest x2 8.43 us: local_sums(): pl.pallas_call(kernel, out_shape=shape((modes, width), jnp.float32), in_s...]
  transfers between devices with their start and end apart: 20 -> 20, of which waited for: 9 -> 9; matrix products, arithmetic and copies ran while one was open for 0% -> 0% of each run, Pallas kernels for 19% -> 26%
where the time goes in v3:
time: 108 us; the launch traced here: 109 us
  Pallas kernels  44.4 us (41%)
  starting transfers between devices  41.7 us (39%)
  waiting for transfers between devices  18.7 us (17%)
  between operations  2.12 us (2%)
  local copies, waits for them, and re-layouts  1.37 us (1%)
    ppermute x17, starting transfers between devices, flipped(): lax.ppermute(block, axis, [(i, i ^ bits) for i in range(lax.axis_size(axi...  32.7 us
    ppermute x17, waiting for transfers between devices, flipped(): lax.ppermute(block, axis, [(i, i ^ bits) for i in range(lax.axis_size(axi...  18.7 us
    ppermute x3, starting transfers between devices, swapped_between_chips(): return lax.ppermute(block, DOF, pairs + [(b, a) for a, b in pairs])  9.04 us
    pallas_call x2, Pallas kernels, local_sums(): pl.pallas_call(kernel, out_shape=shape((modes, width), jnp.float32), in_s...  8.43 us
    pallas_call x1, Pallas kernels, factor_and_project(): pl.pallas_call(kernel, out_shape=(shape((modes, width), both.dtype), shap...  8.3 us
    pallas_call x2, Pallas kernels, next_level(): pl.pallas_call(kernel, out_shape=shape(field.shape, field.dtype), in_spec...  7.66 us
    pallas_call x1, Pallas kernels, stage_and_sum(): pl.pallas_call(kernel, out_shape=(shape(tiles.shape, tiles.dtype), shape(...  5.98 us
    pallas_call x2, Pallas kernels, next_lists(): pl.pallas_call(kernel, out_shape=(shape(far.shape, far.dtype),) * 2, in_s...  5.43 us
  transfers between devices with their start and end apart: 20, of which 9 were waited for; matrix products, arithmetic and copies ran while one was open for 0% of the time, Pallas kernels for 26%

profile of v3, /device:TPU:1, one launch (start us, length us, event | category | flops | bytes accessed | tf_op | source)
XLA Modules:
  0.0 108.5 jit_solution(17390755869622541435)
XLA Ops:
  0.7 1.7 %pick_lists.1 = (bf16[64,4096]{1,0:T(8,128)(2,1)S(1)}, bf16[64,1024]{1,0:T(8,128)(2,1)S(1)}, bf16[64,1024]{1,0:T(8,128)(2,1)S(1)}) custom-call(s32[2]{0:T(128)S(1)} %pad_add_fusion.place, s32[2,8]{1,0:T(2,128)} %send.3, bf16[64,4096]{1,0:T(8,128)(2,1)} %bitcast.8), custom_call_target="tpu_custom_call" | custom-call | tf_op jit(solution)/shard_map/pick_lists/pallas_call | solution.py:60
  2.4 3.3 %collective-permute-start = (bf16[64,1024]{1,0:T(8,128)(2,1)S(1)}, bf16[64,1024]{1,0:T(8,128)(2,1)S(1)}, u32[]{:S(2)}, u32[]{:S(2)}) collective-permute-start(bf16[64,1024]{1,0:T(8,128)(2,1)S(1)} %get-tuple-element.23), channel_id=1, source_target_pairs={{0,2},{2,0},{1,3},{3,1},{4,6},{6,4},{5,7},{7,5},{8,10},{10,8},{9,1... | collective-permute-start | bytes 393224 | tf_op jit(solution)/shard_map/ppermute | solution.py:27
  5.7 1.9 %collective-permute-start.1 = (bf16[64,1024]{1,0:T(8,128)(2,1)S(1)}, bf16[64,1024]{1,0:T(8,128)(2,1)S(1)}, u32[]{:S(2)}, u32[]{:S(2)}) collective-permute-start(bf16[64,1024]{1,0:T(8,128)(2,1)S(1)} %get-tuple-element.24), channel_id=1, source_target_pairs={{2,4},{6,8},{10,12},{14,16},{18,20},{22,24},{26,28},{30,32},{34,36... | collective-permute-start | bytes 393224 | tf_op jit(solution)/shard_map/ppermute | solution.py:33
  8.9 0.7 copy-done
  9.6 0.7 copy-done.1
  10.3 1.3 %make_plan.1 = (s32[32,32]{1,0:T(8,128)S(1)}, s32[72]{0:T(128)S(1)}) custom-call(s32[2]{0:T(128)S(1)} %pad_add_fusion.place, s32[2,8]{1,0:T(2,128)S(1)} %copy-done.1, s32[10,32]{1,0:T(8,128)S(1)} %bitcast.6), custom_call_target="tpu_custom_call" | custom-call | tf_op jit(solution)/shard_map/make_plan/pallas_call | solution.py:115
  11.6 6.0 %stage_and_sum.1 = (bf16[320,128,128]{2,1,0:T(8,128)(2,1)S(1)}, f32[64,4096]{1,0:T(8,128)S(1)}) custom-call(s32[32,32]{1,0:T(8,128)S(1)} %get-tuple-element.18.table, bf16[320,128,128]{2,1,0:T(8,128)(2,1)} %bitcast.7, bf16[64,4096]{1,0:T(8,128)(2,1)S(1)} %get-tuple-element.20.field.rest_0_), custom_call_target="tpu_custom_call" | custom-call | flops 671088640 | bytes 10485760 | tf_op jit(solution)/shard_map/stage_and_sum/pallas_call | solution.py:166
  17.6 2.7 %next_lists_1.1 = (bf16[64,1024]{1,0:T(8,128)(2,1)S(1)}, bf16[64,1024]{1,0:T(8,128)(2,1)S(1)}) custom-call(s32[2]{0:T(128)S(1)} %pad_add_fusion.place, s32[32,32]{1,0:T(8,128)S(1)} %get-tuple-element.18.table, s32[72]{0:T(128)S(1)} %get-tuple-element.19.order, f32[1]{0:T(128)S(6)} %copy.8.lower, f32[1]{0:T(128)S(6)} %copy.9.upper, ...), custom_call_target="tpu_custom_call" | custom-call | tf_op jit(solution)/shard_map/next_lists_1/pallas_call | solution.py:271
  20.3 4.3 %collective-permute-start.3 = (bf16[64,1024]{1,0:T(8,128)(2,1)S(1)}, bf16[64,1024]{1,0:T(8,128)(2,1)S(1)}, u32[]{:S(2)}, u32[]{:S(2)}) collective-permute-start(bf16[64,1024]{1,0:T(8,128)(2,1)S(1)} %get-tuple-element.25.new_far), channel_id=1, source_target_pairs={{2,4},{6,8},{10,12},{14,16},{18,20},{22,24},{26,28},{30,32},{34,36... | collective-permute-start | bytes 393224 | tf_op jit(solution)/shard_map/ppermute | solution.py:33
  24.6 3.8 %next_level_1.1.field = bf16[64,4096]{1,0:T(8,128)(2,1)S(1)} custom-call(s32[2]{0:T(128)S(1)} %pad_add_fusion.place, s32[32,32]{1,0:T(8,128)S(1)} %get-tuple-element.18.table, s32[72]{0:T(128)S(1)} %get-tuple-element.19.order, f32[1]{0:T(128)S(6)} %copy.8.lower, f32[1]{0:T(128)S(6)} %copy.9.upper, bf16[320,128,128]{2,1,0:T(8,128)(2,1)S(1)} %get-tuple-element.21.tiles, ...), custom_call_target="tpu_custom_call" | custom-call | flops 335544320 | bytes 10485760 | tf_op jit(solution)/shard_map/next_level_1/pallas_call | solution.py:312
  28.4 4.2 %local_sums_2.1.total = f32[64,4096]{1,0:T(8,128)S(1)} custom-call(s32[32,32]{1,0:T(8,128)S(1)} %get-tuple-element.18.table, bf16[320,128,128]{2,1,0:T(8,128)(2,1)S(1)} %get-tuple-element.21.tiles, bf16[64,4096]{1,0:T(8,128)(2,1)S(1)} %next_level_1.1.field), custom_call_target="tpu_custom_call" | custom-call | flops 41943040 | tf_op jit(solution)/shard_map/local_sums_2/pallas_call | solution.py:191
  32.7 2.7 %next_lists_2.1 = (bf16[64,1024]{1,0:T(8,128)(2,1)S(1)}, bf16[64,1024]{1,0:T(8,128)(2,1)S(1)}) custom-call(s32[2]{0:T(128)S(1)} %pad_add_fusion.place, s32[32,32]{1,0:T(8,128)S(1)} %get-tuple-element.18.table, s32[72]{0:T(128)S(1)} %get-tuple-element.19.order, f32[1]{0:T(128)S(6)} %copy.8.lower, f32[1]{0:T(128)S(6)} %copy.9.upper, ...), custom_call_target="tpu_custom_call" | custom-call | tf_op jit(solution)/shard_map/next_lists_2/pallas_call | solution.py:271
  35.4 2.9 %collective-permute-start.6 = (bf16[64,1024]{1,0:T(8,128)(2,1)S(1)}, bf16[64,1024]{1,0:T(8,128)(2,1)S(1)}, u32[]{:S(2)}, u32[]{:S(2)}) collective-permute-start(bf16[64,1024]{1,0:T(8,128)(2,1)S(1)} %get-tuple-element.27.new_far), channel_id=1, source_target_pairs={{2,4},{6,8},{10,12},{14,16},{18,20},{22,24},{26,28},{30,32},{34,36... | collective-permute-start | bytes 393224 | tf_op jit(solution)/shard_map/ppermute | solution.py:33
  38.4 3.9 %next_level_2.1.field.own = bf16[64,4096]{1,0:T(8,128)(2,1)S(1)} custom-call(s32[2]{0:T(128)S(1)} %pad_add_fusion.place, s32[32,32]{1,0:T(8,128)S(1)} %get-tuple-element.18.table, s32[72]{0:T(128)S(1)} %get-tuple-element.19.order, f32[1]{0:T(128)S(6)} %copy.8.lower, f32[1]{0:T(128)S(6)} %copy.9.upper, bf16[320,128,128]{2,1,0:T(8,128)(2,1)S(1)} %get-tuple-element.21.tiles, ...), custom_call_target="tpu_custom_call" | custom-call | flops 335544320 | bytes 10485760 | tf_op jit(solution)/shard_map/next_level_2/pallas_call | solution.py:312
  42.3 1.6 %collective-permute-start.4 = (bf16[64,4096]{1,0:T(8,128)(2,1)S(1)}, bf16[64,4096]{1,0:T(8,128)(2,1)S(1)}, u32[]{:S(2)}, u32[]{:S(2)}) collective-permute-start(bf16[64,4096]{1,0:T(8,128)(2,1)S(1)} %next_level_2.1.field.own), channel_id=1, source_target_pairs={{0,1},{1,0},{2,3},{3,2},{4,5},{5,4},{6,7},{7,6},{8,9},{9,8},{10,11... | collective-permute-start | bytes 1572872 | tf_op jit(solution)/shard_map/ppermute | solution.py:27
  43.9 4.2 %local_sums_3.1.total = f32[64,4096]{1,0:T(8,128)S(1)} custom-call(s32[32,32]{1,0:T(8,128)S(1)} %get-tuple-element.18.table, bf16[320,128,128]{2,1,0:T(8,128)(2,1)S(1)} %get-tuple-element.21.tiles, bf16[64,4096]{1,0:T(8,128)(2,1)S(1)} %next_level_2.1.field.own), custom_call_target="tpu_custom_call" | custom-call | flops 41943040 | tf_op jit(solution)/shard_map/local_sums_3/pallas_call | solution.py:191
  48.2 4.6 %image_rows.1.image = bf16[64,4096]{1,0:T(8,128)(2,1)S(1)} custom-call(s32[2]{0:T(128)S(1)} %pad_add_fusion.place, s32[32,32]{1,0:T(8,128)S(1)} %get-tuple-element.18.table, bf16[320,128,128]{2,1,0:T(8,128)(2,1)S(1)} %get-tuple-element.21.tiles, f32[64,4096]{1,0:T(8,128)S(1)} %local_sums_3.1.total, bf16[64,1024]{1,0:T(8,128)(2,1)S(1)} %collective-permute-done.5.near, ...), custom_call_target="tpu_custom_call" | custom-call | flops 6710886400 | bytes 10485760 | tf_op jit(solution)/shard_map/image_rows/pallas_call | solution.py:343
  52.8 4.2 %collective-permute-done.4.partner = bf16[64,4096]{1,0:T(8,128)(2,1)S(1)} collective-permute-done((bf16[64,4096]{1,0:T(8,128)(2,1)S(1)}, bf16[64,4096]{1,0:T(8,128)(2,1)S(1)}, u32[]{:S(2)}, u32[]{:S(2)}) %collective-permute-start.4) | collective-permute-done | bytes 524320 | tf_op jit(solution)/shard_map/ppermute | solution.py:27
  57.0 1.1 %partial_sums.1 = (f32[64,128]{1,0:T(8,128)S(1)}, f32[64,128]{1,0:T(8,128)S(1)}, bf16[128,4096]{1,0:T(8,128)(2,1)S(1)}) custom-call(s32[2]{0:T(128)S(1)} %pad_add_fusion.place, bf16[64,4096]{1,0:T(8,128)(2,1)S(1)} %next_level_2.1.field.own, bf16[64,4096]{1,0:T(8,128)(2,1)S(1)} %collective-permute-done.4.partner, bf16[64,4096]{1,0:T(8,128)(2,1)S(1)} %image_rows.1.image), custom_call_target="tpu_custom_call" | custom-call | tf_op jit(solution)/shard_map/partial_sums/pallas_call | solution.py:372
  58.1 1.5 %collective-permute-start.7 = (f32[64,128]{1,0:T(8,128)S(1)}, f32[64,128]{1,0:T(8,128)S(1)}, u32[]{:S(2)}, u32[]{:S(2)}) collective-permute-start(f32[64,128]{1,0:T(8,128)S(1)} %get-tuple-element.30), channel_id=1, source_target_pairs={{0,2},{2,0},{1,3},{3,1},{4,6},{6,4},{5,7},{7,5},{8,10},{10,8},{9,1... | collective-permute-start | bytes 98312 | tf_op jit(solution)/shard_map/ppermute | solution.py:27
  59.6 0.9 collective-permute-done.7
  60.4 3.4 %collective-permute-start.10 = (f32[64,128]{1,0:T(8,128)S(1)}, f32[64,128]{1,0:T(8,128)S(1)}, u32[]{:S(2)}, u32[]{:S(2)}) collective-permute-start(f32[64,128]{1,0:T(8,128)S(1)} %add.30), channel_id=1, source_target_pairs={{0,48},{16,32},{32,16},{48,0},{1,49},{17,33},{33,17},{49,1},{2,50}... | collective-permute-start | bytes 98312 | tf_op jit(solution)/shard_map/ppermute | solution.py:27
  65.1 3.0 %collective-permute-done.9 = f32[64,128]{1,0:T(8,128)S(1)} collective-permute-done((f32[64,128]{1,0:T(8,128)S(1)}, f32[64,128]{1,0:T(8,128)S(1)}, u32[]{:S(2)}, u32[]{:S(2)}) %collective-permute-start.9) | collective-permute-done | bytes 32800 | tf_op jit(solution)/shard_map/ppermute | solution.py:27
  68.1 4.6 %collective-permute-start.13 = (f32[64,128]{1,0:T(8,128)S(1)}, f32[64,128]{1,0:T(8,128)S(1)}, u32[]{:S(2)}, u32[]{:S(2)}) collective-permute-start(f32[64,128]{1,0:T(8,128)S(1)} %add_add_fusion.2), channel_id=1, source_target_pairs={{0,12},{4,8},{8,4},{12,0},{1,13},{5,9},{9,5},{13,1},{2,14},{6,10},... | collective-permute-start | bytes 98312 | tf_op jit(solution)/shard_map/ppermute | solution.py:27
  72.7 0.7 collective-permute-start.11
  74.0 3.0 %collective-permute-done.12 = f32[64,128]{1,0:T(8,128)S(1)} collective-permute-done((f32[64,128]{1,0:T(8,128)S(1)}, f32[64,128]{1,0:T(8,128)S(1)}, u32[]{:S(2)}, u32[]{:S(2)}) %collective-permute-start.12) | collective-permute-done | bytes 32800 | tf_op jit(solution)/shard_map/ppermute | solution.py:27
  77.0 7.8 %collective-permute-start.16 = (f32[64,128]{1,0:T(8,128)S(1)}, f32[64,128]{1,0:T(8,128)S(1)}, u32[]{:S(2)}, u32[]{:S(2)}) collective-permute-start(f32[64,128]{1,0:T(8,128)S(1)} %add_add_fusion.1), channel_id=1, source_target_pairs={{0,192},{64,128},{128,64},{192,0},{1,193},{65,129},{129,65},{193,1... | collective-permute-start | bytes 98312 | tf_op jit(solution)/shard_map/ppermute | solution.py:27
  84.8 2.6 %collective-permute-start.15 = (f32[64,128]{1,0:T(8,128)S(1)}, f32[64,128]{1,0:T(8,128)S(1)}, u32[]{:S(2)}, u32[]{:S(2)}) collective-permute-start(f32[64,128]{1,0:T(8,128)S(1)} %add_add_fusion.1), channel_id=1, source_target_pairs={{0,128},{64,192},{128,0},{192,64},{1,129},{65,193},{129,1},{193,65... | collective-permute-start | bytes 98312 | tf_op jit(solution)/shard_map/ppermute | solution.py:27
  87.4 4.2 %collective-permute-done.15 = f32[64,128]{1,0:T(8,128)S(1)} collective-permute-done((f32[64,128]{1,0:T(8,128)S(1)}, f32[64,128]{1,0:T(8,128)S(1)}, u32[]{:S(2)}, u32[]{:S(2)}) %collective-permute-start.15) | collective-permute-done | bytes 32800 | tf_op jit(solution)/shard_map/ppermute | solution.py:27
  91.6 5.8 %collective-permute-start.19 = (f32[64,128]{1,0:T(8,128)S(1)}, f32[64,128]{1,0:T(8,128)S(1)}, u32[]{:S(2)}, u32[]{:S(2)}) collective-permute-start(f32[64,128]{1,0:T(8,128)S(1)} %add_add_fusion.own), channel_id=1, source_target_pairs={{0,3},{1,2},{2,1},{3,0},{4,7},{5,6},{6,5},{7,4},{8,11},{9,10},{10,... | collective-permute-start | bytes 98312 | tf_op jit(solution)/shard_map/ppermute | solution.py:27
  97.9 1.7 %collective-permute-done.19.last = f32[64,128]{1,0:T(8,128)S(1)} collective-permute-done((f32[64,128]{1,0:T(8,128)S(1)}, f32[64,128]{1,0:T(8,128)S(1)}, u32[]{:S(2)}, u32[]{:S(2)}) %collective-permute-start.19) | collective-permute-done | bytes 32800 | tf_op jit(solution)/shard_map/ppermute | solution.py:27
  100.2 8.3 %factor_and_project.1 = (bf16[64,4096]{1,0:T(8,128)(2,1)}, f32[128,128]{1,0:T(8,128)}) custom-call(s32[2]{0:T(128)S(1)} %pad_add_fusion.place, f32[64,128]{1,0:T(8,128)S(1)} %add_add_fusion.own, f32[64,128]{1,0:T(8,128)S(1)} %collective-permute-done.17.other_core, f32[64,128]{1,0:T(8,128)S(1)} %collective-permute-done.18.other_mode, ...), custom_call_target="tpu_custom_call" | custom-call | tf_op jit(solution)/shard_map/factor_and_project/pallas_call | solution.py:460
  (29 shorter events, 3.3 us)
Async XLA Ops:
  2.4 15.2 %collective-permute-start = (bf16[64,1024]{1,0:T(8,128)(2,1)S(1)}, bf16[64,1024]{1,0:T(8,128)(2,1)S(1)}, u32[]{:S(2)}, u32[]{:S(2)}) collective-permute-start(bf16[64,1024]{1,0:T(8,128)(2,1)S(1)} %get-tuple-element.23), channel_id=1, source_target_pairs={{0,2},{2,0},{1,3},{3,1},{4,6},{6,4},{5,7},{7,5},{8,10},{10,8},{9,1... | collective-permute-start | bytes 393224 | tf_op jit(solution)/shard_map/ppermute | solution.py:27
  5.7 11.9 %collective-permute-start.1 = (bf16[64,1024]{1,0:T(8,128)(2,1)S(1)}, bf16[64,1024]{1,0:T(8,128)(2,1)S(1)}, u32[]{:S(2)}, u32[]{:S(2)}) collective-permute-start(bf16[64,1024]{1,0:T(8,128)(2,1)S(1)} %get-tuple-element.24), channel_id=1, source_target_pairs={{2,4},{6,8},{10,12},{14,16},{18,20},{22,24},{26,28},{30,32},{34,36... | collective-permute-start | bytes 393224 | tf_op jit(solution)/shard_map/ppermute | solution.py:33
  8.9 0.7 copy-start
  9.6 0.7 copy-start.1
  20.3 12.4 %collective-permute-start.3 = (bf16[64,1024]{1,0:T(8,128)(2,1)S(1)}, bf16[64,1024]{1,0:T(8,128)(2,1)S(1)}, u32[]{:S(2)}, u32[]{:S(2)}) collective-permute-start(bf16[64,1024]{1,0:T(8,128)(2,1)S(1)} %get-tuple-element.25.new_far), channel_id=1, source_target_pairs={{2,4},{6,8},{10,12},{14,16},{18,20},{22,24},{26,28},{30,32},{34,36... | collective-permute-start | bytes 393224 | tf_op jit(solution)/shard_map/ppermute | solution.py:33
  24.5 8.1 %collective-permute-start.2 = (bf16[64,1024]{1,0:T(8,128)(2,1)S(1)}, bf16[64,1024]{1,0:T(8,128)(2,1)S(1)}, u32[]{:S(2)}, u32[]{:S(2)}) collective-permute-start(bf16[64,1024]{1,0:T(8,128)(2,1)S(1)} %get-tuple-element.26.new_near), channel_id=1, source_target_pairs={{0,2},{2,0},{1,3},{3,1},{4,6},{6,4},{5,7},{7,5},{8,10},{10,8},{9,1... | collective-permute-start | bytes 393224 | tf_op jit(solution)/shard_map/ppermute | solution.py:27
  35.4 12.8 %collective-permute-start.6 = (bf16[64,1024]{1,0:T(8,128)(2,1)S(1)}, bf16[64,1024]{1,0:T(8,128)(2,1)S(1)}, u32[]{:S(2)}, u32[]{:S(2)}) collective-permute-start(bf16[64,1024]{1,0:T(8,128)(2,1)S(1)} %get-tuple-element.27.new_far), channel_id=1, source_target_pairs={{2,4},{6,8},{10,12},{14,16},{18,20},{22,24},{26,28},{30,32},{34,36... | collective-permute-start | bytes 393224 | tf_op jit(solution)/shard_map/ppermute | solution.py:33
  38.3 9.9 %collective-permute-start.5 = (bf16[64,1024]{1,0:T(8,128)(2,1)S(1)}, bf16[64,1024]{1,0:T(8,128)(2,1)S(1)}, u32[]{:S(2)}, u32[]{:S(2)}) collective-permute-start(bf16[64,1024]{1,0:T(8,128)(2,1)S(1)} %get-tuple-element.28.new_near), channel_id=1, source_target_pairs={{0,2},{2,0},{1,3},{3,1},{4,6},{6,4},{5,7},{7,5},{8,10},{10,8},{9,1... | collective-permute-start | bytes 393224 | tf_op jit(solution)/shard_map/ppermute | solution.py:27
  42.3 14.7 %collective-permute-start.4 = (bf16[64,4096]{1,0:T(8,128)(2,1)S(1)}, bf16[64,4096]{1,0:T(8,128)(2,1)S(1)}, u32[]{:S(2)}, u32[]{:S(2)}) collective-permute-start(bf16[64,4096]{1,0:T(8,128)(2,1)S(1)} %next_level_2.1.field.own), channel_id=1, source_target_pairs={{0,1},{1,0},{2,3},{3,2},{4,5},{5,4},{6,7},{7,6},{8,9},{9,8},{10,11... | collective-permute-start | bytes 1572872 | tf_op jit(solution)/shard_map/ppermute | solution.py:27
  58.1 2.3 %collective-permute-start.7 = (f32[64,128]{1,0:T(8,128)S(1)}, f32[64,128]{1,0:T(8,128)S(1)}, u32[]{:S(2)}, u32[]{:S(2)}) collective-permute-start(f32[64,128]{1,0:T(8,128)S(1)} %get-tuple-element.30), channel_id=1, source_target_pairs={{0,2},{2,0},{1,3},{3,1},{4,6},{6,4},{5,7},{7,5},{8,10},{10,8},{9,1... | collective-permute-start | bytes 98312 | tf_op jit(solution)/shard_map/ppermute | solution.py:27
  60.4 4.7 %collective-permute-start.10 = (f32[64,128]{1,0:T(8,128)S(1)}, f32[64,128]{1,0:T(8,128)S(1)}, u32[]{:S(2)}, u32[]{:S(2)}) collective-permute-start(f32[64,128]{1,0:T(8,128)S(1)} %add.30), channel_id=1, source_target_pairs={{0,48},{16,32},{32,16},{48,0},{1,49},{17,33},{33,17},{49,1},{2,50}... | collective-permute-start | bytes 98312 | tf_op jit(solution)/shard_map/ppermute | solution.py:27
  63.8 4.3 %collective-permute-start.9 = (f32[64,128]{1,0:T(8,128)S(1)}, f32[64,128]{1,0:T(8,128)S(1)}, u32[]{:S(2)}, u32[]{:S(2)}) collective-permute-start(f32[64,128]{1,0:T(8,128)S(1)} %add.30), channel_id=1, source_target_pairs={{0,32},{16,48},{32,0},{48,16},{1,33},{17,49},{33,1},{49,17},{2,34}... | collective-permute-start | bytes 98312 | tf_op jit(solution)/shard_map/ppermute | solution.py:27
  64.0 4.0 %collective-permute-start.8 = (f32[64,128]{1,0:T(8,128)S(1)}, f32[64,128]{1,0:T(8,128)S(1)}, u32[]{:S(2)}, u32[]{:S(2)}) collective-permute-start(f32[64,128]{1,0:T(8,128)S(1)} %add.30), channel_id=1, source_target_pairs={{0,16},{16,0},{32,48},{48,32},{1,17},{17,1},{33,49},{49,33},{2,18}... | collective-permute-start | bytes 98312 | tf_op jit(solution)/shard_map/ppermute | solution.py:27
  68.1 6.0 %collective-permute-start.13 = (f32[64,128]{1,0:T(8,128)S(1)}, f32[64,128]{1,0:T(8,128)S(1)}, u32[]{:S(2)}, u32[]{:S(2)}) collective-permute-start(f32[64,128]{1,0:T(8,128)S(1)} %add_add_fusion.2), channel_id=1, source_target_pairs={{0,12},{4,8},{8,4},{12,0},{1,13},{5,9},{9,5},{13,1},{2,14},{6,10},... | collective-permute-start | bytes 98312 | tf_op jit(solution)/shard_map/ppermute | solution.py:27
  72.7 4.3 %collective-permute-start.12 = (f32[64,128]{1,0:T(8,128)S(1)}, f32[64,128]{1,0:T(8,128)S(1)}, u32[]{:S(2)}, u32[]{:S(2)}) collective-permute-start(f32[64,128]{1,0:T(8,128)S(1)} %add_add_fusion.2), channel_id=1, source_target_pairs={{0,8},{4,12},{8,0},{12,4},{1,9},{5,13},{9,1},{13,5},{2,10},{6,14},... | collective-permute-start | bytes 98312 | tf_op jit(solution)/shard_map/ppermute | solution.py:27
  72.7 4.3 %collective-permute-start.11 = (f32[64,128]{1,0:T(8,128)S(1)}, f32[64,128]{1,0:T(8,128)S(1)}, u32[]{:S(2)}, u32[]{:S(2)}) collective-permute-start(f32[64,128]{1,0:T(8,128)S(1)} %add_add_fusion.2), channel_id=1, source_target_pairs={{0,4},{4,0},{8,12},{12,8},{1,5},{5,1},{9,13},{13,9},{2,6},{6,2},{1... | collective-permute-start | bytes 98312 | tf_op jit(solution)/shard_map/ppermute | solution.py:27
  77.0 10.4 %collective-permute-start.16 = (f32[64,128]{1,0:T(8,128)S(1)}, f32[64,128]{1,0:T(8,128)S(1)}, u32[]{:S(2)}, u32[]{:S(2)}) collective-permute-start(f32[64,128]{1,0:T(8,128)S(1)} %add_add_fusion.1), channel_id=1, source_target_pairs={{0,192},{64,128},{128,64},{192,0},{1,193},{65,129},{129,65},{193,1... | collective-permute-start | bytes 98312 | tf_op jit(solution)/shard_map/ppermute | solution.py:27
  84.8 6.8 %collective-permute-start.15 = (f32[64,128]{1,0:T(8,128)S(1)}, f32[64,128]{1,0:T(8,128)S(1)}, u32[]{:S(2)}, u32[]{:S(2)}) collective-permute-start(f32[64,128]{1,0:T(8,128)S(1)} %add_add_fusion.1), channel_id=1, source_target_pairs={{0,128},{64,192},{128,0},{192,64},{1,129},{65,193},{129,1},{193,65... | collective-permute-start | bytes 98312 | tf_op jit(solution)/shard_map/ppermute | solution.py:27
  87.4 4.2 %collective-permute-start.14 = (f32[64,128]{1,0:T(8,128)S(1)}, f32[64,128]{1,0:T(8,128)S(1)}, u32[]{:S(2)}, u32[]{:S(2)}) collective-permute-start(f32[64,128]{1,0:T(8,128)S(1)} %add_add_fusion.1), channel_id=1, source_target_pairs={{0,64},{64,0},{128,192},{192,128},{1,65},{65,1},{129,193},{193,129... | collective-permute-start | bytes 98312 | tf_op jit(solution)/shard_map/ppermute | solution.py:27
  91.6 8.0 %collective-permute-start.19 = (f32[64,128]{1,0:T(8,128)S(1)}, f32[64,128]{1,0:T(8,128)S(1)}, u32[]{:S(2)}, u32[]{:S(2)}) collective-permute-start(f32[64,128]{1,0:T(8,128)S(1)} %add_add_fusion.own), channel_id=1, source_target_pairs={{0,3},{1,2},{2,1},{3,0},{4,7},{5,6},{6,5},{7,4},{8,11},{9,10},{10,... | collective-permute-start | bytes 98312 | tf_op jit(solution)/shard_map/ppermute | solution.py:27
  97.5 2.8 %collective-permute-start.18 = (f32[64,128]{1,0:T(8,128)S(1)}, f32[64,128]{1,0:T(8,128)S(1)}, u32[]{:S(2)}, u32[]{:S(2)}) collective-permute-start(f32[64,128]{1,0:T(8,128)S(1)} %add_add_fusion.own), channel_id=1, source_target_pairs={{0,1},{1,0},{2,3},{3,2},{4,5},{5,4},{6,7},{7,6},{8,9},{9,8},{10,11... | collective-permute-start | bytes 98312 | tf_op jit(solution)/shard_map/ppermute | solution.py:27
  97.8 2.4 %collective-permute-start.17 = (f32[64,128]{1,0:T(8,128)S(1)}, f32[64,128]{1,0:T(8,128)S(1)}, u32[]{:S(2)}, u32[]{:S(2)}) collective-permute-start(f32[64,128]{1,0:T(8,128)S(1)} %add_add_fusion.own), channel_id=1, source_target_pairs={{0,2},{2,0},{1,3},{3,1},{4,6},{6,4},{5,7},{7,5},{8,10},{10,8},{9,1... | collective-permute-start | bytes 98312 | tf_op jit(solution)/shard_map/ppermute | solution.py:27

commit v4 on v3

--- a/solution.py
+++ b/solution.py
@@ -72,66 +72,53 @@
     )
 
 
-def make_plan(place, send_rows, tile_cols, ghosts):
-    nnz, rows = tile_cols.shape
-    count = send_rows.shape[1]
-
-    def kernel(place, send, cols, table, order, taken):
-        code = [cols[k : k + 1, :] for k in range(nnz)]
-        local = [(one < rows).astype(jnp.int32) for one in code]
-        locals_before, total = [], jnp.zeros_like(code[0])
-        for one in local:
-            locals_before.append(total)
-            total = total + one
-        position = [
-            jnp.where(local[k] == 1, locals_before[k], total + k - locals_before[k]) for k in range(nnz)
-        ]
-        for p in range(nnz):
-            source, entry = jnp.zeros_like(total), jnp.zeros_like(total)
-            for k in range(nnz):
-                source = jnp.where(position[k] == p, code[k], source)
-                entry = jnp.where(position[k] == p, k, entry)
-            table[p : p + 1, :] = jnp.where(p < total, source, rows)
-            table[nnz + p : nnz + p + 1, :] = jnp.where(p < total, ghosts, source - rows)
-            table[2 * nnz + p : 2 * nnz + p + 1, :] = entry
-        table[3 * nnz : 3 * nnz + 1, :] = nnz // 2 - (total >> 1)
-
-        core = place[1]
-        for row in range(rows):
-            taken[row] = 0
-        for slot in range(count):
-            for start, which in ((0, core), (count, 1 - core)):
-                row = send[which, slot]
-                taken[row] = 1
-                order[start + slot] = row
-        at = jnp.int32(2 * count)
-        for row in range(rows):
-            order[at] = row
-            at = at + 1 - taken[row]
-        for i in range(GROUP):
-            order[at + i] = order[0]
-        order[2 * rows] = (at + GROUP - 1) // GROUP
-
-    return pl.pallas_call(
-        kernel,
-        out_shape=(shape((3 * nnz + 2, rows), jnp.int32), shape((2 * rows + 8,), jnp.int32)),
-        in_specs=[SMEM, SMEM, VMEM],
-        out_specs=(VMEM, SMEM),
-        scratch_shapes=[pltpu.SMEM((rows,), jnp.int32)],
-        compiler_params=params(4),
-        name="make_plan",
-    )(place, send_rows, tile_cols)
+def make_plan(core, code, send, table, order, taken):
+    nnz, rows, count = len(code), code[0].shape[1], send.shape[1]
+    local = [(one < rows).astype(jnp.int32) for one in code]
+    locals_before, total = [], jnp.zeros_like(code[0])
+    for one in local:
+        locals_before.append(total)
+        total = total + one
+    position = [jnp.where(local[k] == 1, locals_before[k], total + k - locals_before[k]) for k in range(nnz)]
+    for p in range(nnz):
+        source, entry = jnp.zeros_like(total), jnp.zeros_like(total)
+        for k in range(nnz):
+            source = jnp.where(position[k] == p, code[k], source)
+            entry = jnp.where(position[k] == p, k, entry)
+        table[p : p + 1, :] = jnp.where(p < total, source, rows)
+        table[nnz + p : nnz + p + 1, :] = jnp.where(p < total, 2 * count, source - rows)
+        table[2 * nnz + p : 2 * nnz + p + 1, :] = entry
+    table[3 * nnz : 3 * nnz + 1, :] = nnz // 2 - (total >> 1)
+
+    for row in range(rows):
+        taken[row] = 0
+    for slot in range(count):
+        for start, which in ((0, core), (count, 1 - core)):
+            row = send[which, slot]
+            taken[row] = 1
+            order[start + slot] = row
+    at = jnp.int32(2 * count)
+    for row in range(rows):
+        order[at] = row
+        at = at + 1 - taken[row]
+    for i in range(GROUP):
+        order[at + i] = order[0]
+    order[2 * rows] = (at + GROUP - 1) // GROUP
 
 
 def local_rows(table, tiles, sources, total, step, nnz):
-    tile = tiles.shape[1]
     for u in range(GROUP):
         row = step * GROUP + u
-        source = [sources[:, columns(table[p, row], tile)] for p in range(nnz - 2)]
-        stored = [tiles[row * nnz + table[2 * nnz + p, row]] for p in range(nnz - 2)]
-        total[:, columns(row, tile)] = lax.dot_general(
-            jnp.concatenate(source, axis=1), jnp.concatenate(stored, axis=1), NT, preferred_element_type=jnp.float32
-        )
+        total[:, columns(row, tiles.shape[1])] = summed(table, tiles, sources, row, 0, range(nnz - 2), nnz)
+
+
+def summed(table, tiles, sources, row, kind, positions, nnz):
+    tile = tiles.shape[1]
+    source = [sources[:, columns(table[kind * nnz + p, row], tile)] for p in positions]
+    stored = [tiles[row * nnz + table[2 * nnz + p, row]] for p in positions]
+    return jnp.dot(
+        jnp.concatenate(source, axis=1), jnp.concatenate(stored, axis=0), preferred_element_type=jnp.float32
+    )
 
 
 def fill_sources(field, sources):
@@ -140,39 +127,80 @@
     sources[:, width:] = jnp.zeros((field.shape[0], sources.shape[1] - width), sources.dtype)
 
 
-def stage_and_sum(table, tiles, field, rows, nnz):
+def stage_and_sum(place, send_rows, tile_cols, tiles, field):
     modes, width = field.shape
+    nnz, rows = tile_cols.shape
     tile = tiles.shape[1]
     per_chunk = GROUP // 2 * nnz
     chunks = rows * nnz // per_chunk
-
-    def kernel(table, tiles, field, staged, total, sources, sems):
+    table_shape = (3 * nnz + 2, rows)
+
+    def kernel(place, send_hbm, cols_hbm, tiles, field, staged, total, table, order, *scratch):
+        sources, raw, cols, made, send, taken, sems, small = scratch
+
         def chunk(i):
             here = pl.ds(i * per_chunk, per_chunk)
-            return pltpu.make_async_copy(tiles.at[here], staged.at[here], sems.at[i])
-
+            return pltpu.make_async_copy(tiles.at[here], raw.at[here], sems.at[i])
+
+        lists = [
+            pltpu.make_async_copy(send_hbm, send, small.at[0]),
+            pltpu.make_async_copy(cols_hbm, cols, small.at[1]),
+        ]
+        for copy in lists:
+            copy.start()
         for i in range(chunks):
             chunk(i).start()
         fill_sources(field, sources)
+        for copy in lists:
+            copy.wait()
+        make_plan(place[1], [cols[k : k + 1, :] for k in range(nnz)], send, made, order, taken)
+        copy = pltpu.make_async_copy(made, table, small.at[2])
+        copy.start()
+        copy.wait()
 
         def step(i, carry):
             chunk(2 * i).wait()
             chunk(2 * i + 1).wait()
+
+            def turn(j, carry):
+                for u in range(GROUP):
+                    at = i * 2 * per_chunk + j * GROUP + u
+                    staged[at] = raw[at].T
+                return carry
+
+            lax.fori_loop(0, 2 * per_chunk // GROUP, turn, 0)
             local_rows(table, staged, sources, total, i, nnz)
             return carry
 
         lax.fori_loop(0, rows // GROUP, step, 0)
 
-    return pl.pallas_call(
-        kernel,
-        out_shape=(shape(tiles.shape, tiles.dtype), shape((modes, width), jnp.float32)),
-        in_specs=[SMEM, HBM, VMEM],
-        out_specs=(VMEM, VMEM),
-        scratch_shapes=[pltpu.VMEM((modes, width + tile), field.dtype), pltpu.SemaphoreType.DMA((chunks,))],
-        compiler_params=params(8),
+    def in_hbm(array):
+        return pltpu.with_memory_space_constraint(array, pltpu.HBM)
+
+    return pl.pallas_call(
+        kernel,
+        out_shape=(
+            shape(tiles.shape, tiles.dtype),
+            shape((modes, width), jnp.float32),
+            shape(table_shape, jnp.int32),
+            shape((2 * rows + 8,), jnp.int32),
+        ),
+        in_specs=[SMEM, HBM, HBM, HBM, VMEM],
+        out_specs=(VMEM, VMEM, SMEM, SMEM),
+        scratch_shapes=[
+            pltpu.VMEM((modes, width + tile), field.dtype),
+            pltpu.VMEM(tiles.shape, tiles.dtype),
+            pltpu.VMEM(tile_cols.shape, jnp.int32),
+            pltpu.VMEM(table_shape, jnp.int32),
+            pltpu.SMEM(send_rows.shape, jnp.int32),
+            pltpu.SMEM((rows,), jnp.int32),
+            pltpu.SemaphoreType.DMA((chunks,)),
+            pltpu.SemaphoreType.DMA((3,)),
+        ],
+        compiler_params=params(16),
         cost_estimate=pl.CostEstimate(flops=2 * tiles.size * modes, bytes_accessed=2 * tiles.size, transcendentals=0),
         name="stage_and_sum",
-    )(table, pltpu.with_memory_space_constraint(tiles, pltpu.HBM), field)
+    )(place, in_hbm(send_rows), in_hbm(tile_cols), in_hbm(tiles), field)
 
 
 def local_sums(level, table, tiles, field, rows, nnz):
@@ -213,25 +241,17 @@
     most = table[3 * nnz, rows[0]]
     for row in rows[1:]:
         most = jnp.maximum(most, table[3 * nnz, row])
-
-    def add(q):
+    usual = 3
+    for u, row in enumerate(rows):
+        positions = range(nnz - 2 * usual, nnz)
+        partial[:, u * tile : (u + 1) * tile] = summed(table, tiles, ghosts, row, 1, positions, nnz)
+
+    @pl.when(most > usual)
+    def _():
         for u, row in enumerate(rows):
-            source = [ghosts[:, columns(table[nnz + 2 * q + i, row], tile)] for i in range(2)]
-            stored = [tiles[row * nnz + table[2 * nnz + 2 * q + i, row]] for i in range(2)]
-            product = lax.dot_general(
-                jnp.concatenate(source, axis=1),
-                jnp.concatenate(stored, axis=1),
-                NT,
-                preferred_element_type=jnp.float32,
-            )
             here = slice(u * tile, (u + 1) * tile)
-            partial[:, here] = product if q == nnz // 2 - 1 else partial[:, here] + product
-
-    for q in reversed(range(nnz // 2)):
-        if q == nnz // 2 - 1:
-            add(q)
-        else:
-            pl.when(most >= nnz // 2 - q)(lambda q=q: add(q))
+            partial[:, here] = partial[:, here] + summed(table, tiles, ghosts, row, 1, range(nnz - 2 * usual), nnz)
+
     return rows
 
 
@@ -471,14 +491,14 @@
 def shards(stiffness_tiles, tile_cols, send_rows, block, lower_bound, upper_bound):
     rows, nnz, tile, _ = stiffness_tiles.shape
     dof_total = block.shape[0] * lax.axis_size(DOF)
-    ghosts = 2 * send_rows.shape[1]
     place = jnp.stack([lax.axis_index(M), lax.axis_index(C)]).astype(jnp.int32)
     bounds = (lower_bound, upper_bound)
 
     level_0, far, near = pick_lists(place, send_rows, block.T, tile)
     far, near = swapped_between_chips(far), flipped(near, C, 1)
-    table, order = make_plan(place, send_rows, tile_cols.T, ghosts)
-    tiles, total = stage_and_sum(table, stiffness_tiles.reshape(rows * nnz, tile, tile), level_0, rows, nnz)
+    tiles, total, table, order = stage_and_sum(
+        place, send_rows, tile_cols.T, stiffness_tiles.reshape(rows * nnz, tile, tile), level_0
+    )
 
     def level(index, total, near, far, field, previous=None):
         known = (nnz, place, table, order, bounds, tiles, total, near, far, field, previous)

time: 108 us -> 109 us (level); the launches traced: 109 us -> 108 us
  Pallas kernels: 44.4 us -> 40.3 us
  waiting for transfers between devices: 18.7 us -> 21.6 us
  starting transfers between devices: 41.7 us -> 44.2 us
  local copies, waits for them, and re-layouts: 1.37 us -> 0 us
    pallas_call x1, Pallas kernels: 5.98 us -> 12.5 us  [stage_and_sum(): pl.pallas_call(kernel, out_shape=(shape(tiles.shape, tiles.dtype), shape(...]
    ppermute x17, starting transfers between devices: 32.7 us -> 35.8 us  [flipped(): lax.ppermute(block, axis, [(i, i ^ bits) for i in range(lax.axis_size(axi...]
    pallas_call x2, Pallas kernels: 8.43 us -> 5.48 us  [local_sums(): pl.pallas_call(kernel, out_shape=shape((modes, width), jnp.float32), in_s...]
    ppermute x17, waiting for transfers between devices: 18.7 us -> 21.6 us  [flipped(): lax.ppermute(block, axis, [(i, i ^ bits) for i in range(lax.axis_size(axi...]
    pallas_call x2, Pallas kernels: 7.66 us -> 4.87 us  [next_level(): pl.pallas_call(kernel, out_shape=shape(field.shape, field.dtype), in_spec...]
    pallas_call x1, Pallas kernels: 4.61 us -> 2.69 us  [image_rows(): pl.pallas_call(kernel, out_shape=shape((modes, width), near.dtype), in_sp...]
    pallas_call x2, Pallas kernels: 5.43 us -> 3.71 us  [next_lists(): pl.pallas_call(kernel, out_shape=(shape(far.shape, far.dtype),) * 2, in_s...]
    unnamed x4 -> x0, local copies, waits for them, and re-layouts: 1.37 us -> none
  transfers between devices with their start and end apart: 20 -> 20, of which waited for: 9 -> 10; matrix products, arithmetic and copies ran while one was open for 0% -> 0% of each run, Pallas kernels for 26% -> 24%
where the time goes in v4:
time: 109 us; the launch traced here: 108 us
  starting transfers between devices  44.2 us (41%)
  Pallas kernels  40.3 us (37%)
  waiting for transfers between devices  21.6 us (20%)
  between operations  2.12 us (2%)
    ppermute x17, starting transfers between devices, flipped(): lax.ppermute(block, axis, [(i, i ^ bits) for i in range(lax.axis_size(axi...  35.8 us
    ppermute x17, waiting for transfers between devices, flipped(): lax.ppermute(block, axis, [(i, i ^ bits) for i in range(lax.axis_size(axi...  21.6 us
    pallas_call x1, Pallas kernels, stage_and_sum(): pl.pallas_call(kernel, out_shape=(shape(tiles.shape, tiles.dtype), shape(...  12.5 us
    ppermute x3, starting transfers between devices, swapped_between_chips(): return lax.ppermute(block, DOF, pairs + [(b, a) for a, b in pairs])  8.38 us
    pallas_call x1, Pallas kernels, factor_and_project(): pl.pallas_call(kernel, out_shape=(shape((modes, width), both.dtype), shap...  8.3 us
    pallas_call x2, Pallas kernels, local_sums(): pl.pallas_call(kernel, out_shape=shape((modes, width), jnp.float32), in_s...  5.48 us
    pallas_call x2, Pallas kernels, next_level(): pl.pallas_call(kernel, out_shape=shape(field.shape, field.dtype), in_spec...  4.87 us
    pallas_call x2, Pallas kernels, next_lists(): pl.pallas_call(kernel, out_shape=(shape(far.shape, far.dtype),) * 2, in_s...  3.71 us
  transfers between devices with their start and end apart: 20, of which 10 were waited for; matrix products, arithmetic and copies ran while one was open for 0% of the time, Pallas kernels for 24%

profile of v4, /device:TPU:1, one launch (start us, length us, event | category | flops | bytes accessed | tf_op | source)
XLA Modules:
  0.0 108.3 jit_solution(8239944405216223251)
XLA Ops:
  0.7 1.7 %pick_lists.1 = (bf16[64,4096]{1,0:T(8,128)(2,1)S(1)}, bf16[64,1024]{1,0:T(8,128)(2,1)S(1)}, bf16[64,1024]{1,0:T(8,128)(2,1)S(1)}) custom-call(s32[2]{0:T(128)S(1)} %pad_add_fusion.place, s32[2,8]{1,0:T(2,128)} %send_hbm.1, bf16[64,4096]{1,0:T(8,128)(2,1)} %bitcast.7), custom_call_target="tpu_custom_call" | custom-call | tf_op jit(solution)/shard_map/pick_lists/pallas_call | solution.py:60
  2.4 3.3 %collective-permute-start = (bf16[64,1024]{1,0:T(8,128)(2,1)S(1)}, bf16[64,1024]{1,0:T(8,128)(2,1)S(1)}, u32[]{:S(2)}, u32[]{:S(2)}) collective-permute-start(bf16[64,1024]{1,0:T(8,128)(2,1)S(1)} %get-tuple-element.23), channel_id=1, source_target_pairs={{0,2},{2,0},{1,3},{3,1},{4,6},{6,4},{5,7},{7,5},{8,10},{10,8},{9,1... | collective-permute-start | bytes 393224 | tf_op jit(solution)/shard_map/ppermute | solution.py:27
  5.7 1.9 %collective-permute-start.1 = (bf16[64,1024]{1,0:T(8,128)(2,1)S(1)}, bf16[64,1024]{1,0:T(8,128)(2,1)S(1)}, u32[]{:S(2)}, u32[]{:S(2)}) collective-permute-start(bf16[64,1024]{1,0:T(8,128)(2,1)S(1)} %get-tuple-element.24), channel_id=1, source_target_pairs={{2,4},{6,8},{10,12},{14,16},{18,20},{22,24},{26,28},{30,32},{34,36... | collective-permute-start | bytes 393224 | tf_op jit(solution)/shard_map/ppermute | solution.py:33
  8.9 12.5 %stage_and_sum.1 = (bf16[320,128,128]{2,1,0:T(8,128)(2,1)S(1)}, f32[64,4096]{1,0:T(8,128)S(1)}, s32[32,32]{1,0:T(8,128)S(1)}, s32[72]{0:T(128)S(1)}) custom-call(s32[2]{0:T(128)S(1)} %pad_add_fusion.place, s32[2,8]{1,0:T(2,128)} %send_hbm.1, s32[10,32]{1,0:T(8,128)} %bitcast.8, bf16[320,128,128]{2,1,0:T(8,128)(2,1)} %bitcast.6, ...), custom_call_target="tpu_custom_call" | custom-call | flops 671088640 | bytes 10485760 | tf_op jit(solution)/shard_map/stage_and_sum/pallas_call | solution.py:180
  21.4 1.8 %next_lists_1.1 = (bf16[64,1024]{1,0:T(8,128)(2,1)S(1)}, bf16[64,1024]{1,0:T(8,128)(2,1)S(1)}) custom-call(s32[2]{0:T(128)S(1)} %pad_add_fusion.place, s32[32,32]{1,0:T(8,128)S(1)} %get-tuple-element.19.table, s32[72]{0:T(128)S(1)} %get-tuple-element.20.order, f32[1]{0:T(128)S(6)} %copy.8.lower, f32[1]{0:T(128)S(6)} %copy.9.upper, ...), custom_call_target="tpu_custom_call" | custom-call | tf_op jit(solution)/shard_map/next_lists_1/pallas_call | solution.py:291
  23.3 3.9 %collective-permute-start.3 = (bf16[64,1024]{1,0:T(8,128)(2,1)S(1)}, bf16[64,1024]{1,0:T(8,128)(2,1)S(1)}, u32[]{:S(2)}, u32[]{:S(2)}) collective-permute-start(bf16[64,1024]{1,0:T(8,128)(2,1)S(1)} %get-tuple-element.25.new_far), channel_id=1, source_target_pairs={{2,4},{6,8},{10,12},{14,16},{18,20},{22,24},{26,28},{30,32},{34,36... | collective-permute-start | bytes 393224 | tf_op jit(solution)/shard_map/ppermute | solution.py:33
  27.3 2.4 %next_level_1.1.field = bf16[64,4096]{1,0:T(8,128)(2,1)S(1)} custom-call(s32[2]{0:T(128)S(1)} %pad_add_fusion.place, s32[32,32]{1,0:T(8,128)S(1)} %get-tuple-element.19.table, s32[72]{0:T(128)S(1)} %get-tuple-element.20.order, f32[1]{0:T(128)S(6)} %copy.8.lower, f32[1]{0:T(128)S(6)} %copy.9.upper, bf16[320,128,128]{2,1,0:T(8,128)(2,1)S(1)} %get-tuple-element.21.tiles, ...), custom_call_target="tpu_custom_call" | custom-call | flops 335544320 | bytes 10485760 | tf_op jit(solution)/shard_map/next_level_1/pallas_call | solution.py:332
  29.7 2.7 %local_sums_2.1.total = f32[64,4096]{1,0:T(8,128)S(1)} custom-call(s32[32,32]{1,0:T(8,128)S(1)} %get-tuple-element.19.table, bf16[320,128,128]{2,1,0:T(8,128)(2,1)S(1)} %get-tuple-element.21.tiles, bf16[64,4096]{1,0:T(8,128)(2,1)S(1)} %next_level_1.1.field), custom_call_target="tpu_custom_call" | custom-call | flops 41943040 | tf_op jit(solution)/shard_map/local_sums_2/pallas_call | solution.py:219
  32.5 1.9 %next_lists_2.1 = (bf16[64,1024]{1,0:T(8,128)(2,1)S(1)}, bf16[64,1024]{1,0:T(8,128)(2,1)S(1)}) custom-call(s32[2]{0:T(128)S(1)} %pad_add_fusion.place, s32[32,32]{1,0:T(8,128)S(1)} %get-tuple-element.19.table, s32[72]{0:T(128)S(1)} %get-tuple-element.20.order, f32[1]{0:T(128)S(6)} %copy.8.lower, f32[1]{0:T(128)S(6)} %copy.9.upper, ...), custom_call_target="tpu_custom_call" | custom-call | tf_op jit(solution)/shard_map/next_lists_2/pallas_call | solution.py:291
  34.4 2.5 %collective-permute-start.6 = (bf16[64,1024]{1,0:T(8,128)(2,1)S(1)}, bf16[64,1024]{1,0:T(8,128)(2,1)S(1)}, u32[]{:S(2)}, u32[]{:S(2)}) collective-permute-start(bf16[64,1024]{1,0:T(8,128)(2,1)S(1)} %get-tuple-element.27.new_far), channel_id=1, source_target_pairs={{2,4},{6,8},{10,12},{14,16},{18,20},{22,24},{26,28},{30,32},{34,36... | collective-permute-start | bytes 393224 | tf_op jit(solution)/shard_map/ppermute | solution.py:33
  37.0 2.5 %next_level_2.1.field.own = bf16[64,4096]{1,0:T(8,128)(2,1)S(1)} custom-call(s32[2]{0:T(128)S(1)} %pad_add_fusion.place, s32[32,32]{1,0:T(8,128)S(1)} %get-tuple-element.19.table, s32[72]{0:T(128)S(1)} %get-tuple-element.20.order, f32[1]{0:T(128)S(6)} %copy.8.lower, f32[1]{0:T(128)S(6)} %copy.9.upper, bf16[320,128,128]{2,1,0:T(8,128)(2,1)S(1)} %get-tuple-element.21.tiles, ...), custom_call_target="tpu_custom_call" | custom-call | flops 335544320 | bytes 10485760 | tf_op jit(solution)/shard_map/next_level_2/pallas_call | solution.py:332
  39.5 1.7 %collective-permute-start.4 = (bf16[64,4096]{1,0:T(8,128)(2,1)S(1)}, bf16[64,4096]{1,0:T(8,128)(2,1)S(1)}, u32[]{:S(2)}, u32[]{:S(2)}) collective-permute-start(bf16[64,4096]{1,0:T(8,128)(2,1)S(1)} %next_level_2.1.field.own), channel_id=1, source_target_pairs={{0,1},{1,0},{2,3},{3,2},{4,5},{5,4},{6,7},{7,6},{8,9},{9,8},{10,11... | collective-permute-start | bytes 1572872 | tf_op jit(solution)/shard_map/ppermute | solution.py:27
  41.2 2.7 %local_sums_3.1.total = f32[64,4096]{1,0:T(8,128)S(1)} custom-call(s32[32,32]{1,0:T(8,128)S(1)} %get-tuple-element.19.table, bf16[320,128,128]{2,1,0:T(8,128)(2,1)S(1)} %get-tuple-element.21.tiles, bf16[64,4096]{1,0:T(8,128)(2,1)S(1)} %next_level_2.1.field.own), custom_call_target="tpu_custom_call" | custom-call | flops 41943040 | tf_op jit(solution)/shard_map/local_sums_3/pallas_call | solution.py:219
  44.0 2.7 %image_rows.1.image = bf16[64,4096]{1,0:T(8,128)(2,1)S(1)} custom-call(s32[2]{0:T(128)S(1)} %pad_add_fusion.place, s32[32,32]{1,0:T(8,128)S(1)} %get-tuple-element.19.table, bf16[320,128,128]{2,1,0:T(8,128)(2,1)S(1)} %get-tuple-element.21.tiles, f32[64,4096]{1,0:T(8,128)S(1)} %local_sums_3.1.total, bf16[64,1024]{1,0:T(8,128)(2,1)S(1)} %collective-permute-done.5.near, ...), custom_call_target="tpu_custom_call" | custom-call | flops 6710886400 | bytes 10485760 | tf_op jit(solution)/shard_map/image_rows/pallas_call | solution.py:363
  46.6 7.3 %collective-permute-done.4.partner = bf16[64,4096]{1,0:T(8,128)(2,1)S(1)} collective-permute-done((bf16[64,4096]{1,0:T(8,128)(2,1)S(1)}, bf16[64,4096]{1,0:T(8,128)(2,1)S(1)}, u32[]{:S(2)}, u32[]{:S(2)}) %collective-permute-start.4) | collective-permute-done | bytes 524320 | tf_op jit(solution)/shard_map/ppermute | solution.py:27
  53.9 1.1 %partial_sums.1 = (f32[64,128]{1,0:T(8,128)S(1)}, f32[64,128]{1,0:T(8,128)S(1)}, bf16[128,4096]{1,0:T(8,128)(2,1)S(1)}) custom-call(s32[2]{0:T(128)S(1)} %pad_add_fusion.place, bf16[64,4096]{1,0:T(8,128)(2,1)S(1)} %next_level_2.1.field.own, bf16[64,4096]{1,0:T(8,128)(2,1)S(1)} %collective-permute-done.4.partner, bf16[64,4096]{1,0:T(8,128)(2,1)S(1)} %image_rows.1.image), custom_call_target="tpu_custom_call" | custom-call | tf_op jit(solution)/shard_map/partial_sums/pallas_call | solution.py:392
  55.0 1.6 %collective-permute-start.7 = (f32[64,128]{1,0:T(8,128)S(1)}, f32[64,128]{1,0:T(8,128)S(1)}, u32[]{:S(2)}, u32[]{:S(2)}) collective-permute-start(f32[64,128]{1,0:T(8,128)S(1)} %get-tuple-element.30), channel_id=1, source_target_pairs={{0,2},{2,0},{1,3},{3,1},{4,6},{6,4},{5,7},{7,5},{8,10},{10,8},{9,1... | collective-permute-start | bytes 98312 | tf_op jit(solution)/shard_map/ppermute | solution.py:27
  56.7 0.9 collective-permute-done.7
  57.5 4.4 %collective-permute-start.10 = (f32[64,128]{1,0:T(8,128)S(1)}, f32[64,128]{1,0:T(8,128)S(1)}, u32[]{:S(2)}, u32[]{:S(2)}) collective-permute-start(f32[64,128]{1,0:T(8,128)S(1)} %add.30), channel_id=1, source_target_pairs={{0,48},{16,32},{32,16},{48,0},{1,49},{17,33},{33,17},{49,1},{2,50}... | collective-permute-start | bytes 98312 | tf_op jit(solution)/shard_map/ppermute | solution.py:27
  62.0 0.7 collective-permute-start.9
  63.3 3.0 %collective-permute-done.9 = f32[64,128]{1,0:T(8,128)S(1)} collective-permute-done((f32[64,128]{1,0:T(8,128)S(1)}, f32[64,128]{1,0:T(8,128)S(1)}, u32[]{:S(2)}, u32[]{:S(2)}) %collective-permute-start.9) | collective-permute-done | bytes 32800 | tf_op jit(solution)/shard_map/ppermute | solution.py:27
  66.2 7.2 %collective-permute-start.13 = (f32[64,128]{1,0:T(8,128)S(1)}, f32[64,128]{1,0:T(8,128)S(1)}, u32[]{:S(2)}, u32[]{:S(2)}) collective-permute-start(f32[64,128]{1,0:T(8,128)S(1)} %add_add_fusion.2), channel_id=1, source_target_pairs={{0,12},{4,8},{8,4},{12,0},{1,13},{5,9},{9,5},{13,1},{2,14},{6,10},... | collective-permute-start | bytes 98312 | tf_op jit(solution)/shard_map/ppermute | solution.py:27
  73.5 0.7 collective-permute-start.11
  74.8 3.0 %collective-permute-done.12 = f32[64,128]{1,0:T(8,128)S(1)} collective-permute-done((f32[64,128]{1,0:T(8,128)S(1)}, f32[64,128]{1,0:T(8,128)S(1)}, u32[]{:S(2)}, u32[]{:S(2)}) %collective-permute-start.12) | collective-permute-done | bytes 32800 | tf_op jit(solution)/shard_map/ppermute | solution.py:27
  77.7 4.2 %collective-permute-start.16 = (f32[64,128]{1,0:T(8,128)S(1)}, f32[64,128]{1,0:T(8,128)S(1)}, u32[]{:S(2)}, u32[]{:S(2)}) collective-permute-start(f32[64,128]{1,0:T(8,128)S(1)} %add_add_fusion.1), channel_id=1, source_target_pairs={{0,192},{64,128},{128,64},{192,0},{1,193},{65,129},{129,65},{193,1... | collective-permute-start | bytes 98312 | tf_op jit(solution)/shard_map/ppermute | solution.py:27
  81.9 5.3 %collective-permute-start.15 = (f32[64,128]{1,0:T(8,128)S(1)}, f32[64,128]{1,0:T(8,128)S(1)}, u32[]{:S(2)}, u32[]{:S(2)}) collective-permute-start(f32[64,128]{1,0:T(8,128)S(1)} %add_add_fusion.1), channel_id=1, source_target_pairs={{0,128},{64,192},{128,0},{192,64},{1,129},{65,193},{129,1},{193,65... | collective-permute-start | bytes 98312 | tf_op jit(solution)/shard_map/ppermute | solution.py:27
  87.2 1.4 %collective-permute-done.15 = f32[64,128]{1,0:T(8,128)S(1)} collective-permute-done((f32[64,128]{1,0:T(8,128)S(1)}, f32[64,128]{1,0:T(8,128)S(1)}, u32[]{:S(2)}, u32[]{:S(2)}) %collective-permute-start.15) | collective-permute-done | bytes 32800 | tf_op jit(solution)/shard_map/ppermute | solution.py:27
  88.6 2.6 %collective-permute-done.14 = f32[64,128]{1,0:T(8,128)S(1)} collective-permute-done((f32[64,128]{1,0:T(8,128)S(1)}, f32[64,128]{1,0:T(8,128)S(1)}, u32[]{:S(2)}, u32[]{:S(2)}) %collective-permute-start.14) | collective-permute-done | bytes 32800 | tf_op jit(solution)/shard_map/ppermute | solution.py:27
  91.2 6.1 %collective-permute-start.19 = (f32[64,128]{1,0:T(8,128)S(1)}, f32[64,128]{1,0:T(8,128)S(1)}, u32[]{:S(2)}, u32[]{:S(2)}) collective-permute-start(f32[64,128]{1,0:T(8,128)S(1)} %add_add_fusion.own), channel_id=1, source_target_pairs={{0,3},{1,2},{2,1},{3,0},{4,7},{5,6},{6,5},{7,4},{8,11},{9,10},{10,... | collective-permute-start | bytes 98312 | tf_op jit(solution)/shard_map/ppermute | solution.py:27
  97.7 1.2 %collective-permute-done.19.last = f32[64,128]{1,0:T(8,128)S(1)} collective-permute-done((f32[64,128]{1,0:T(8,128)S(1)}, f32[64,128]{1,0:T(8,128)S(1)}, u32[]{:S(2)}, u32[]{:S(2)}) %collective-permute-start.19) | collective-permute-done | bytes 32800 | tf_op jit(solution)/shard_map/ppermute | solution.py:27
  98.9 1.1 %collective-permute-done.18.other_mode = f32[64,128]{1,0:T(8,128)S(1)} collective-permute-done((f32[64,128]{1,0:T(8,128)S(1)}, f32[64,128]{1,0:T(8,128)S(1)}, u32[]{:S(2)}, u32[]{:S(2)}) %collective-permute-start.18) | collective-permute-done | bytes 32800 | tf_op jit(solution)/shard_map/ppermute | solution.py:27
  100.0 8.3 %factor_and_project.1 = (bf16[64,4096]{1,0:T(8,128)(2,1)}, f32[128,128]{1,0:T(8,128)}) custom-call(s32[2]{0:T(128)S(1)} %pad_add_fusion.place, f32[64,128]{1,0:T(8,128)S(1)} %add_add_fusion.own, f32[64,128]{1,0:T(8,128)S(1)} %collective-permute-done.17.other_core, f32[64,128]{1,0:T(8,128)S(1)} %collective-permute-done.18.other_mode, ...), custom_call_target="tpu_custom_call" | custom-call | tf_op jit(solution)/shard_map/factor_and_project/pallas_call | solution.py:480
  (24 shorter events, 2.1 us)
Async XLA Ops:
  2.4 19.0 %collective-permute-start = (bf16[64,1024]{1,0:T(8,128)(2,1)S(1)}, bf16[64,1024]{1,0:T(8,128)(2,1)S(1)}, u32[]{:S(2)}, u32[]{:S(2)}) collective-permute-start(bf16[64,1024]{1,0:T(8,128)(2,1)S(1)} %get-tuple-element.23), channel_id=1, source_target_pairs={{0,2},{2,0},{1,3},{3,1},{4,6},{6,4},{5,7},{7,5},{8,10},{10,8},{9,1... | collective-permute-start | bytes 393224 | tf_op jit(solution)/shard_map/ppermute | solution.py:27
  5.7 15.7 %collective-permute-start.1 = (bf16[64,1024]{1,0:T(8,128)(2,1)S(1)}, bf16[64,1024]{1,0:T(8,128)(2,1)S(1)}, u32[]{:S(2)}, u32[]{:S(2)}) collective-permute-start(bf16[64,1024]{1,0:T(8,128)(2,1)S(1)} %get-tuple-element.24), channel_id=1, source_target_pairs={{2,4},{6,8},{10,12},{14,16},{18,20},{22,24},{26,28},{30,32},{34,36... | collective-permute-start | bytes 393224 | tf_op jit(solution)/shard_map/ppermute | solution.py:33
  23.3 9.2 %collective-permute-start.3 = (bf16[64,1024]{1,0:T(8,128)(2,1)S(1)}, bf16[64,1024]{1,0:T(8,128)(2,1)S(1)}, u32[]{:S(2)}, u32[]{:S(2)}) collective-permute-start(bf16[64,1024]{1,0:T(8,128)(2,1)S(1)} %get-tuple-element.25.new_far), channel_id=1, source_target_pairs={{2,4},{6,8},{10,12},{14,16},{18,20},{22,24},{26,28},{30,32},{34,36... | collective-permute-start | bytes 393224 | tf_op jit(solution)/shard_map/ppermute | solution.py:33
  27.2 5.2 %collective-permute-start.2 = (bf16[64,1024]{1,0:T(8,128)(2,1)S(1)}, bf16[64,1024]{1,0:T(8,128)(2,1)S(1)}, u32[]{:S(2)}, u32[]{:S(2)}) collective-permute-start(bf16[64,1024]{1,0:T(8,128)(2,1)S(1)} %get-tuple-element.26.new_near), channel_id=1, source_target_pairs={{0,2},{2,0},{1,3},{3,1},{4,6},{6,4},{5,7},{7,5},{8,10},{10,8},{9,1... | collective-permute-start | bytes 393224 | tf_op jit(solution)/shard_map/ppermute | solution.py:27
  34.4 9.6 %collective-permute-start.6 = (bf16[64,1024]{1,0:T(8,128)(2,1)S(1)}, bf16[64,1024]{1,0:T(8,128)(2,1)S(1)}, u32[]{:S(2)}, u32[]{:S(2)}) collective-permute-start(bf16[64,1024]{1,0:T(8,128)(2,1)S(1)} %get-tuple-element.27.new_far), channel_id=1, source_target_pairs={{2,4},{6,8},{10,12},{14,16},{18,20},{22,24},{26,28},{30,32},{34,36... | collective-permute-start | bytes 393224 | tf_op jit(solution)/shard_map/ppermute | solution.py:33
  36.9 7.0 %collective-permute-start.5 = (bf16[64,1024]{1,0:T(8,128)(2,1)S(1)}, bf16[64,1024]{1,0:T(8,128)(2,1)S(1)}, u32[]{:S(2)}, u32[]{:S(2)}) collective-permute-start(bf16[64,1024]{1,0:T(8,128)(2,1)S(1)} %get-tuple-element.28.new_near), channel_id=1, source_target_pairs={{0,2},{2,0},{1,3},{3,1},{4,6},{6,4},{5,7},{7,5},{8,10},{10,8},{9,1... | collective-permute-start | bytes 393224 | tf_op jit(solution)/shard_map/ppermute | solution.py:27
  39.5 14.4 %collective-permute-start.4 = (bf16[64,4096]{1,0:T(8,128)(2,1)S(1)}, bf16[64,4096]{1,0:T(8,128)(2,1)S(1)}, u32[]{:S(2)}, u32[]{:S(2)}) collective-permute-start(bf16[64,4096]{1,0:T(8,128)(2,1)S(1)} %next_level_2.1.field.own), channel_id=1, source_target_pairs={{0,1},{1,0},{2,3},{3,2},{4,5},{5,4},{6,7},{7,6},{8,9},{9,8},{10,11... | collective-permute-start | bytes 1572872 | tf_op jit(solution)/shard_map/ppermute | solution.py:27
  55.0 2.5 %collective-permute-start.7 = (f32[64,128]{1,0:T(8,128)S(1)}, f32[64,128]{1,0:T(8,128)S(1)}, u32[]{:S(2)}, u32[]{:S(2)}) collective-permute-start(f32[64,128]{1,0:T(8,128)S(1)} %get-tuple-element.30), channel_id=1, source_target_pairs={{0,2},{2,0},{1,3},{3,1},{4,6},{6,4},{5,7},{7,5},{8,10},{10,8},{9,1... | collective-permute-start | bytes 98312 | tf_op jit(solution)/shard_map/ppermute | solution.py:27
  57.5 5.7 %collective-permute-start.10 = (f32[64,128]{1,0:T(8,128)S(1)}, f32[64,128]{1,0:T(8,128)S(1)}, u32[]{:S(2)}, u32[]{:S(2)}) collective-permute-start(f32[64,128]{1,0:T(8,128)S(1)} %add.30), channel_id=1, source_target_pairs={{0,48},{16,32},{32,16},{48,0},{1,49},{17,33},{33,17},{49,1},{2,50}... | collective-permute-start | bytes 98312 | tf_op jit(solution)/shard_map/ppermute | solution.py:27
  62.0 4.3 %collective-permute-start.9 = (f32[64,128]{1,0:T(8,128)S(1)}, f32[64,128]{1,0:T(8,128)S(1)}, u32[]{:S(2)}, u32[]{:S(2)}) collective-permute-start(f32[64,128]{1,0:T(8,128)S(1)} %add.30), channel_id=1, source_target_pairs={{0,32},{16,48},{32,0},{48,16},{1,33},{17,49},{33,1},{49,17},{2,34}... | collective-permute-start | bytes 98312 | tf_op jit(solution)/shard_map/ppermute | solution.py:27
  62.6 3.6 %collective-permute-start.8 = (f32[64,128]{1,0:T(8,128)S(1)}, f32[64,128]{1,0:T(8,128)S(1)}, u32[]{:S(2)}, u32[]{:S(2)}) collective-permute-start(f32[64,128]{1,0:T(8,128)S(1)} %add.30), channel_id=1, source_target_pairs={{0,16},{16,0},{32,48},{48,32},{1,17},{17,1},{33,49},{49,33},{2,18}... | collective-permute-start | bytes 98312 | tf_op jit(solution)/shard_map/ppermute | solution.py:27
  66.2 8.5 %collective-permute-start.13 = (f32[64,128]{1,0:T(8,128)S(1)}, f32[64,128]{1,0:T(8,128)S(1)}, u32[]{:S(2)}, u32[]{:S(2)}) collective-permute-start(f32[64,128]{1,0:T(8,128)S(1)} %add_add_fusion.2), channel_id=1, source_target_pairs={{0,12},{4,8},{8,4},{12,0},{1,13},{5,9},{9,5},{13,1},{2,14},{6,10},... | collective-permute-start | bytes 98312 | tf_op jit(solution)/shard_map/ppermute | solution.py:27
  73.5 4.3 %collective-permute-start.12 = (f32[64,128]{1,0:T(8,128)S(1)}, f32[64,128]{1,0:T(8,128)S(1)}, u32[]{:S(2)}, u32[]{:S(2)}) collective-permute-start(f32[64,128]{1,0:T(8,128)S(1)} %add_add_fusion.2), channel_id=1, source_target_pairs={{0,8},{4,12},{8,0},{12,4},{1,9},{5,13},{9,1},{13,5},{2,10},{6,14},... | collective-permute-start | bytes 98312 | tf_op jit(solution)/shard_map/ppermute | solution.py:27
  73.5 4.3 %collective-permute-start.11 = (f32[64,128]{1,0:T(8,128)S(1)}, f32[64,128]{1,0:T(8,128)S(1)}, u32[]{:S(2)}, u32[]{:S(2)}) collective-permute-start(f32[64,128]{1,0:T(8,128)S(1)} %add_add_fusion.2), channel_id=1, source_target_pairs={{0,4},{4,0},{8,12},{12,8},{1,5},{5,1},{9,13},{13,9},{2,6},{6,2},{1... | collective-permute-start | bytes 98312 | tf_op jit(solution)/shard_map/ppermute | solution.py:27
  77.7 9.5 %collective-permute-start.16 = (f32[64,128]{1,0:T(8,128)S(1)}, f32[64,128]{1,0:T(8,128)S(1)}, u32[]{:S(2)}, u32[]{:S(2)}) collective-permute-start(f32[64,128]{1,0:T(8,128)S(1)} %add_add_fusion.1), channel_id=1, source_target_pairs={{0,192},{64,128},{128,64},{192,0},{1,193},{65,129},{129,65},{193,1... | collective-permute-start | bytes 98312 | tf_op jit(solution)/shard_map/ppermute | solution.py:27
  81.9 6.7 %collective-permute-start.15 = (f32[64,128]{1,0:T(8,128)S(1)}, f32[64,128]{1,0:T(8,128)S(1)}, u32[]{:S(2)}, u32[]{:S(2)}) collective-permute-start(f32[64,128]{1,0:T(8,128)S(1)} %add_add_fusion.1), channel_id=1, source_target_pairs={{0,128},{64,192},{128,0},{192,64},{1,129},{65,193},{129,1},{193,65... | collective-permute-start | bytes 98312 | tf_op jit(solution)/shard_map/ppermute | solution.py:27
  87.2 4.0 %collective-permute-start.14 = (f32[64,128]{1,0:T(8,128)S(1)}, f32[64,128]{1,0:T(8,128)S(1)}, u32[]{:S(2)}, u32[]{:S(2)}) collective-permute-start(f32[64,128]{1,0:T(8,128)S(1)} %add_add_fusion.1), channel_id=1, source_target_pairs={{0,64},{64,0},{128,192},{192,128},{1,65},{65,1},{129,193},{193,129... | collective-permute-start | bytes 98312 | tf_op jit(solution)/shard_map/ppermute | solution.py:27
  91.2 7.7 %collective-permute-start.19 = (f32[64,128]{1,0:T(8,128)S(1)}, f32[64,128]{1,0:T(8,128)S(1)}, u32[]{:S(2)}, u32[]{:S(2)}) collective-permute-start(f32[64,128]{1,0:T(8,128)S(1)} %add_add_fusion.own), channel_id=1, source_target_pairs={{0,3},{1,2},{2,1},{3,0},{4,7},{5,6},{6,5},{7,4},{8,11},{9,10},{10,... | collective-permute-start | bytes 98312 | tf_op jit(solution)/shard_map/ppermute | solution.py:27
  97.2 2.8 %collective-permute-start.18 = (f32[64,128]{1,0:T(8,128)S(1)}, f32[64,128]{1,0:T(8,128)S(1)}, u32[]{:S(2)}, u32[]{:S(2)}) collective-permute-start(f32[64,128]{1,0:T(8,128)S(1)} %add_add_fusion.own), channel_id=1, source_target_pairs={{0,1},{1,0},{2,3},{3,2},{4,5},{5,4},{6,7},{7,6},{8,9},{9,8},{10,11... | collective-permute-start | bytes 98312 | tf_op jit(solution)/shard_map/ppermute | solution.py:27
  97.3 2.7 %collective-permute-start.17 = (f32[64,128]{1,0:T(8,128)S(1)}, f32[64,128]{1,0:T(8,128)S(1)}, u32[]{:S(2)}, u32[]{:S(2)}) collective-permute-start(f32[64,128]{1,0:T(8,128)S(1)} %add_add_fusion.own), channel_id=1, source_target_pairs={{0,2},{2,0},{1,3},{3,1},{4,6},{6,4},{5,7},{7,5},{8,10},{10,8},{9,1... | collective-permute-start | bytes 98312 | tf_op jit(solution)/shard_map/ppermute | solution.py:27

commit v5 on v4

--- a/solution.py
+++ b/solution.py
@@ -13,6 +13,7 @@
 HBM = pl.BlockSpec(memory_space=pltpu.HBM)
 NT = (((1,), (1,)), ((), ()))
 GROUP = 8
+IN_FLIGHT = 4
 
 
 def params(mib):
@@ -106,10 +107,8 @@
     order[2 * rows] = (at + GROUP - 1) // GROUP
 
 
-def local_rows(table, tiles, sources, total, step, nnz):
-    for u in range(GROUP):
-        row = step * GROUP + u
-        total[:, columns(row, tiles.shape[1])] = summed(table, tiles, sources, row, 0, range(nnz - 2), nnz)
+def local_row(table, tiles, sources, total, row, nnz):
+    total[:, columns(row, tiles.shape[1])] = summed(table, tiles, sources, row, 0, range(nnz - 2), nnz)
 
 
 def summed(table, tiles, sources, row, kind, positions, nnz):
@@ -148,31 +147,43 @@
         ]
         for copy in lists:
             copy.start()
-        for i in range(chunks):
+        for i in range(IN_FLIGHT):
             chunk(i).start()
         fill_sources(field, sources)
+        def arrive(step):
+            for i in (2 * step, 2 * step + 1):
+                chunk(i).wait()
+
+                @pl.when(i + IN_FLIGHT < chunks)
+                def _():
+                    chunk(i + IN_FLIGHT).start()
+
+        def turn(step, u):
+            for k in range(nnz):
+                at = (step * GROUP + u) * nnz + k
+                staged[at] = raw[at].T
+
+        steps = rows // GROUP
         for copy in lists:
             copy.wait()
+        arrive(0)
+        for u in range(GROUP):
+            turn(0, u)
         make_plan(place[1], [cols[k : k + 1, :] for k in range(nnz)], send, made, order, taken)
         copy = pltpu.make_async_copy(made, table, small.at[2])
         copy.start()
         copy.wait()
 
         def step(i, carry):
-            chunk(2 * i).wait()
-            chunk(2 * i + 1).wait()
-
-            def turn(j, carry):
-                for u in range(GROUP):
-                    at = i * 2 * per_chunk + j * GROUP + u
-                    staged[at] = raw[at].T
-                return carry
-
-            lax.fori_loop(0, 2 * per_chunk // GROUP, turn, 0)
-            local_rows(table, staged, sources, total, i, nnz)
+            arrive(i + 1)
+            for u in range(GROUP):
+                turn(i + 1, u)
+                local_row(table, staged, sources, total, i * GROUP + u, nnz)
             return carry
 
-        lax.fori_loop(0, rows // GROUP, step, 0)
+        lax.fori_loop(0, steps - 1, step, 0)
+        for u in range(GROUP):
+            local_row(table, staged, sources, total, (steps - 1) * GROUP + u, nnz)
 
     def in_hbm(array):
         return pltpu.with_memory_space_constraint(array, pltpu.HBM)
@@ -211,7 +222,8 @@
         fill_sources(field, sources)
 
         def step(i, carry):
-            local_rows(table, tiles, sources, total, i, nnz)
+            for u in range(GROUP):
+                local_row(table, tiles, sources, total, i * GROUP + u, nnz)
             return carry
 
         lax.fori_loop(0, rows // GROUP, step, 0)
@@ -344,60 +356,82 @@
     )(*operands)
 
 
-def image_rows(nnz, place, table, tiles, total, near, far):
-    modes, width = total.shape
-    tile = tiles.shape[1]
-
-    def kernel(place, table, tiles, total, near, far, out, ghosts, partial):
-        fill_ghosts(place[1], near, far, ghosts)
+def last_level(nnz, place, table, send_rows, bounds, tiles, total, near, far, field, previous):
+    modes, width = field.shape
+    tile = tiles.shape[1]
+
+    def kernel(place, table, send, lower, upper, tiles, total, near, far, field, previous, *rest):
+        out, new_far, new_near, ghosts, partial = rest
+        core = place[1]
+        fill_ghosts(core, near, far, ghosts)
+
+        def store(u, row, value):
+            out[:, columns(row, tile)] = value
+
+        def step(i, carry):
+            rows = ghost_rows(table, None, tiles, ghosts, partial, i * GROUP, nnz)
+            level_rows(2, (lower, upper), rows, total, partial, field, previous, store)
+            return carry
+
+        lax.fori_loop(0, width // tile // GROUP, step, 0)
+        for slot in range(far.shape[1] // tile):
+            here = slice(slot * tile, (slot + 1) * tile)
+            new_far[:, here] = out[:, columns(send[core, slot], tile)]
+            new_near[:, here] = out[:, columns(send[1 - core, slot], tile)]
+
+    part = shape(far.shape, far.dtype)
+    return pl.pallas_call(
+        kernel,
+        out_shape=(shape(field.shape, field.dtype), part, part),
+        in_specs=[SMEM] * 5 + [VMEM] * 6,
+        out_specs=(VMEM,) * 3,
+        scratch_shapes=[
+            pltpu.VMEM((modes, 2 * far.shape[1] + tile), far.dtype),
+            pltpu.VMEM((modes, GROUP * tile), jnp.float32),
+        ],
+        compiler_params=params(8),
+        name="last_level",
+    )(place, table, send_rows, *bounds, tiles, total, near, far, field, previous)
+
+
+def partial_sums(nnz, place, table, tiles, total, near, far, own, partner):
+    modes, width = own.shape
+    tile = tiles.shape[1]
+    product = shape((modes, 2 * modes), jnp.float32)
+
+    def kernel(place, table, tiles, total, near, far, own, partner, keep, send, both, ghosts, partial, left):
+        mode, core = place[0], place[1]
+        fill_ghosts(core, near, far, ghosts)
+        both[columns(mode, modes), :] = own[...]
+        both[columns(1 - mode, modes), :] = partner[...]
+        left[columns(core, modes), :] = own[...]
 
         def step(i, carry):
             rows = ghost_rows(table, None, tiles, ghosts, partial, i * GROUP, nnz)
             for u, row in enumerate(rows):
                 here = columns(row, tile)
-                out[:, here] = (total[:, here] + partial[:, u * tile : (u + 1) * tile]).astype(out.dtype)
+                value = total[:, here] + partial[:, u * tile : (u + 1) * tile]
+                left[columns(1 - core, modes), here] = value.astype(own.dtype)
             return carry
 
         lax.fori_loop(0, width // tile // GROUP, step, 0)
-
-    return pl.pallas_call(
-        kernel,
-        out_shape=shape((modes, width), near.dtype),
-        in_specs=[SMEM] * 2 + [VMEM] * 4,
-        out_specs=VMEM,
+        sums = lax.dot_general(left[...], both[...], NT, preferred_element_type=jnp.float32)
+        keep[...] = sums[:modes]
+        send[...] = sums[modes:]
+
+    return pl.pallas_call(
+        kernel,
+        out_shape=(product, product, shape((2 * modes, width), own.dtype)),
+        in_specs=[SMEM] * 2 + [VMEM] * 6,
+        out_specs=(VMEM,) * 3,
         scratch_shapes=[
             pltpu.VMEM((modes, 2 * near.shape[1] + tile), near.dtype),
             pltpu.VMEM((modes, GROUP * tile), jnp.float32),
+            pltpu.VMEM((2 * modes, width), own.dtype),
         ],
-        compiler_params=params(8),
-        cost_estimate=pl.CostEstimate(flops=20 * tiles.size * modes, bytes_accessed=2 * tiles.size, transcendentals=0),
-        name="image_rows",
-    )(place, table, tiles, total, near, far)
-
-
-def partial_sums(place, own, partner, image):
-    modes, width = own.shape
-    product = shape((modes, 2 * modes), jnp.float32)
-
-    def kernel(place, own, partner, image, keep, send, both, left):
-        mode, core = place[0], place[1]
-        both[columns(mode, modes), :] = own[...]
-        both[columns(1 - mode, modes), :] = partner[...]
-        left[columns(core, modes), :] = own[...]
-        left[columns(1 - core, modes), :] = image[...]
-        sums = lax.dot_general(left[...], both[...], NT, preferred_element_type=jnp.float32)
-        keep[...] = sums[:modes]
-        send[...] = sums[modes:]
-
-    return pl.pallas_call(
-        kernel,
-        out_shape=(product, product, shape((2 * modes, width), own.dtype)),
-        in_specs=[SMEM] + [VMEM] * 3,
-        out_specs=(VMEM,) * 3,
-        scratch_shapes=[pltpu.VMEM((2 * modes, width), own.dtype)],
         compiler_params=params(12),
         name="partial_sums",
-    )(place, own, partner, image)
+    )(place, table, tiles, total, near, far, own, partner)
 
 
 def sum_over_chips(value):
@@ -500,18 +534,22 @@
         place, send_rows, tile_cols.T, stiffness_tiles.reshape(rows * nnz, tile, tile), level_0
     )
 
-    def level(index, total, near, far, field, previous=None):
-        known = (nnz, place, table, order, bounds, tiles, total, near, far, field, previous)
-        new_far, new_near = next_lists(index, *known)
-        arrived = flipped(new_near, C, 1), swapped_between_chips(new_far)
-        field = next_level(index, *known, new_far, new_near)
-        return field, *arrived, local_sums(index + 1, table, tiles, field, rows, nnz)
-
-    level_1, near, far, total = level(1, total, near, far, level_0)
-    filtered, near, far, total = level(2, total, near, far, level_1, level_0)
+    def exchange(near, far):
+        return flipped(near, C, 1), swapped_between_chips(far)
+
+    known = (nnz, place, table, order, bounds, tiles, total, near, far, level_0, None)
+    far, near = next_lists(1, *known)
+    level_1 = next_level(1, *known, far, near)
+    near, far = exchange(near, far)
+    total = local_sums(2, table, tiles, level_1, rows, nnz)
+
+    filtered, far, near = last_level(
+        nnz, place, table, send_rows, bounds, tiles, total, near, far, level_1, level_0
+    )
     partner = flipped(filtered, M, 1)
-    image = image_rows(nnz, place, table, tiles, total, near, far)
-    keep, send, both = partial_sums(place, filtered, partner, image)
+    near, far = exchange(near, far)
+    total = local_sums(3, table, tiles, filtered, rows, nnz)
+    keep, send, both = partial_sums(nnz, place, table, tiles, total, near, far, filtered, partner)
     quarter = sum_over_chips(keep + flipped(send, C, 1))
     quarters = (quarter, flipped(quarter, C, 1), flipped(quarter, M, 1), flipped(quarter, (C, M), 3))
     basis, ritz = factor_and_project(place, quarters, both, dof_total)

time: 109 us -> 102 us (0.936)
  Pallas kernels: 40.3 us -> 35.7 us
  waiting for transfers between devices: 21.6 us -> 18.2 us
    pallas_call x1, Pallas kernels: 12.5 us -> 8.85 us  [stage_and_sum(): pl.pallas_call(kernel, out_shape=(shape(tiles.shape, tiles.dtype), shape(...]
    ppermute x17, waiting for transfers between devices: 21.6 us -> 18.1 us  [flipped(): lax.ppermute(block, axis, [(i, i ^ bits) for i in range(lax.axis_size(axi...]
    pallas_call x2 -> x1, Pallas kernels: 4.87 us -> 2.37 us  [next_level(): pl.pallas_call(kernel, out_shape=shape(field.shape, field.dtype), in_spec...]
    pallas_call x1, Pallas kernels: 1.09 us -> 3.52 us  [partial_sums(): pl.pallas_call(kernel, out_shape=(product, product, shape((2 * modes, wid...]
    pallas_call x2 -> x1, Pallas kernels: 3.71 us -> 2.13 us  [next_lists(): pl.pallas_call(kernel, out_shape=(shape(far.shape, far.dtype),) * 2, in_s...]
  transfers between devices with their start and end apart: 20 -> 20, of which waited for: 10 -> 10; matrix products, arithmetic and copies ran while one was open for 0% -> 0% of each run, Pallas kernels for 24% -> 17%
where the time goes in v5:
time: 102 us; the launch traced here: 101 us
  starting transfers between devices  45 us (44%)
  Pallas kernels  35.7 us (35%)
  waiting for transfers between devices  18.2 us (18%)
  between operations  2.11 us (2%)
    ppermute x17, starting transfers between devices, flipped(): lax.ppermute(block, axis, [(i, i ^ bits) for i in range(lax.axis_size(axi...  36 us
    ppermute x17, waiting for transfers between devices, flipped(): lax.ppermute(block, axis, [(i, i ^ bits) for i in range(lax.axis_size(axi...  18.1 us
    ppermute x3, starting transfers between devices, swapped_between_chips(): return lax.ppermute(block, DOF, pairs + [(b, a) for a, b in pairs])  9.04 us
    pallas_call x1, Pallas kernels, stage_and_sum(): pl.pallas_call(kernel, out_shape=(shape(tiles.shape, tiles.dtype), shape(...  8.85 us
    pallas_call x1, Pallas kernels, factor_and_project(): pl.pallas_call(kernel, out_shape=(shape((modes, width), both.dtype), shap...  8.3 us
    pallas_call x2, Pallas kernels, local_sums(): pl.pallas_call(kernel, out_shape=shape((modes, width), jnp.float32), in_s...  5.5 us
    pallas_call x1, Pallas kernels, partial_sums(): pl.pallas_call(kernel, out_shape=(product, product, shape((2 * modes, wid...  3.52 us
    pallas_call x1, Pallas kernels, last_level(): pl.pallas_call(kernel, out_shape=(shape(field.shape, field.dtype), part,...  3.36 us
  transfers between devices with their start and end apart: 20, of which 10 were waited for; matrix products, arithmetic and copies ran while one was open for 0% of the time, Pallas kernels for 17%

profile of v5, /device:TPU:1, one launch (start us, length us, event | category | flops | bytes accessed | tf_op | source)
XLA Modules:
  0.0 101.2 jit_solution(2471451126851530383)
XLA Ops:
  0.7 1.7 %pick_lists.1 = (bf16[64,4096]{1,0:T(8,128)(2,1)S(1)}, bf16[64,1024]{1,0:T(8,128)(2,1)S(1)}, bf16[64,1024]{1,0:T(8,128)(2,1)S(1)}) custom-call(s32[2]{0:T(128)S(1)} %pad_add_fusion.place, s32[2,8]{1,0:T(2,128)} %send.3, bf16[64,4096]{1,0:T(8,128)(2,1)} %bitcast.7), custom_call_target="tpu_custom_call" | custom-call | tf_op jit(solution)/shard_map/pick_lists/pallas_call | solution.py:61
  2.4 3.3 %collective-permute-start = (bf16[64,1024]{1,0:T(8,128)(2,1)S(1)}, bf16[64,1024]{1,0:T(8,128)(2,1)S(1)}, u32[]{:S(2)}, u32[]{:S(2)}) collective-permute-start(bf16[64,1024]{1,0:T(8,128)(2,1)S(1)} %get-tuple-element.24), channel_id=1, source_target_pairs={{0,2},{2,0},{1,3},{3,1},{4,6},{6,4},{5,7},{7,5},{8,10},{10,8},{9,1... | collective-permute-start | bytes 393224 | tf_op jit(solution)/shard_map/ppermute | solution.py:28
  5.7 1.9 %collective-permute-start.1 = (bf16[64,1024]{1,0:T(8,128)(2,1)S(1)}, bf16[64,1024]{1,0:T(8,128)(2,1)S(1)}, u32[]{:S(2)}, u32[]{:S(2)}) collective-permute-start(bf16[64,1024]{1,0:T(8,128)(2,1)S(1)} %get-tuple-element.25), channel_id=1, source_target_pairs={{2,4},{6,8},{10,12},{14,16},{18,20},{22,24},{26,28},{30,32},{34,36... | collective-permute-start | bytes 393224 | tf_op jit(solution)/shard_map/ppermute | solution.py:34
  8.9 8.9 %stage_and_sum.1 = (bf16[320,128,128]{2,1,0:T(8,128)(2,1)S(1)}, f32[64,4096]{1,0:T(8,128)S(1)}, s32[32,32]{1,0:T(8,128)S(1)}, s32[72]{0:T(128)S(1)}) custom-call(s32[2]{0:T(128)S(1)} %pad_add_fusion.place, s32[2,8]{1,0:T(2,128)} %send.3, s32[10,32]{1,0:T(8,128)} %bitcast.8, bf16[320,128,128]{2,1,0:T(8,128)(2,1)} %bitcast.6, ...), custom_call_target="tpu_custom_call" | custom-call | flops 671088640 | bytes 10485760 | tf_op jit(solution)/shard_map/stage_and_sum/pallas_call | solution.py:191
  17.8 2.1 %next_lists_1.1 = (bf16[64,1024]{1,0:T(8,128)(2,1)S(1)}, bf16[64,1024]{1,0:T(8,128)(2,1)S(1)}) custom-call(s32[2]{0:T(128)S(1)} %pad_add_fusion.place, s32[32,32]{1,0:T(8,128)S(1)} %get-tuple-element.20.table, s32[72]{0:T(128)S(1)} %get-tuple-element.22.order, f32[1]{0:T(128)S(6)} %copy.8.lower, f32[1]{0:T(128)S(6)} %copy.9.upper, ...), custom_call_target="tpu_custom_call" | custom-call | tf_op jit(solution)/shard_map/next_lists_1/pallas_call | solution.py:303
  19.9 3.3 %collective-permute-start.3 = (bf16[64,1024]{1,0:T(8,128)(2,1)S(1)}, bf16[64,1024]{1,0:T(8,128)(2,1)S(1)}, u32[]{:S(2)}, u32[]{:S(2)}) collective-permute-start(bf16[64,1024]{1,0:T(8,128)(2,1)S(1)} %get-tuple-element.26.new_far), channel_id=1, source_target_pairs={{2,4},{6,8},{10,12},{14,16},{18,20},{22,24},{26,28},{30,32},{34,36... | collective-permute-start | bytes 393224 | tf_op jit(solution)/shard_map/ppermute | solution.py:34
  23.4 2.4 %next_level_1.1.field = bf16[64,4096]{1,0:T(8,128)(2,1)S(1)} custom-call(s32[2]{0:T(128)S(1)} %pad_add_fusion.place, s32[32,32]{1,0:T(8,128)S(1)} %get-tuple-element.20.table, s32[72]{0:T(128)S(1)} %get-tuple-element.22.order, f32[1]{0:T(128)S(6)} %copy.8.lower, f32[1]{0:T(128)S(6)} %copy.9.upper, bf16[320,128,128]{2,1,0:T(8,128)(2,1)S(1)} %get-tuple-element.21.tiles, ...), custom_call_target="tpu_custom_call" | custom-call | flops 335544320 | bytes 10485760 | tf_op jit(solution)/shard_map/next_level_1/pallas_call | solution.py:344
  25.8 2.8 %local_sums_2.1.total = f32[64,4096]{1,0:T(8,128)S(1)} custom-call(s32[32,32]{1,0:T(8,128)S(1)} %get-tuple-element.20.table, bf16[320,128,128]{2,1,0:T(8,128)(2,1)S(1)} %get-tuple-element.21.tiles, bf16[64,4096]{1,0:T(8,128)(2,1)S(1)} %next_level_1.1.field), custom_call_target="tpu_custom_call" | custom-call | flops 41943040 | tf_op jit(solution)/shard_map/local_sums_2/pallas_call | solution.py:231
  28.6 3.4 %last_level.1 = (bf16[64,4096]{1,0:T(8,128)(2,1)S(1)}, bf16[64,1024]{1,0:T(8,128)(2,1)S(1)}, bf16[64,1024]{1,0:T(8,128)(2,1)S(1)}) custom-call(s32[2]{0:T(128)S(1)} %pad_add_fusion.place, s32[32,32]{1,0:T(8,128)S(1)} %get-tuple-element.20.table, s32[2,8]{1,0:T(2,128)S(1)} %copy-done, f32[1]{0:T(128)S(6)} %copy.8.lower, f32[1]{0:T(128)S(6)} %copy.9.upper, ...), custom_call_target="tpu_custom_call" | custom-call | tf_op jit(solution)/shard_map/last_level/pallas_call | solution.py:383
  32.0 1.3 %collective-permute-start.4 = (bf16[64,1024]{1,0:T(8,128)(2,1)S(1)}, bf16[64,1024]{1,0:T(8,128)(2,1)S(1)}, u32[]{:S(2)}, u32[]{:S(2)}) collective-permute-start(bf16[64,1024]{1,0:T(8,128)(2,1)S(1)} %get-tuple-element.29), channel_id=1, source_target_pairs={{0,2},{2,0},{1,3},{3,1},{4,6},{6,4},{5,7},{7,5},{8,10},{10,8},{9,1... | collective-permute-start | bytes 393224 | tf_op jit(solution)/shard_map/ppermute | solution.py:28
  33.3 3.8 %collective-permute-start.5 = (bf16[64,1024]{1,0:T(8,128)(2,1)S(1)}, bf16[64,1024]{1,0:T(8,128)(2,1)S(1)}, u32[]{:S(2)}, u32[]{:S(2)}) collective-permute-start(bf16[64,1024]{1,0:T(8,128)(2,1)S(1)} %get-tuple-element.30), channel_id=1, source_target_pairs={{2,4},{6,8},{10,12},{14,16},{18,20},{22,24},{26,28},{30,32},{34,36... | collective-permute-start | bytes 393224 | tf_op jit(solution)/shard_map/ppermute | solution.py:34
  37.1 2.8 %local_sums_3.1.total = f32[64,4096]{1,0:T(8,128)S(1)} custom-call(s32[32,32]{1,0:T(8,128)S(1)} %get-tuple-element.20.table, bf16[320,128,128]{2,1,0:T(8,128)(2,1)S(1)} %get-tuple-element.21.tiles, bf16[64,4096]{1,0:T(8,128)(2,1)S(1)} %get-tuple-element.28.field.own), custom_call_target="tpu_custom_call" | custom-call | flops 41943040 | tf_op jit(solution)/shard_map/local_sums_3/pallas_call | solution.py:231
  40.0 4.3 %collective-permute-done.6.partner = bf16[64,4096]{1,0:T(8,128)(2,1)S(1)} collective-permute-done((bf16[64,4096]{1,0:T(8,128)(2,1)S(1)}, bf16[64,4096]{1,0:T(8,128)(2,1)S(1)}, u32[]{:S(2)}, u32[]{:S(2)}) %collective-permute-start.6) | collective-permute-done | bytes 524320 | tf_op jit(solution)/shard_map/ppermute | solution.py:28
  44.3 3.5 %partial_sums.1 = (f32[64,128]{1,0:T(8,128)S(1)}, f32[64,128]{1,0:T(8,128)S(1)}, bf16[128,4096]{1,0:T(8,128)(2,1)S(1)}) custom-call(s32[2]{0:T(128)S(1)} %pad_add_fusion.place, s32[32,32]{1,0:T(8,128)S(1)} %get-tuple-element.20.table, bf16[320,128,128]{2,1,0:T(8,128)(2,1)S(1)} %get-tuple-element.21.tiles, f32[64,4096]{1,0:T(8,128)S(1)} %local_sums_3.1.total, ...), custom_call_target="tpu_custom_call" | custom-call | tf_op jit(solution)/shard_map/partial_sums/pallas_call | solution.py:422
  47.9 2.4 %collective-permute-start.7 = (f32[64,128]{1,0:T(8,128)S(1)}, f32[64,128]{1,0:T(8,128)S(1)}, u32[]{:S(2)}, u32[]{:S(2)}) collective-permute-start(f32[64,128]{1,0:T(8,128)S(1)} %get-tuple-element.32), channel_id=1, source_target_pairs={{0,2},{2,0},{1,3},{3,1},{4,6},{6,4},{5,7},{7,5},{8,10},{10,8},{9,1... | collective-permute-start | bytes 98312 | tf_op jit(solution)/shard_map/ppermute | solution.py:28
  50.2 0.9 collective-permute-done.7
  51.1 2.4 %collective-permute-start.10 = (f32[64,128]{1,0:T(8,128)S(1)}, f32[64,128]{1,0:T(8,128)S(1)}, u32[]{:S(2)}, u32[]{:S(2)}) collective-permute-start(f32[64,128]{1,0:T(8,128)S(1)} %add.30), channel_id=1, source_target_pairs={{0,48},{16,32},{32,16},{48,0},{1,49},{17,33},{33,17},{49,1},{2,50}... | collective-permute-start | bytes 98312 | tf_op jit(solution)/shard_map/ppermute | solution.py:28
  53.5 1.4 %collective-permute-start.9 = (f32[64,128]{1,0:T(8,128)S(1)}, f32[64,128]{1,0:T(8,128)S(1)}, u32[]{:S(2)}, u32[]{:S(2)}) collective-permute-start(f32[64,128]{1,0:T(8,128)S(1)} %add.30), channel_id=1, source_target_pairs={{0,32},{16,48},{32,0},{48,16},{1,33},{17,49},{33,1},{49,17},{2,34}... | collective-permute-start | bytes 98312 | tf_op jit(solution)/shard_map/ppermute | solution.py:28
  55.1 2.7 %collective-permute-done.9 = f32[64,128]{1,0:T(8,128)S(1)} collective-permute-done((f32[64,128]{1,0:T(8,128)S(1)}, f32[64,128]{1,0:T(8,128)S(1)}, u32[]{:S(2)}, u32[]{:S(2)}) %collective-permute-start.9) | collective-permute-done | bytes 32800 | tf_op jit(solution)/shard_map/ppermute | solution.py:28
  57.8 7.1 %collective-permute-start.13 = (f32[64,128]{1,0:T(8,128)S(1)}, f32[64,128]{1,0:T(8,128)S(1)}, u32[]{:S(2)}, u32[]{:S(2)}) collective-permute-start(f32[64,128]{1,0:T(8,128)S(1)} %add_add_fusion.2), channel_id=1, source_target_pairs={{0,12},{4,8},{8,4},{12,0},{1,13},{5,9},{9,5},{13,1},{2,14},{6,10},... | collective-permute-start | bytes 98312 | tf_op jit(solution)/shard_map/ppermute | solution.py:28
  64.9 0.7 collective-permute-start.11
  65.6 0.6 collective-permute-done.13
  66.2 3.0 %collective-permute-done.12 = f32[64,128]{1,0:T(8,128)S(1)} collective-permute-done((f32[64,128]{1,0:T(8,128)S(1)}, f32[64,128]{1,0:T(8,128)S(1)}, u32[]{:S(2)}, u32[]{:S(2)}) %collective-permute-start.12) | collective-permute-done | bytes 32800 | tf_op jit(solution)/shard_map/ppermute | solution.py:28
  69.2 8.4 %collective-permute-start.16 = (f32[64,128]{1,0:T(8,128)S(1)}, f32[64,128]{1,0:T(8,128)S(1)}, u32[]{:S(2)}, u32[]{:S(2)}) collective-permute-start(f32[64,128]{1,0:T(8,128)S(1)} %add_add_fusion.1), channel_id=1, source_target_pairs={{0,192},{64,128},{128,64},{192,0},{1,193},{65,129},{129,65},{193,1... | collective-permute-start | bytes 98312 | tf_op jit(solution)/shard_map/ppermute | solution.py:28
  77.6 2.5 %collective-permute-start.15 = (f32[64,128]{1,0:T(8,128)S(1)}, f32[64,128]{1,0:T(8,128)S(1)}, u32[]{:S(2)}, u32[]{:S(2)}) collective-permute-start(f32[64,128]{1,0:T(8,128)S(1)} %add_add_fusion.1), channel_id=1, source_target_pairs={{0,128},{64,192},{128,0},{192,64},{1,129},{65,193},{129,1},{193,65... | collective-permute-start | bytes 98312 | tf_op jit(solution)/shard_map/ppermute | solution.py:28
  80.1 0.2 collective-permute-start.14
  80.3 4.1 %collective-permute-done.15 = f32[64,128]{1,0:T(8,128)S(1)} collective-permute-done((f32[64,128]{1,0:T(8,128)S(1)}, f32[64,128]{1,0:T(8,128)S(1)}, u32[]{:S(2)}, u32[]{:S(2)}) %collective-permute-start.15) | collective-permute-done | bytes 32800 | tf_op jit(solution)/shard_map/ppermute | solution.py:28
  84.4 5.7 %collective-permute-start.19 = (f32[64,128]{1,0:T(8,128)S(1)}, f32[64,128]{1,0:T(8,128)S(1)}, u32[]{:S(2)}, u32[]{:S(2)}) collective-permute-start(f32[64,128]{1,0:T(8,128)S(1)} %add_add_fusion.own), channel_id=1, source_target_pairs={{0,3},{1,2},{2,1},{3,0},{4,7},{5,6},{6,5},{7,4},{8,11},{9,10},{10,... | collective-permute-start | bytes 98312 | tf_op jit(solution)/shard_map/ppermute | solution.py:28
  90.1 0.5 collective-permute-start.17
  90.6 1.1 %collective-permute-done.19.last = f32[64,128]{1,0:T(8,128)S(1)} collective-permute-done((f32[64,128]{1,0:T(8,128)S(1)}, f32[64,128]{1,0:T(8,128)S(1)}, u32[]{:S(2)}, u32[]{:S(2)}) %collective-permute-start.19) | collective-permute-done | bytes 32800 | tf_op jit(solution)/shard_map/ppermute | solution.py:28
  91.7 1.1 %collective-permute-done.18.other_mode = f32[64,128]{1,0:T(8,128)S(1)} collective-permute-done((f32[64,128]{1,0:T(8,128)S(1)}, f32[64,128]{1,0:T(8,128)S(1)}, u32[]{:S(2)}, u32[]{:S(2)}) %collective-permute-start.18) | collective-permute-done | bytes 32800 | tf_op jit(solution)/shard_map/ppermute | solution.py:28
  92.9 8.3 %factor_and_project.1 = (bf16[64,4096]{1,0:T(8,128)(2,1)}, f32[128,128]{1,0:T(8,128)}) custom-call(s32[2]{0:T(128)S(1)} %pad_add_fusion.place, f32[64,128]{1,0:T(8,128)S(1)} %add_add_fusion.own, f32[64,128]{1,0:T(8,128)S(1)} %collective-permute-done.17.other_core, f32[64,128]{1,0:T(8,128)S(1)} %collective-permute-done.18.other_mode, ...), custom_call_target="tpu_custom_call" | custom-call | tf_op jit(solution)/shard_map/factor_and_project/pallas_call | solution.py:514
  (24 shorter events, 0.6 us)
Async XLA Ops:
  2.4 15.4 %collective-permute-start = (bf16[64,1024]{1,0:T(8,128)(2,1)S(1)}, bf16[64,1024]{1,0:T(8,128)(2,1)S(1)}, u32[]{:S(2)}, u32[]{:S(2)}) collective-permute-start(bf16[64,1024]{1,0:T(8,128)(2,1)S(1)} %get-tuple-element.24), channel_id=1, source_target_pairs={{0,2},{2,0},{1,3},{3,1},{4,6},{6,4},{5,7},{7,5},{8,10},{10,8},{9,1... | collective-permute-start | bytes 393224 | tf_op jit(solution)/shard_map/ppermute | solution.py:28
  5.7 12.1 %collective-permute-start.1 = (bf16[64,1024]{1,0:T(8,128)(2,1)S(1)}, bf16[64,1024]{1,0:T(8,128)(2,1)S(1)}, u32[]{:S(2)}, u32[]{:S(2)}) collective-permute-start(bf16[64,1024]{1,0:T(8,128)(2,1)S(1)} %get-tuple-element.25), channel_id=1, source_target_pairs={{2,4},{6,8},{10,12},{14,16},{18,20},{22,24},{26,28},{30,32},{34,36... | collective-permute-start | bytes 393224 | tf_op jit(solution)/shard_map/ppermute | solution.py:34
  19.9 8.6 %collective-permute-start.3 = (bf16[64,1024]{1,0:T(8,128)(2,1)S(1)}, bf16[64,1024]{1,0:T(8,128)(2,1)S(1)}, u32[]{:S(2)}, u32[]{:S(2)}) collective-permute-start(bf16[64,1024]{1,0:T(8,128)(2,1)S(1)} %get-tuple-element.26.new_far), channel_id=1, source_target_pairs={{2,4},{6,8},{10,12},{14,16},{18,20},{22,24},{26,28},{30,32},{34,36... | collective-permute-start | bytes 393224 | tf_op jit(solution)/shard_map/ppermute | solution.py:34
  23.3 5.3 %copy-start = (s32[2,8]{1,0:T(2,128)S(1)}, s32[2,8]{1,0:T(2,128)}, u32[]{:S(2)}) copy-start(s32[2,8]{1,0:T(2,128)} %send.3) | copy-start | bytes 196
  23.3 5.3 %collective-permute-start.2 = (bf16[64,1024]{1,0:T(8,128)(2,1)S(1)}, bf16[64,1024]{1,0:T(8,128)(2,1)S(1)}, u32[]{:S(2)}, u32[]{:S(2)}) collective-permute-start(bf16[64,1024]{1,0:T(8,128)(2,1)S(1)} %get-tuple-element.27.new_near), channel_id=1, source_target_pairs={{0,2},{2,0},{1,3},{3,1},{4,6},{6,4},{5,7},{7,5},{8,10},{10,8},{9,1... | collective-permute-start | bytes 393224 | tf_op jit(solution)/shard_map/ppermute | solution.py:28
  31.9 12.4 %collective-permute-start.6 = (bf16[64,4096]{1,0:T(8,128)(2,1)S(1)}, bf16[64,4096]{1,0:T(8,128)(2,1)S(1)}, u32[]{:S(2)}, u32[]{:S(2)}) collective-permute-start(bf16[64,4096]{1,0:T(8,128)(2,1)S(1)} %get-tuple-element.28.field.own), channel_id=1, source_target_pairs={{0,1},{1,0},{2,3},{3,2},{4,5},{5,4},{6,7},{7,6},{8,9},{9,8},{10,11... | collective-permute-start | bytes 1572872 | tf_op jit(solution)/shard_map/ppermute | solution.py:28
  32.0 7.8 %collective-permute-start.4 = (bf16[64,1024]{1,0:T(8,128)(2,1)S(1)}, bf16[64,1024]{1,0:T(8,128)(2,1)S(1)}, u32[]{:S(2)}, u32[]{:S(2)}) collective-permute-start(bf16[64,1024]{1,0:T(8,128)(2,1)S(1)} %get-tuple-element.29), channel_id=1, source_target_pairs={{0,2},{2,0},{1,3},{3,1},{4,6},{6,4},{5,7},{7,5},{8,10},{10,8},{9,1... | collective-permute-start | bytes 393224 | tf_op jit(solution)/shard_map/ppermute | solution.py:28
  33.3 6.7 %collective-permute-start.5 = (bf16[64,1024]{1,0:T(8,128)(2,1)S(1)}, bf16[64,1024]{1,0:T(8,128)(2,1)S(1)}, u32[]{:S(2)}, u32[]{:S(2)}) collective-permute-start(bf16[64,1024]{1,0:T(8,128)(2,1)S(1)} %get-tuple-element.30), channel_id=1, source_target_pairs={{2,4},{6,8},{10,12},{14,16},{18,20},{22,24},{26,28},{30,32},{34,36... | collective-permute-start | bytes 393224 | tf_op jit(solution)/shard_map/ppermute | solution.py:34
  47.9 3.2 %collective-permute-start.7 = (f32[64,128]{1,0:T(8,128)S(1)}, f32[64,128]{1,0:T(8,128)S(1)}, u32[]{:S(2)}, u32[]{:S(2)}) collective-permute-start(f32[64,128]{1,0:T(8,128)S(1)} %get-tuple-element.32), channel_id=1, source_target_pairs={{0,2},{2,0},{1,3},{3,1},{4,6},{6,4},{5,7},{7,5},{8,10},{10,8},{9,1... | collective-permute-start | bytes 98312 | tf_op jit(solution)/shard_map/ppermute | solution.py:28
  51.1 4.0 %collective-permute-start.10 = (f32[64,128]{1,0:T(8,128)S(1)}, f32[64,128]{1,0:T(8,128)S(1)}, u32[]{:S(2)}, u32[]{:S(2)}) collective-permute-start(f32[64,128]{1,0:T(8,128)S(1)} %add.30), channel_id=1, source_target_pairs={{0,48},{16,32},{32,16},{48,0},{1,49},{17,33},{33,17},{49,1},{2,50}... | collective-permute-start | bytes 98312 | tf_op jit(solution)/shard_map/ppermute | solution.py:28
  53.5 4.3 %collective-permute-start.9 = (f32[64,128]{1,0:T(8,128)S(1)}, f32[64,128]{1,0:T(8,128)S(1)}, u32[]{:S(2)}, u32[]{:S(2)}) collective-permute-start(f32[64,128]{1,0:T(8,128)S(1)} %add.30), channel_id=1, source_target_pairs={{0,32},{16,48},{32,0},{48,16},{1,33},{17,49},{33,1},{49,17},{2,34}... | collective-permute-start | bytes 98312 | tf_op jit(solution)/shard_map/ppermute | solution.py:28
  54.9 2.9 %collective-permute-start.8 = (f32[64,128]{1,0:T(8,128)S(1)}, f32[64,128]{1,0:T(8,128)S(1)}, u32[]{:S(2)}, u32[]{:S(2)}) collective-permute-start(f32[64,128]{1,0:T(8,128)S(1)} %add.30), channel_id=1, source_target_pairs={{0,16},{16,0},{32,48},{48,32},{1,17},{17,1},{33,49},{49,33},{2,18}... | collective-permute-start | bytes 98312 | tf_op jit(solution)/shard_map/ppermute | solution.py:28
  57.8 8.4 %collective-permute-start.13 = (f32[64,128]{1,0:T(8,128)S(1)}, f32[64,128]{1,0:T(8,128)S(1)}, u32[]{:S(2)}, u32[]{:S(2)}) collective-permute-start(f32[64,128]{1,0:T(8,128)S(1)} %add_add_fusion.2), channel_id=1, source_target_pairs={{0,12},{4,8},{8,4},{12,0},{1,13},{5,9},{9,5},{13,1},{2,14},{6,10},... | collective-permute-start | bytes 98312 | tf_op jit(solution)/shard_map/ppermute | solution.py:28
  64.9 4.3 %collective-permute-start.12 = (f32[64,128]{1,0:T(8,128)S(1)}, f32[64,128]{1,0:T(8,128)S(1)}, u32[]{:S(2)}, u32[]{:S(2)}) collective-permute-start(f32[64,128]{1,0:T(8,128)S(1)} %add_add_fusion.2), channel_id=1, source_target_pairs={{0,8},{4,12},{8,0},{12,4},{1,9},{5,13},{9,1},{13,5},{2,10},{6,14},... | collective-permute-start | bytes 98312 | tf_op jit(solution)/shard_map/ppermute | solution.py:28
  64.9 4.3 %collective-permute-start.11 = (f32[64,128]{1,0:T(8,128)S(1)}, f32[64,128]{1,0:T(8,128)S(1)}, u32[]{:S(2)}, u32[]{:S(2)}) collective-permute-start(f32[64,128]{1,0:T(8,128)S(1)} %add_add_fusion.2), channel_id=1, source_target_pairs={{0,4},{4,0},{8,12},{12,8},{1,5},{5,1},{9,13},{13,9},{2,6},{6,2},{1... | collective-permute-start | bytes 98312 | tf_op jit(solution)/shard_map/ppermute | solution.py:28
  69.2 11.1 %collective-permute-start.16 = (f32[64,128]{1,0:T(8,128)S(1)}, f32[64,128]{1,0:T(8,128)S(1)}, u32[]{:S(2)}, u32[]{:S(2)}) collective-permute-start(f32[64,128]{1,0:T(8,128)S(1)} %add_add_fusion.1), channel_id=1, source_target_pairs={{0,192},{64,128},{128,64},{192,0},{1,193},{65,129},{129,65},{193,1... | collective-permute-start | bytes 98312 | tf_op jit(solution)/shard_map/ppermute | solution.py:28
  77.6 6.8 %collective-permute-start.15 = (f32[64,128]{1,0:T(8,128)S(1)}, f32[64,128]{1,0:T(8,128)S(1)}, u32[]{:S(2)}, u32[]{:S(2)}) collective-permute-start(f32[64,128]{1,0:T(8,128)S(1)} %add_add_fusion.1), channel_id=1, source_target_pairs={{0,128},{64,192},{128,0},{192,64},{1,129},{65,193},{129,1},{193,65... | collective-permute-start | bytes 98312 | tf_op jit(solution)/shard_map/ppermute | solution.py:28
  80.1 4.3 %collective-permute-start.14 = (f32[64,128]{1,0:T(8,128)S(1)}, f32[64,128]{1,0:T(8,128)S(1)}, u32[]{:S(2)}, u32[]{:S(2)}) collective-permute-start(f32[64,128]{1,0:T(8,128)S(1)} %add_add_fusion.1), channel_id=1, source_target_pairs={{0,64},{64,0},{128,192},{192,128},{1,65},{65,1},{129,193},{193,129... | collective-permute-start | bytes 98312 | tf_op jit(solution)/shard_map/ppermute | solution.py:28
  84.4 7.3 %collective-permute-start.19 = (f32[64,128]{1,0:T(8,128)S(1)}, f32[64,128]{1,0:T(8,128)S(1)}, u32[]{:S(2)}, u32[]{:S(2)}) collective-permute-start(f32[64,128]{1,0:T(8,128)S(1)} %add_add_fusion.own), channel_id=1, source_target_pairs={{0,3},{1,2},{2,1},{3,0},{4,7},{5,6},{6,5},{7,4},{8,11},{9,10},{10,... | collective-permute-start | bytes 98312 | tf_op jit(solution)/shard_map/ppermute | solution.py:28
  90.1 2.8 %collective-permute-start.18 = (f32[64,128]{1,0:T(8,128)S(1)}, f32[64,128]{1,0:T(8,128)S(1)}, u32[]{:S(2)}, u32[]{:S(2)}) collective-permute-start(f32[64,128]{1,0:T(8,128)S(1)} %add_add_fusion.own), channel_id=1, source_target_pairs={{0,1},{1,0},{2,3},{3,2},{4,5},{5,4},{6,7},{7,6},{8,9},{9,8},{10,11... | collective-permute-start | bytes 98312 | tf_op jit(solution)/shard_map/ppermute | solution.py:28
  90.1 2.8 %collective-permute-start.17 = (f32[64,128]{1,0:T(8,128)S(1)}, f32[64,128]{1,0:T(8,128)S(1)}, u32[]{:S(2)}, u32[]{:S(2)}) collective-permute-start(f32[64,128]{1,0:T(8,128)S(1)} %add_add_fusion.own), channel_id=1, source_target_pairs={{0,2},{2,0},{1,3},{3,1},{4,6},{6,4},{5,7},{7,5},{8,10},{10,8},{9,1... | collective-permute-start | bytes 98312 | tf_op jit(solution)/shard_map/ppermute | solution.py:28

commit v6 on v5

--- a/solution.py
+++ b/solution.py
@@ -1,3 +1,5 @@
+import functools
+
 import jax
 import jax.numpy as jnp
 from jax import lax
@@ -13,6 +15,7 @@
 HBM = pl.BlockSpec(memory_space=pltpu.HBM)
 NT = (((1,), (1,)), ((), ()))
 GROUP = 8
+IMAGE_COST = 10**6
 IN_FLIGHT = 4
 
 
@@ -120,10 +123,12 @@
     )
 
 
-def fill_sources(field, sources):
-    width = field.shape[1]
-    sources[:, :width] = field[...]
-    sources[:, width:] = jnp.zeros((field.shape[0], sources.shape[1] - width), sources.dtype)
+def fill_sources(fields, sources):
+    at = 0
+    for field in fields:
+        sources[:, at : at + field.shape[1]] = field[...]
+        at += field.shape[1]
+    sources[:, at:] = jnp.zeros((sources.shape[0], sources.shape[1] - at), sources.dtype)
 
 
 def stage_and_sum(place, send_rows, tile_cols, tiles, field):
@@ -149,7 +154,7 @@
             copy.start()
         for i in range(IN_FLIGHT):
             chunk(i).start()
-        fill_sources(field, sources)
+        fill_sources((field,), sources)
         def arrive(step):
             for i in (2 * step, 2 * step + 1):
                 chunk(i).wait()
@@ -214,12 +219,13 @@
     )(place, in_hbm(send_rows), in_hbm(tile_cols), in_hbm(tiles), field)
 
 
-def local_sums(level, table, tiles, field, rows, nnz):
-    modes, width = field.shape
-    tile = tiles.shape[1]
-
-    def kernel(table, tiles, field, total, sources):
-        fill_sources(field, sources)
+def local_sums(level, table, tiles, fields, rows, nnz):
+    modes, tile = fields[0].shape[0], tiles.shape[1]
+    width = rows * tile
+
+    def kernel(table, tiles, *rest):
+        *fields, total, sources = rest
+        fill_sources(fields, sources)
 
         def step(i, carry):
             for u in range(GROUP):
@@ -231,13 +237,13 @@
     return pl.pallas_call(
         kernel,
         out_shape=shape((modes, width), jnp.float32),
-        in_specs=[SMEM, VMEM, VMEM],
+        in_specs=[SMEM] + [VMEM] * (1 + len(fields)),
         out_specs=VMEM,
-        scratch_shapes=[pltpu.VMEM((modes, width + tile), field.dtype)],
+        scratch_shapes=[pltpu.VMEM((modes, width + tile), fields[0].dtype)],
         compiler_params=params(8),
         cost_estimate=pl.CostEstimate(flops=tiles.size * modes // 8, bytes_accessed=0, transcendentals=0),
         name=f"local_sums_{level}",
-    )(table, tiles, field)
+    )(table, tiles, *fields)
 
 
 def fill_ghosts(core, near, far, ghosts):
@@ -359,33 +365,38 @@
 def last_level(nnz, place, table, send_rows, bounds, tiles, total, near, far, field, previous):
     modes, width = field.shape
     tile = tiles.shape[1]
+    groups = width // tile // GROUP
 
     def kernel(place, table, send, lower, upper, tiles, total, near, far, field, previous, *rest):
-        out, new_far, new_near, ghosts, partial = rest
+        first, second, new_far, new_near, whole, ghosts, partial = rest
         core = place[1]
         fill_ghosts(core, near, far, ghosts)
 
-        def store(u, row, value):
-            out[:, columns(row, tile)] = value
-
-        def step(i, carry):
+        def step(i, carry, out, start):
+            def store(u, row, value):
+                whole[:, columns(row, tile)] = value
+                out[:, columns(row - start * GROUP, tile)] = value
+
             rows = ghost_rows(table, None, tiles, ghosts, partial, i * GROUP, nnz)
             level_rows(2, (lower, upper), rows, total, partial, field, previous, store)
             return carry
 
-        lax.fori_loop(0, width // tile // GROUP, step, 0)
+        for out, start, stop in ((first, 0, groups - 1), (second, groups - 1, groups)):
+            lax.fori_loop(start, stop, functools.partial(step, out=out, start=start), 0)
         for slot in range(far.shape[1] // tile):
             here = slice(slot * tile, (slot + 1) * tile)
-            new_far[:, here] = out[:, columns(send[core, slot], tile)]
-            new_near[:, here] = out[:, columns(send[1 - core, slot], tile)]
+            new_far[:, here] = whole[:, columns(send[core, slot], tile)]
+            new_near[:, here] = whole[:, columns(send[1 - core, slot], tile)]
 
     part = shape(far.shape, far.dtype)
-    return pl.pallas_call(
-        kernel,
-        out_shape=(shape(field.shape, field.dtype), part, part),
+    parts = [shape((modes, count * GROUP * tile), field.dtype) for count in (groups - 1, 1)]
+    return pl.pallas_call(
+        kernel,
+        out_shape=(*parts, part, part),
         in_specs=[SMEM] * 5 + [VMEM] * 6,
-        out_specs=(VMEM,) * 3,
+        out_specs=(VMEM,) * 4,
         scratch_shapes=[
+            pltpu.VMEM((modes, width), field.dtype),
             pltpu.VMEM((modes, 2 * far.shape[1] + tile), far.dtype),
             pltpu.VMEM((modes, GROUP * tile), jnp.float32),
         ],
@@ -394,44 +405,65 @@
     )(place, table, send_rows, *bounds, tiles, total, near, far, field, previous)
 
 
-def partial_sums(nnz, place, table, tiles, total, near, far, own, partner):
-    modes, width = own.shape
+def image_rows(nnz, place, table, tiles, total, near, far):
+    modes, width = total.shape
     tile = tiles.shape[1]
-    product = shape((modes, 2 * modes), jnp.float32)
-
-    def kernel(place, table, tiles, total, near, far, own, partner, keep, send, both, ghosts, partial, left):
-        mode, core = place[0], place[1]
-        fill_ghosts(core, near, far, ghosts)
-        both[columns(mode, modes), :] = own[...]
-        both[columns(1 - mode, modes), :] = partner[...]
-        left[columns(core, modes), :] = own[...]
+
+    def kernel(place, table, tiles, total, near, far, out, ghosts, partial):
+        fill_ghosts(place[1], near, far, ghosts)
 
         def step(i, carry):
             rows = ghost_rows(table, None, tiles, ghosts, partial, i * GROUP, nnz)
             for u, row in enumerate(rows):
                 here = columns(row, tile)
-                value = total[:, here] + partial[:, u * tile : (u + 1) * tile]
-                left[columns(1 - core, modes), here] = value.astype(own.dtype)
+                out[:, here] = (total[:, here] + partial[:, u * tile : (u + 1) * tile]).astype(out.dtype)
             return carry
 
         lax.fori_loop(0, width // tile // GROUP, step, 0)
+
+    return pl.pallas_call(
+        kernel,
+        out_shape=shape((modes, width), near.dtype),
+        in_specs=[SMEM] * 2 + [VMEM] * 4,
+        out_specs=VMEM,
+        scratch_shapes=[
+            pltpu.VMEM((modes, 2 * near.shape[1] + tile), near.dtype),
+            pltpu.VMEM((modes, GROUP * tile), jnp.float32),
+        ],
+        compiler_params=params(8),
+        cost_estimate=pl.CostEstimate(flops=IMAGE_COST, bytes_accessed=0, transcendentals=0),
+        name="image_rows",
+    )(place, table, tiles, total, near, far)
+
+
+def partial_sums(place, own, partner, image):
+    modes, width = image.shape
+    product = shape((modes, 2 * modes), jnp.float32)
+
+    def kernel(place, own_first, own_second, first, second, image, keep, send, both, left):
+        mode, core = place[0], place[1]
+        split = own_first.shape[1]
+        for out, row, parts in (
+            (both, mode, (own_first, own_second)),
+            (both, 1 - mode, (first, second)),
+            (left, core, (own_first, own_second)),
+        ):
+            out[columns(row, modes), :split] = parts[0][...]
+            out[columns(row, modes), split:] = parts[1][...]
+        left[columns(1 - core, modes), :] = image[...]
         sums = lax.dot_general(left[...], both[...], NT, preferred_element_type=jnp.float32)
         keep[...] = sums[:modes]
         send[...] = sums[modes:]
 
     return pl.pallas_call(
         kernel,
-        out_shape=(product, product, shape((2 * modes, width), own.dtype)),
-        in_specs=[SMEM] * 2 + [VMEM] * 6,
+        out_shape=(product, product, shape((2 * modes, width), image.dtype)),
+        in_specs=[SMEM] + [VMEM] * 5,
         out_specs=(VMEM,) * 3,
-        scratch_shapes=[
-            pltpu.VMEM((modes, 2 * near.shape[1] + tile), near.dtype),
-            pltpu.VMEM((modes, GROUP * tile), jnp.float32),
-            pltpu.VMEM((2 * modes, width), own.dtype),
-        ],
+        scratch_shapes=[pltpu.VMEM((2 * modes, width), image.dtype)],
         compiler_params=params(12),
         name="partial_sums",
-    )(place, table, tiles, total, near, far, own, partner)
+    )(place, *own, *partner, image)
 
 
 def sum_over_chips(value):
@@ -541,15 +573,16 @@
     far, near = next_lists(1, *known)
     level_1 = next_level(1, *known, far, near)
     near, far = exchange(near, far)
-    total = local_sums(2, table, tiles, level_1, rows, nnz)
-
-    filtered, far, near = last_level(
+    total = local_sums(2, table, tiles, (level_1,), rows, nnz)
+
+    *filtered, far, near = last_level(
         nnz, place, table, send_rows, bounds, tiles, total, near, far, level_1, level_0
     )
-    partner = flipped(filtered, M, 1)
     near, far = exchange(near, far)
+    partner = [flipped(part, M, 1) for part in filtered]
     total = local_sums(3, table, tiles, filtered, rows, nnz)
-    keep, send, both = partial_sums(nnz, place, table, tiles, total, near, far, filtered, partner)
+    image = image_rows(nnz, place, table, tiles, total, near, far)
+    keep, send, both = partial_sums(place, filtered, partner, image)
     quarter = sum_over_chips(keep + flipped(send, C, 1))
     quarters = (quarter, flipped(quarter, C, 1), flipped(quarter, M, 1), flipped(quarter, (C, M), 3))
     basis, ritz = factor_and_project(place, quarters, both, dof_total)

time: 102 us -> 101 us (level); the launches traced: 101 us -> 101 us
  waiting for transfers between devices: 18.2 us -> 17.1 us
    pallas_call x1 -> x2, Pallas kernels: 3.36 us -> 6.39 us  [the longest x1 3.42 us: last_level(): pl.pallas_call(kernel, out_shape=(*parts, part, part), in_specs=[SMEM] *...]
    pallas_call x1, Pallas kernels: 3.52 us -> 1.09 us  [partial_sums(): pl.pallas_call(kernel, out_shape=(product, product, shape((2 * modes, wid...]
    ppermute x17 -> x18, starting transfers between devices: 36 us -> 37.9 us  [flipped(): lax.ppermute(block, axis, [(i, i ^ bits) for i in range(lax.axis_size(axi...]
    ppermute x3, starting transfers between devices: 9.04 us -> 7.68 us  [swapped_between_chips(): return lax.ppermute(block, DOF, pairs + [(b, a) for a, b in pairs])]
    ppermute x17 -> x18, waiting for transfers between devices: 18.1 us -> 16.8 us  [flipped(): lax.ppermute(block, axis, [(i, i ^ bits) for i in range(lax.axis_size(axi...]
  transfers between devices with their start and end apart: 20 -> 21, of which waited for: 10 -> 10; matrix products, arithmetic and copies ran while one was open for 0% -> 0% of each run, Pallas kernels for 17% -> 19%
where the time goes in v6:
time: 101 us
  starting transfers between devices  45.6 us (45%)
  Pallas kernels  36.3 us (36%)
  waiting for transfers between devices  17.1 us (17%)
  between operations  2.12 us (2%)
    ppermute x18, starting transfers between devices, flipped(): lax.ppermute(block, axis, [(i, i ^ bits) for i in range(lax.axis_size(axi...  37.9 us
    ppermute x18, waiting for transfers between devices, flipped(): lax.ppermute(block, axis, [(i, i ^ bits) for i in range(lax.axis_size(axi...  16.8 us
    pallas_call x1, Pallas kernels, stage_and_sum(): pl.pallas_call(kernel, out_shape=(shape(tiles.shape, tiles.dtype), shape(...  8.85 us
    pallas_call x1, Pallas kernels, factor_and_project(): pl.pallas_call(kernel, out_shape=(shape((modes, width), both.dtype), shap...  8.3 us
    ppermute x3, starting transfers between devices, swapped_between_chips(): return lax.ppermute(block, DOF, pairs + [(b, a) for a, b in pairs])  7.68 us
    pallas_call x2, Pallas kernels, local_sums(): pl.pallas_call(kernel, out_shape=shape((modes, width), jnp.float32), in_s...  5.49 us
    pallas_call x1, Pallas kernels, last_level(): pl.pallas_call(kernel, out_shape=(*parts, part, part), in_specs=[SMEM] *...  3.42 us
    pallas_call x1, Pallas kernels, image_rows(): pl.pallas_call(kernel, out_shape=shape((modes, width), near.dtype), in_sp...  2.97 us
  transfers between devices with their start and end apart: 21, of which 10 were waited for; matrix products, arithmetic and copies ran while one was open for 0% of the time, Pallas kernels for 19%

profile of v6, /device:TPU:1, one launch (start us, length us, event | category | flops | bytes accessed | tf_op | source)
XLA Modules:
  0.0 101.2 jit_solution(3911867334348276452)
XLA Ops:
  0.7 1.7 %pick_lists.1 = (bf16[64,4096]{1,0:T(8,128)(2,1)S(1)}, bf16[64,1024]{1,0:T(8,128)(2,1)S(1)}, bf16[64,1024]{1,0:T(8,128)(2,1)S(1)}) custom-call(s32[2]{0:T(128)S(1)} %pad_add_fusion.place, s32[2,8]{1,0:T(2,128)} %send.3, bf16[64,4096]{1,0:T(8,128)(2,1)} %bitcast.7), custom_call_target="tpu_custom_call" | custom-call | tf_op jit(solution)/shard_map/pick_lists/pallas_call | solution.py:64
  2.4 3.3 %collective-permute-start = (bf16[64,1024]{1,0:T(8,128)(2,1)S(1)}, bf16[64,1024]{1,0:T(8,128)(2,1)S(1)}, u32[]{:S(2)}, u32[]{:S(2)}) collective-permute-start(bf16[64,1024]{1,0:T(8,128)(2,1)S(1)} %get-tuple-element.25), channel_id=1, source_target_pairs={{0,2},{2,0},{1,3},{3,1},{4,6},{6,4},{5,7},{7,5},{8,10},{10,8},{9,1... | collective-permute-start | bytes 393224 | tf_op jit(solution)/shard_map/ppermute | solution.py:31
  5.7 1.9 %collective-permute-start.1 = (bf16[64,1024]{1,0:T(8,128)(2,1)S(1)}, bf16[64,1024]{1,0:T(8,128)(2,1)S(1)}, u32[]{:S(2)}, u32[]{:S(2)}) collective-permute-start(bf16[64,1024]{1,0:T(8,128)(2,1)S(1)} %get-tuple-element.26), channel_id=1, source_target_pairs={{2,4},{6,8},{10,12},{14,16},{18,20},{22,24},{26,28},{30,32},{34,36... | collective-permute-start | bytes 393224 | tf_op jit(solution)/shard_map/ppermute | solution.py:37
  8.9 8.9 %stage_and_sum.1 = (bf16[320,128,128]{2,1,0:T(8,128)(2,1)S(1)}, f32[64,4096]{1,0:T(8,128)S(1)}, s32[32,32]{1,0:T(8,128)S(1)}, s32[72]{0:T(128)S(1)}) custom-call(s32[2]{0:T(128)S(1)} %pad_add_fusion.place, s32[2,8]{1,0:T(2,128)} %send.3, s32[10,32]{1,0:T(8,128)} %bitcast.8, bf16[320,128,128]{2,1,0:T(8,128)(2,1)} %bitcast.6, ...), custom_call_target="tpu_custom_call" | custom-call | flops 671088640 | bytes 10485760 | tf_op jit(solution)/shard_map/stage_and_sum/pallas_call | solution.py:196
  17.8 2.1 %next_lists_1.1 = (bf16[64,1024]{1,0:T(8,128)(2,1)S(1)}, bf16[64,1024]{1,0:T(8,128)(2,1)S(1)}) custom-call(s32[2]{0:T(128)S(1)} %pad_add_fusion.place, s32[32,32]{1,0:T(8,128)S(1)} %get-tuple-element.21.table, s32[72]{0:T(128)S(1)} %get-tuple-element.23.order, f32[1]{0:T(128)S(6)} %copy.8.lower, f32[1]{0:T(128)S(6)} %copy.9.upper, ...), custom_call_target="tpu_custom_call" | custom-call | tf_op jit(solution)/shard_map/next_lists_1/pallas_call | solution.py:309
  19.9 3.3 %collective-permute-start.3 = (bf16[64,1024]{1,0:T(8,128)(2,1)S(1)}, bf16[64,1024]{1,0:T(8,128)(2,1)S(1)}, u32[]{:S(2)}, u32[]{:S(2)}) collective-permute-start(bf16[64,1024]{1,0:T(8,128)(2,1)S(1)} %get-tuple-element.27.new_far), channel_id=1, source_target_pairs={{2,4},{6,8},{10,12},{14,16},{18,20},{22,24},{26,28},{30,32},{34,36... | collective-permute-start | bytes 393224 | tf_op jit(solution)/shard_map/ppermute | solution.py:37
  23.4 2.4 %next_level_1.1.rest_0_.field = bf16[64,4096]{1,0:T(8,128)(2,1)S(1)} custom-call(s32[2]{0:T(128)S(1)} %pad_add_fusion.place, s32[32,32]{1,0:T(8,128)S(1)} %get-tuple-element.21.table, s32[72]{0:T(128)S(1)} %get-tuple-element.23.order, f32[1]{0:T(128)S(6)} %copy.8.lower, f32[1]{0:T(128)S(6)} %copy.9.upper, ...), custom_call_target="tpu_custom_call" | custom-call | flops 335544320 | bytes 10485760 | tf_op jit(solution)/shard_map/next_level_1/pallas_call | solution.py:350
  25.8 2.7 %local_sums_2.1.total = f32[64,4096]{1,0:T(8,128)S(1)} custom-call(s32[32,32]{1,0:T(8,128)S(1)} %get-tuple-element.21.table, bf16[320,128,128]{2,1,0:T(8,128)(2,1)S(1)} %get-tuple-element.22.tiles, bf16[64,4096]{1,0:T(8,128)(2,1)S(1)} %next_level_1.1.rest_0_.field), custom_call_target="tpu_custom_call" | custom-call | flops 41943040 | tf_op jit(solution)/shard_map/local_sums_2/pallas_call | solution.py:237
  28.6 3.4 %last_level.1 = (bf16[64,3072]{1,0:T(8,128)(2,1)S(1)}, bf16[64,1024]{1,0:T(8,128)(2,1)S(1)}, bf16[64,1024]{1,0:T(8,128)(2,1)S(1)}, bf16[64,1024]{1,0:T(8,128)(2,1)S(1)}) custom-call(s32[2]{0:T(128)S(1)} %pad_add_fusion.place, s32[32,32]{1,0:T(8,128)S(1)} %get-tuple-element.21.table, s32[2,8]{1,0:T(2,128)S(1)} %copy-done, f32[1]{0:T(128)S(6)} %copy.8.lower, ...), custom_call_target="tpu_custom_call" | custom-call | tf_op jit(solution)/shard_map/last_level/pallas_call | solution.py:393
  32.1 1.3 %collective-permute-start.6 = (bf16[64,1024]{1,0:T(8,128)(2,1)S(1)}, bf16[64,1024]{1,0:T(8,128)(2,1)S(1)}, u32[]{:S(2)}, u32[]{:S(2)}) collective-permute-start(bf16[64,1024]{1,0:T(8,128)(2,1)S(1)} %get-tuple-element.31), channel_id=1, source_target_pairs={{0,2},{2,0},{1,3},{3,1},{4,6},{6,4},{5,7},{7,5},{8,10},{10,8},{9,1... | collective-permute-start | bytes 393224 | tf_op jit(solution)/shard_map/ppermute | solution.py:31
  33.4 2.4 %collective-permute-start.7 = (bf16[64,1024]{1,0:T(8,128)(2,1)S(1)}, bf16[64,1024]{1,0:T(8,128)(2,1)S(1)}, u32[]{:S(2)}, u32[]{:S(2)}) collective-permute-start(bf16[64,1024]{1,0:T(8,128)(2,1)S(1)} %get-tuple-element.32), channel_id=1, source_target_pairs={{2,4},{6,8},{10,12},{14,16},{18,20},{22,24},{26,28},{30,32},{34,36... | collective-permute-start | bytes 393224 | tf_op jit(solution)/shard_map/ppermute | solution.py:37
  35.8 1.1 %collective-permute-start.5 = (bf16[64,1024]{1,0:T(8,128)(2,1)S(1)}, bf16[64,1024]{1,0:T(8,128)(2,1)S(1)}, u32[]{:S(2)}, u32[]{:S(2)}) collective-permute-start(bf16[64,1024]{1,0:T(8,128)(2,1)S(1)} %get-tuple-element.30.rest_1_.own_second), channel_id=1, source_target_pairs={{0,1},{1,0},{2,3},{3,2},{4,5},{5,4},{6,7},{7,6},{8,9},{9,8},{10,11... | collective-permute-start | bytes 393224 | tf_op jit(solution)/shard_map/ppermute | solution.py:31
  36.9 2.7 %local_sums_3.1.total = f32[64,4096]{1,0:T(8,128)S(1)} custom-call(s32[32,32]{1,0:T(8,128)S(1)} %get-tuple-element.21.table, bf16[320,128,128]{2,1,0:T(8,128)(2,1)S(1)} %get-tuple-element.22.tiles, bf16[64,3072]{1,0:T(8,128)(2,1)S(1)} %get-tuple-element.29.rest_0_.own_first, bf16[64,1024]{1,0:T(8,128)(2,1)S(1)} %get-tuple-element.30.rest_1_.own_second), custom_call_target="tpu_custom_call" | custom-call | flops 41943040 | tf_op jit(solution)/shard_map/local_sums_3/pallas_call | solution.py:237
  39.9 3.0 %image_rows.1.image = bf16[64,4096]{1,0:T(8,128)(2,1)S(1)} custom-call(s32[2]{0:T(128)S(1)} %pad_add_fusion.place, s32[32,32]{1,0:T(8,128)S(1)} %get-tuple-element.21.table, bf16[320,128,128]{2,1,0:T(8,128)(2,1)S(1)} %get-tuple-element.22.tiles, f32[64,4096]{1,0:T(8,128)S(1)} %local_sums_3.1.total, bf16[64,1024]{1,0:T(8,128)(2,1)S(1)} %collective-permute-done.6.near, ...), custom_call_target="tpu_custom_call" | custom-call | flops 1000000 | tf_op jit(solution)/shard_map/image_rows/pallas_call | solution.py:424
  42.9 1.5 %collective-permute-done.5.second = bf16[64,1024]{1,0:T(8,128)(2,1)S(1)} collective-permute-done((bf16[64,1024]{1,0:T(8,128)(2,1)S(1)}, bf16[64,1024]{1,0:T(8,128)(2,1)S(1)}, u32[]{:S(2)}, u32[]{:S(2)}) %collective-permute-start.5) | collective-permute-done | bytes 131104 | tf_op jit(solution)/shard_map/ppermute | solution.py:31
  44.4 1.1 %partial_sums.1 = (f32[64,128]{1,0:T(8,128)S(1)}, f32[64,128]{1,0:T(8,128)S(1)}, bf16[128,4096]{1,0:T(8,128)(2,1)S(1)}) custom-call(s32[2]{0:T(128)S(1)} %pad_add_fusion.place, bf16[64,3072]{1,0:T(8,128)(2,1)S(1)} %get-tuple-element.29.rest_0_.own_first, bf16[64,1024]{1,0:T(8,128)(2,1)S(1)} %get-tuple-element.30.rest_1_.own_second, ...), custom_call_target="tpu_custom_call" | custom-call | tf_op jit(solution)/shard_map/partial_sums/pallas_call | solution.py:458
  45.5 2.1 %collective-permute-start.8 = (f32[64,128]{1,0:T(8,128)S(1)}, f32[64,128]{1,0:T(8,128)S(1)}, u32[]{:S(2)}, u32[]{:S(2)}) collective-permute-start(f32[64,128]{1,0:T(8,128)S(1)} %get-tuple-element.34), channel_id=1, source_target_pairs={{0,2},{2,0},{1,3},{3,1},{4,6},{6,4},{5,7},{7,5},{8,10},{10,8},{9,1... | collective-permute-start | bytes 98312 | tf_op jit(solution)/shard_map/ppermute | solution.py:31
  47.6 0.9 collective-permute-done.8
  48.5 3.6 %collective-permute-start.11 = (f32[64,128]{1,0:T(8,128)S(1)}, f32[64,128]{1,0:T(8,128)S(1)}, u32[]{:S(2)}, u32[]{:S(2)}) collective-permute-start(f32[64,128]{1,0:T(8,128)S(1)} %add.30), channel_id=1, source_target_pairs={{0,48},{16,32},{32,16},{48,0},{1,49},{17,33},{33,17},{49,1},{2,50}... | collective-permute-start | bytes 98312 | tf_op jit(solution)/shard_map/ppermute | solution.py:31
  52.8 0.6 collective-permute-done.11
  53.4 3.0 %collective-permute-done.10 = f32[64,128]{1,0:T(8,128)S(1)} collective-permute-done((f32[64,128]{1,0:T(8,128)S(1)}, f32[64,128]{1,0:T(8,128)S(1)}, u32[]{:S(2)}, u32[]{:S(2)}) %collective-permute-start.10) | collective-permute-done | bytes 32800 | tf_op jit(solution)/shard_map/ppermute | solution.py:31
  56.4 7.6 %collective-permute-start.14 = (f32[64,128]{1,0:T(8,128)S(1)}, f32[64,128]{1,0:T(8,128)S(1)}, u32[]{:S(2)}, u32[]{:S(2)}) collective-permute-start(f32[64,128]{1,0:T(8,128)S(1)} %add_add_fusion.2), channel_id=1, source_target_pairs={{0,12},{4,8},{8,4},{12,0},{1,13},{5,9},{9,5},{13,1},{2,14},{6,10},... | collective-permute-start | bytes 98312 | tf_op jit(solution)/shard_map/ppermute | solution.py:31
  64.0 0.7 collective-permute-start.12
  64.6 0.6 collective-permute-done.14
  65.3 3.0 %collective-permute-done.13 = f32[64,128]{1,0:T(8,128)S(1)} collective-permute-done((f32[64,128]{1,0:T(8,128)S(1)}, f32[64,128]{1,0:T(8,128)S(1)}, u32[]{:S(2)}, u32[]{:S(2)}) %collective-permute-start.13) | collective-permute-done | bytes 32800 | tf_op jit(solution)/shard_map/ppermute | solution.py:31
  68.3 9.8 %collective-permute-start.17 = (f32[64,128]{1,0:T(8,128)S(1)}, f32[64,128]{1,0:T(8,128)S(1)}, u32[]{:S(2)}, u32[]{:S(2)}) collective-permute-start(f32[64,128]{1,0:T(8,128)S(1)} %add_add_fusion.1), channel_id=1, source_target_pairs={{0,192},{64,128},{128,64},{192,0},{1,193},{65,129},{129,65},{193,1... | collective-permute-start | bytes 98312 | tf_op jit(solution)/shard_map/ppermute | solution.py:31
  78.0 1.3 %collective-permute-start.16 = (f32[64,128]{1,0:T(8,128)S(1)}, f32[64,128]{1,0:T(8,128)S(1)}, u32[]{:S(2)}, u32[]{:S(2)}) collective-permute-start(f32[64,128]{1,0:T(8,128)S(1)} %add_add_fusion.1), channel_id=1, source_target_pairs={{0,128},{64,192},{128,0},{192,64},{1,129},{65,193},{129,1},{193,65... | collective-permute-start | bytes 98312 | tf_op jit(solution)/shard_map/ppermute | solution.py:31
  79.3 0.9 collective-permute-start.15
  80.2 5.0 %collective-permute-done.16 = f32[64,128]{1,0:T(8,128)S(1)} collective-permute-done((f32[64,128]{1,0:T(8,128)S(1)}, f32[64,128]{1,0:T(8,128)S(1)}, u32[]{:S(2)}, u32[]{:S(2)}) %collective-permute-start.16) | collective-permute-done | bytes 32800 | tf_op jit(solution)/shard_map/ppermute | solution.py:31
  85.2 4.9 %collective-permute-start.20 = (f32[64,128]{1,0:T(8,128)S(1)}, f32[64,128]{1,0:T(8,128)S(1)}, u32[]{:S(2)}, u32[]{:S(2)}) collective-permute-start(f32[64,128]{1,0:T(8,128)S(1)} %add_add_fusion.own), channel_id=1, source_target_pairs={{0,3},{1,2},{2,1},{3,0},{4,7},{5,6},{6,5},{7,4},{8,11},{9,10},{10,... | collective-permute-start | bytes 98312 | tf_op jit(solution)/shard_map/ppermute | solution.py:31
  90.7 1.7 %collective-permute-done.20.last = f32[64,128]{1,0:T(8,128)S(1)} collective-permute-done((f32[64,128]{1,0:T(8,128)S(1)}, f32[64,128]{1,0:T(8,128)S(1)}, u32[]{:S(2)}, u32[]{:S(2)}) %collective-permute-start.20) | collective-permute-done | bytes 32800 | tf_op jit(solution)/shard_map/ppermute | solution.py:31
  92.9 8.3 %factor_and_project.1 = (bf16[64,4096]{1,0:T(8,128)(2,1)}, f32[128,128]{1,0:T(8,128)}) custom-call(s32[2]{0:T(128)S(1)} %pad_add_fusion.place, f32[64,128]{1,0:T(8,128)S(1)} %add_add_fusion.own, f32[64,128]{1,0:T(8,128)S(1)} %collective-permute-done.18.other_core, f32[64,128]{1,0:T(8,128)S(1)} %collective-permute-done.19.other_mode, ...), custom_call_target="tpu_custom_call" | custom-call | tf_op jit(solution)/shard_map/factor_and_project/pallas_call | solution.py:546
  (27 shorter events, 2.3 us)
Async XLA Ops:
  2.4 15.4 %collective-permute-start = (bf16[64,1024]{1,0:T(8,128)(2,1)S(1)}, bf16[64,1024]{1,0:T(8,128)(2,1)S(1)}, u32[]{:S(2)}, u32[]{:S(2)}) collective-permute-start(bf16[64,1024]{1,0:T(8,128)(2,1)S(1)} %get-tuple-element.25), channel_id=1, source_target_pairs={{0,2},{2,0},{1,3},{3,1},{4,6},{6,4},{5,7},{7,5},{8,10},{10,8},{9,1... | collective-permute-start | bytes 393224 | tf_op jit(solution)/shard_map/ppermute | solution.py:31
  5.7 12.1 %collective-permute-start.1 = (bf16[64,1024]{1,0:T(8,128)(2,1)S(1)}, bf16[64,1024]{1,0:T(8,128)(2,1)S(1)}, u32[]{:S(2)}, u32[]{:S(2)}) collective-permute-start(bf16[64,1024]{1,0:T(8,128)(2,1)S(1)} %get-tuple-element.26), channel_id=1, source_target_pairs={{2,4},{6,8},{10,12},{14,16},{18,20},{22,24},{26,28},{30,32},{34,36... | collective-permute-start | bytes 393224 | tf_op jit(solution)/shard_map/ppermute | solution.py:37
  19.9 8.6 %collective-permute-start.3 = (bf16[64,1024]{1,0:T(8,128)(2,1)S(1)}, bf16[64,1024]{1,0:T(8,128)(2,1)S(1)}, u32[]{:S(2)}, u32[]{:S(2)}) collective-permute-start(bf16[64,1024]{1,0:T(8,128)(2,1)S(1)} %get-tuple-element.27.new_far), channel_id=1, source_target_pairs={{2,4},{6,8},{10,12},{14,16},{18,20},{22,24},{26,28},{30,32},{34,36... | collective-permute-start | bytes 393224 | tf_op jit(solution)/shard_map/ppermute | solution.py:37
  23.3 5.3 %copy-start = (s32[2,8]{1,0:T(2,128)S(1)}, s32[2,8]{1,0:T(2,128)}, u32[]{:S(2)}) copy-start(s32[2,8]{1,0:T(2,128)} %send.3) | copy-start | bytes 196
  23.3 5.3 %collective-permute-start.2 = (bf16[64,1024]{1,0:T(8,128)(2,1)S(1)}, bf16[64,1024]{1,0:T(8,128)(2,1)S(1)}, u32[]{:S(2)}, u32[]{:S(2)}) collective-permute-start(bf16[64,1024]{1,0:T(8,128)(2,1)S(1)} %get-tuple-element.28.new_near), channel_id=1, source_target_pairs={{0,2},{2,0},{1,3},{3,1},{4,6},{6,4},{5,7},{7,5},{8,10},{10,8},{9,1... | collective-permute-start | bytes 393224 | tf_op jit(solution)/shard_map/ppermute | solution.py:31
  32.0 12.4 %collective-permute-start.4 = (bf16[64,3072]{1,0:T(8,128)(2,1)S(1)}, bf16[64,3072]{1,0:T(8,128)(2,1)S(1)}, u32[]{:S(2)}, u32[]{:S(2)}) collective-permute-start(bf16[64,3072]{1,0:T(8,128)(2,1)S(1)} %get-tuple-element.29.rest_0_.own_first), channel_id=1, source_target_pairs={{0,1},{1,0},{2,3},{3,2},{4,5},{5,4},{6,7},{7,6},{8,9},{9,8},{10,11... | collective-permute-start | bytes 1179656 | tf_op jit(solution)/shard_map/ppermute | solution.py:31
  32.1 7.6 %collective-permute-start.6 = (bf16[64,1024]{1,0:T(8,128)(2,1)S(1)}, bf16[64,1024]{1,0:T(8,128)(2,1)S(1)}, u32[]{:S(2)}, u32[]{:S(2)}) collective-permute-start(bf16[64,1024]{1,0:T(8,128)(2,1)S(1)} %get-tuple-element.31), channel_id=1, source_target_pairs={{0,2},{2,0},{1,3},{3,1},{4,6},{6,4},{5,7},{7,5},{8,10},{10,8},{9,1... | collective-permute-start | bytes 393224 | tf_op jit(solution)/shard_map/ppermute | solution.py:31
  33.4 6.6 %collective-permute-start.7 = (bf16[64,1024]{1,0:T(8,128)(2,1)S(1)}, bf16[64,1024]{1,0:T(8,128)(2,1)S(1)}, u32[]{:S(2)}, u32[]{:S(2)}) collective-permute-start(bf16[64,1024]{1,0:T(8,128)(2,1)S(1)} %get-tuple-element.32), channel_id=1, source_target_pairs={{2,4},{6,8},{10,12},{14,16},{18,20},{22,24},{26,28},{30,32},{34,36... | collective-permute-start | bytes 393224 | tf_op jit(solution)/shard_map/ppermute | solution.py:37
  35.8 8.6 %collective-permute-start.5 = (bf16[64,1024]{1,0:T(8,128)(2,1)S(1)}, bf16[64,1024]{1,0:T(8,128)(2,1)S(1)}, u32[]{:S(2)}, u32[]{:S(2)}) collective-permute-start(bf16[64,1024]{1,0:T(8,128)(2,1)S(1)} %get-tuple-element.30.rest_1_.own_second), channel_id=1, source_target_pairs={{0,1},{1,0},{2,3},{3,2},{4,5},{5,4},{6,7},{7,6},{8,9},{9,8},{10,11... | collective-permute-start | bytes 393224 | tf_op jit(solution)/shard_map/ppermute | solution.py:31
  45.5 3.0 %collective-permute-start.8 = (f32[64,128]{1,0:T(8,128)S(1)}, f32[64,128]{1,0:T(8,128)S(1)}, u32[]{:S(2)}, u32[]{:S(2)}) collective-permute-start(f32[64,128]{1,0:T(8,128)S(1)} %get-tuple-element.34), channel_id=1, source_target_pairs={{0,2},{2,0},{1,3},{3,1},{4,6},{6,4},{5,7},{7,5},{8,10},{10,8},{9,1... | collective-permute-start | bytes 98312 | tf_op jit(solution)/shard_map/ppermute | solution.py:31
  48.5 4.9 %collective-permute-start.11 = (f32[64,128]{1,0:T(8,128)S(1)}, f32[64,128]{1,0:T(8,128)S(1)}, u32[]{:S(2)}, u32[]{:S(2)}) collective-permute-start(f32[64,128]{1,0:T(8,128)S(1)} %add.30), channel_id=1, source_target_pairs={{0,48},{16,32},{32,16},{48,0},{1,49},{17,33},{33,17},{49,1},{2,50}... | collective-permute-start | bytes 98312 | tf_op jit(solution)/shard_map/ppermute | solution.py:31
  52.1 4.3 %collective-permute-start.10 = (f32[64,128]{1,0:T(8,128)S(1)}, f32[64,128]{1,0:T(8,128)S(1)}, u32[]{:S(2)}, u32[]{:S(2)}) collective-permute-start(f32[64,128]{1,0:T(8,128)S(1)} %add.30), channel_id=1, source_target_pairs={{0,32},{16,48},{32,0},{48,16},{1,33},{17,49},{33,1},{49,17},{2,34}... | collective-permute-start | bytes 98312 | tf_op jit(solution)/shard_map/ppermute | solution.py:31
  52.6 3.8 %collective-permute-start.9 = (f32[64,128]{1,0:T(8,128)S(1)}, f32[64,128]{1,0:T(8,128)S(1)}, u32[]{:S(2)}, u32[]{:S(2)}) collective-permute-start(f32[64,128]{1,0:T(8,128)S(1)} %add.30), channel_id=1, source_target_pairs={{0,16},{16,0},{32,48},{48,32},{1,17},{17,1},{33,49},{49,33},{2,18}... | collective-permute-start | bytes 98312 | tf_op jit(solution)/shard_map/ppermute | solution.py:31
  56.4 8.9 %collective-permute-start.14 = (f32[64,128]{1,0:T(8,128)S(1)}, f32[64,128]{1,0:T(8,128)S(1)}, u32[]{:S(2)}, u32[]{:S(2)}) collective-permute-start(f32[64,128]{1,0:T(8,128)S(1)} %add_add_fusion.2), channel_id=1, source_target_pairs={{0,12},{4,8},{8,4},{12,0},{1,13},{5,9},{9,5},{13,1},{2,14},{6,10},... | collective-permute-start | bytes 98312 | tf_op jit(solution)/shard_map/ppermute | solution.py:31
  64.0 4.3 %collective-permute-start.13 = (f32[64,128]{1,0:T(8,128)S(1)}, f32[64,128]{1,0:T(8,128)S(1)}, u32[]{:S(2)}, u32[]{:S(2)}) collective-permute-start(f32[64,128]{1,0:T(8,128)S(1)} %add_add_fusion.2), channel_id=1, source_target_pairs={{0,8},{4,12},{8,0},{12,4},{1,9},{5,13},{9,1},{13,5},{2,10},{6,14},... | collective-permute-start | bytes 98312 | tf_op jit(solution)/shard_map/ppermute | solution.py:31
  64.0 4.3 %collective-permute-start.12 = (f32[64,128]{1,0:T(8,128)S(1)}, f32[64,128]{1,0:T(8,128)S(1)}, u32[]{:S(2)}, u32[]{:S(2)}) collective-permute-start(f32[64,128]{1,0:T(8,128)S(1)} %add_add_fusion.2), channel_id=1, source_target_pairs={{0,4},{4,0},{8,12},{12,8},{1,5},{5,1},{9,13},{13,9},{2,6},{6,2},{1... | collective-permute-start | bytes 98312 | tf_op jit(solution)/shard_map/ppermute | solution.py:31
  68.3 12.0 %collective-permute-start.17 = (f32[64,128]{1,0:T(8,128)S(1)}, f32[64,128]{1,0:T(8,128)S(1)}, u32[]{:S(2)}, u32[]{:S(2)}) collective-permute-start(f32[64,128]{1,0:T(8,128)S(1)} %add_add_fusion.1), channel_id=1, source_target_pairs={{0,192},{64,128},{128,64},{192,0},{1,193},{65,129},{129,65},{193,1... | collective-permute-start | bytes 98312 | tf_op jit(solution)/shard_map/ppermute | solution.py:31
  78.0 7.2 %collective-permute-start.16 = (f32[64,128]{1,0:T(8,128)S(1)}, f32[64,128]{1,0:T(8,128)S(1)}, u32[]{:S(2)}, u32[]{:S(2)}) collective-permute-start(f32[64,128]{1,0:T(8,128)S(1)} %add_add_fusion.1), channel_id=1, source_target_pairs={{0,128},{64,192},{128,0},{192,64},{1,129},{65,193},{129,1},{193,65... | collective-permute-start | bytes 98312 | tf_op jit(solution)/shard_map/ppermute | solution.py:31
  79.3 5.9 %collective-permute-start.15 = (f32[64,128]{1,0:T(8,128)S(1)}, f32[64,128]{1,0:T(8,128)S(1)}, u32[]{:S(2)}, u32[]{:S(2)}) collective-permute-start(f32[64,128]{1,0:T(8,128)S(1)} %add_add_fusion.1), channel_id=1, source_target_pairs={{0,64},{64,0},{128,192},{192,128},{1,65},{65,1},{129,193},{193,129... | collective-permute-start | bytes 98312 | tf_op jit(solution)/shard_map/ppermute | solution.py:31
  85.2 7.1 %collective-permute-start.20 = (f32[64,128]{1,0:T(8,128)S(1)}, f32[64,128]{1,0:T(8,128)S(1)}, u32[]{:S(2)}, u32[]{:S(2)}) collective-permute-start(f32[64,128]{1,0:T(8,128)S(1)} %add_add_fusion.own), channel_id=1, source_target_pairs={{0,3},{1,2},{2,1},{3,0},{4,7},{5,6},{6,5},{7,4},{8,11},{9,10},{10,... | collective-permute-start | bytes 98312 | tf_op jit(solution)/shard_map/ppermute | solution.py:31
  90.2 2.8 %collective-permute-start.19 = (f32[64,128]{1,0:T(8,128)S(1)}, f32[64,128]{1,0:T(8,128)S(1)}, u32[]{:S(2)}, u32[]{:S(2)}) collective-permute-start(f32[64,128]{1,0:T(8,128)S(1)} %add_add_fusion.own), channel_id=1, source_target_pairs={{0,1},{1,0},{2,3},{3,2},{4,5},{5,4},{6,7},{7,6},{8,9},{9,8},{10,11... | collective-permute-start | bytes 98312 | tf_op jit(solution)/shard_map/ppermute | solution.py:31
  90.5 2.4 %collective-permute-start.18 = (f32[64,128]{1,0:T(8,128)S(1)}, f32[64,128]{1,0:T(8,128)S(1)}, u32[]{:S(2)}, u32[]{:S(2)}) collective-permute-start(f32[64,128]{1,0:T(8,128)S(1)} %add_add_fusion.own), channel_id=1, source_target_pairs={{0,2},{2,0},{1,3},{3,1},{4,6},{6,4},{5,7},{7,5},{8,10},{10,8},{9,1... | collective-permute-start | bytes 98312 | tf_op jit(solution)/shard_map/ppermute | solution.py:31

commit v7 on v6

--- a/solution.py
+++ b/solution.py
@@ -468,7 +468,7 @@
 
 def sum_over_chips(value):
     for axis in (X, Y, Z):
-        others = [flipped(value, axis, bits) for bits in (1, 2, 3)]
+        others = [flipped(value, axis, bits) for bits in (1, 3, 2)]
         value = (value + others[0]) + (others[1] + others[2])
     return value
 
@@ -499,12 +499,12 @@
         solved = [None] * rows
         for s in reversed(range(rows)):
             value = unit[s] * reciprocal[s]
-            for t in range(s + 1, rows):
+            for t in reversed(range(s + 1, rows)):
                 value = value - ratio[t, s] * solved[t]
             solved[s] = value
         for k in range(b + 1, len(blocks)):
             value = blocks[k]
-            for s in range(rows):
+            for s in reversed(range(rows)):
                 value = value - spread(blocks[k], first + s) * solved[s]
             blocks[k] = value
         value = blocks[b]

time: 101 us -> 98.8 us (0.978)
  Pallas kernels: 36.3 us -> 34.6 us
  waiting for transfers between devices: 17.1 us -> 16 us
    ppermute x3, starting transfers between devices: 7.68 us -> 8.95 us  [swapped_between_chips(): return lax.ppermute(block, DOF, pairs + [(b, a) for a, b in pairs])]
    ppermute x18, waiting for transfers between devices: 16.8 us -> 15.7 us  [flipped(): lax.ppermute(block, axis, [(i, i ^ bits) for i in range(lax.axis_size(axi...]
  transfers between devices with their start and end apart: 21 -> 21, of which waited for: 10 -> 11; matrix products, arithmetic and copies ran while one was open for 0% -> 0% of each run, Pallas kernels for 19% -> 20%
where the time goes in v7:
time: 98.8 us; the launch traced here: 98.9 us
  starting transfers between devices  46.1 us (47%)
  Pallas kernels  34.6 us (35%)
  waiting for transfers between devices  16 us (16%)
  between operations  2.12 us (2%)
    ppermute x18, starting transfers between devices, flipped(): lax.ppermute(block, axis, [(i, i ^ bits) for i in range(lax.axis_size(axi...  37.2 us
    ppermute x18, waiting for transfers between devices, flipped(): lax.ppermute(block, axis, [(i, i ^ bits) for i in range(lax.axis_size(axi...  15.7 us
    ppermute x3, starting transfers between devices, swapped_between_chips(): return lax.ppermute(block, DOF, pairs + [(b, a) for a, b in pairs])  8.95 us
    pallas_call x1, Pallas kernels, stage_and_sum(): pl.pallas_call(kernel, out_shape=(shape(tiles.shape, tiles.dtype), shape(...  8.85 us
    pallas_call x1, Pallas kernels, factor_and_project(): pl.pallas_call(kernel, out_shape=(shape((modes, width), both.dtype), shap...  7.48 us
    pallas_call x2, Pallas kernels, local_sums(): pl.pallas_call(kernel, out_shape=shape((modes, width), jnp.float32), in_s...  5.5 us
    pallas_call x1, Pallas kernels, last_level(): pl.pallas_call(kernel, out_shape=(*parts, part, part), in_specs=[SMEM] *...  3.1 us
    pallas_call x1, Pallas kernels, image_rows(): pl.pallas_call(kernel, out_shape=shape((modes, width), near.dtype), in_sp...  2.7 us
  transfers between devices with their start and end apart: 21, of which 11 were waited for; matrix products, arithmetic and copies ran while one was open for 0% of the time, Pallas kernels for 20%

profile of v7, /device:TPU:1, one launch (start us, length us, event | category | flops | bytes accessed | tf_op | source)
XLA Modules:
  0.0 98.9 jit_solution(17087000451827532738)
XLA Ops:
  0.7 1.7 %pick_lists.1 = (bf16[64,4096]{1,0:T(8,128)(2,1)S(1)}, bf16[64,1024]{1,0:T(8,128)(2,1)S(1)}, bf16[64,1024]{1,0:T(8,128)(2,1)S(1)}) custom-call(s32[2]{0:T(128)S(1)} %pad_add_fusion.place, s32[2,8]{1,0:T(2,128)} %send.3, bf16[64,4096]{1,0:T(8,128)(2,1)} %bitcast.7), custom_call_target="tpu_custom_call" | custom-call | tf_op jit(solution)/shard_map/pick_lists/pallas_call | solution.py:64
  2.4 3.3 %collective-permute-start = (bf16[64,1024]{1,0:T(8,128)(2,1)S(1)}, bf16[64,1024]{1,0:T(8,128)(2,1)S(1)}, u32[]{:S(2)}, u32[]{:S(2)}) collective-permute-start(bf16[64,1024]{1,0:T(8,128)(2,1)S(1)} %get-tuple-element.25), channel_id=1, source_target_pairs={{0,2},{2,0},{1,3},{3,1},{4,6},{6,4},{5,7},{7,5},{8,10},{10,8},{9,1... | collective-permute-start | bytes 393224 | tf_op jit(solution)/shard_map/ppermute | solution.py:31
  5.7 1.9 %collective-permute-start.1 = (bf16[64,1024]{1,0:T(8,128)(2,1)S(1)}, bf16[64,1024]{1,0:T(8,128)(2,1)S(1)}, u32[]{:S(2)}, u32[]{:S(2)}) collective-permute-start(bf16[64,1024]{1,0:T(8,128)(2,1)S(1)} %get-tuple-element.26), channel_id=1, source_target_pairs={{2,4},{6,8},{10,12},{14,16},{18,20},{22,24},{26,28},{30,32},{34,36... | collective-permute-start | bytes 393224 | tf_op jit(solution)/shard_map/ppermute | solution.py:37
  8.9 8.8 %stage_and_sum.1 = (bf16[320,128,128]{2,1,0:T(8,128)(2,1)S(1)}, f32[64,4096]{1,0:T(8,128)S(1)}, s32[32,32]{1,0:T(8,128)S(1)}, s32[72]{0:T(128)S(1)}) custom-call(s32[2]{0:T(128)S(1)} %pad_add_fusion.place, s32[2,8]{1,0:T(2,128)} %send.3, s32[10,32]{1,0:T(8,128)} %bitcast.8, bf16[320,128,128]{2,1,0:T(8,128)(2,1)} %bitcast.6, ...), custom_call_target="tpu_custom_call" | custom-call | flops 671088640 | bytes 10485760 | tf_op jit(solution)/shard_map/stage_and_sum/pallas_call | solution.py:196
  17.8 1.8 %next_lists_1.1 = (bf16[64,1024]{1,0:T(8,128)(2,1)S(1)}, bf16[64,1024]{1,0:T(8,128)(2,1)S(1)}) custom-call(s32[2]{0:T(128)S(1)} %pad_add_fusion.place, s32[32,32]{1,0:T(8,128)S(1)} %get-tuple-element.21.table, s32[72]{0:T(128)S(1)} %get-tuple-element.23.order, f32[1]{0:T(128)S(6)} %copy.8.lower, f32[1]{0:T(128)S(6)} %copy.9.upper, ...), custom_call_target="tpu_custom_call" | custom-call | tf_op jit(solution)/shard_map/next_lists_1/pallas_call | solution.py:309
  19.6 4.0 %collective-permute-start.3 = (bf16[64,1024]{1,0:T(8,128)(2,1)S(1)}, bf16[64,1024]{1,0:T(8,128)(2,1)S(1)}, u32[]{:S(2)}, u32[]{:S(2)}) collective-permute-start(bf16[64,1024]{1,0:T(8,128)(2,1)S(1)} %get-tuple-element.27.new_far), channel_id=1, source_target_pairs={{2,4},{6,8},{10,12},{14,16},{18,20},{22,24},{26,28},{30,32},{34,36... | collective-permute-start | bytes 393224 | tf_op jit(solution)/shard_map/ppermute | solution.py:37
  23.7 2.4 %next_level_1.1.rest_0_.field = bf16[64,4096]{1,0:T(8,128)(2,1)S(1)} custom-call(s32[2]{0:T(128)S(1)} %pad_add_fusion.place, s32[32,32]{1,0:T(8,128)S(1)} %get-tuple-element.21.table, s32[72]{0:T(128)S(1)} %get-tuple-element.23.order, f32[1]{0:T(128)S(6)} %copy.8.lower, f32[1]{0:T(128)S(6)} %copy.9.upper, ...), custom_call_target="tpu_custom_call" | custom-call | flops 335544320 | bytes 10485760 | tf_op jit(solution)/shard_map/next_level_1/pallas_call | solution.py:350
  26.1 2.8 %local_sums_2.1.total = f32[64,4096]{1,0:T(8,128)S(1)} custom-call(s32[32,32]{1,0:T(8,128)S(1)} %get-tuple-element.21.table, bf16[320,128,128]{2,1,0:T(8,128)(2,1)S(1)} %get-tuple-element.22.tiles, bf16[64,4096]{1,0:T(8,128)(2,1)S(1)} %next_level_1.1.rest_0_.field), custom_call_target="tpu_custom_call" | custom-call | flops 41943040 | tf_op jit(solution)/shard_map/local_sums_2/pallas_call | solution.py:237
  28.9 3.1 %last_level.1 = (bf16[64,3072]{1,0:T(8,128)(2,1)S(1)}, bf16[64,1024]{1,0:T(8,128)(2,1)S(1)}, bf16[64,1024]{1,0:T(8,128)(2,1)S(1)}, bf16[64,1024]{1,0:T(8,128)(2,1)S(1)}) custom-call(s32[2]{0:T(128)S(1)} %pad_add_fusion.place, s32[32,32]{1,0:T(8,128)S(1)} %get-tuple-element.21.table, s32[2,8]{1,0:T(2,128)S(1)} %copy-done, f32[1]{0:T(128)S(6)} %copy.8.lower, ...), custom_call_target="tpu_custom_call" | custom-call | tf_op jit(solution)/shard_map/last_level/pallas_call | solution.py:393
  32.1 0.7 collective-permute-start.6
  32.8 3.1 %collective-permute-start.7 = (bf16[64,1024]{1,0:T(8,128)(2,1)S(1)}, bf16[64,1024]{1,0:T(8,128)(2,1)S(1)}, u32[]{:S(2)}, u32[]{:S(2)}) collective-permute-start(bf16[64,1024]{1,0:T(8,128)(2,1)S(1)} %get-tuple-element.32), channel_id=1, source_target_pairs={{2,4},{6,8},{10,12},{14,16},{18,20},{22,24},{26,28},{30,32},{34,36... | collective-permute-start | bytes 393224 | tf_op jit(solution)/shard_map/ppermute | solution.py:37
  36.3 2.7 %local_sums_3.1.total = f32[64,4096]{1,0:T(8,128)S(1)} custom-call(s32[32,32]{1,0:T(8,128)S(1)} %get-tuple-element.21.table, bf16[320,128,128]{2,1,0:T(8,128)(2,1)S(1)} %get-tuple-element.22.tiles, bf16[64,3072]{1,0:T(8,128)(2,1)S(1)} %get-tuple-element.29.rest_0_.own_first, bf16[64,1024]{1,0:T(8,128)(2,1)S(1)} %get-tuple-element.30.rest_1_.own_second), custom_call_target="tpu_custom_call" | custom-call | flops 41943040 | tf_op jit(solution)/shard_map/local_sums_3/pallas_call | solution.py:237
  39.3 2.7 %image_rows.1.image = bf16[64,4096]{1,0:T(8,128)(2,1)S(1)} custom-call(s32[2]{0:T(128)S(1)} %pad_add_fusion.place, s32[32,32]{1,0:T(8,128)S(1)} %get-tuple-element.21.table, bf16[320,128,128]{2,1,0:T(8,128)(2,1)S(1)} %get-tuple-element.22.tiles, f32[64,4096]{1,0:T(8,128)S(1)} %local_sums_3.1.total, bf16[64,1024]{1,0:T(8,128)(2,1)S(1)} %collective-permute-done.6.near, ...), custom_call_target="tpu_custom_call" | custom-call | flops 1000000 | tf_op jit(solution)/shard_map/image_rows/pallas_call | solution.py:424
  42.0 3.0 %collective-permute-done.5.second = bf16[64,1024]{1,0:T(8,128)(2,1)S(1)} collective-permute-done((bf16[64,1024]{1,0:T(8,128)(2,1)S(1)}, bf16[64,1024]{1,0:T(8,128)(2,1)S(1)}, u32[]{:S(2)}, u32[]{:S(2)}) %collective-permute-start.5) | collective-permute-done | bytes 131104 | tf_op jit(solution)/shard_map/ppermute | solution.py:31
  45.1 1.1 %partial_sums.1 = (f32[64,128]{1,0:T(8,128)S(1)}, f32[64,128]{1,0:T(8,128)S(1)}, bf16[128,4096]{1,0:T(8,128)(2,1)S(1)}) custom-call(s32[2]{0:T(128)S(1)} %pad_add_fusion.place, bf16[64,3072]{1,0:T(8,128)(2,1)S(1)} %get-tuple-element.29.rest_0_.own_first, bf16[64,1024]{1,0:T(8,128)(2,1)S(1)} %get-tuple-element.30.rest_1_.own_second, ...), custom_call_target="tpu_custom_call" | custom-call | tf_op jit(solution)/shard_map/partial_sums/pallas_call | solution.py:458
  46.2 1.4 %collective-permute-start.8 = (f32[64,128]{1,0:T(8,128)S(1)}, f32[64,128]{1,0:T(8,128)S(1)}, u32[]{:S(2)}, u32[]{:S(2)}) collective-permute-start(f32[64,128]{1,0:T(8,128)S(1)} %get-tuple-element.34), channel_id=1, source_target_pairs={{0,2},{2,0},{1,3},{3,1},{4,6},{6,4},{5,7},{7,5},{8,10},{10,8},{9,1... | collective-permute-start | bytes 98312 | tf_op jit(solution)/shard_map/ppermute | solution.py:31
  47.6 0.9 collective-permute-done.8
  48.5 2.5 %collective-permute-start.11 = (f32[64,128]{1,0:T(8,128)S(1)}, f32[64,128]{1,0:T(8,128)S(1)}, u32[]{:S(2)}, u32[]{:S(2)}) collective-permute-start(f32[64,128]{1,0:T(8,128)S(1)} %add.30), channel_id=1, source_target_pairs={{0,32},{16,48},{32,0},{48,16},{1,33},{17,49},{33,1},{49,17},{2,34}... | collective-permute-start | bytes 98312 | tf_op jit(solution)/shard_map/ppermute | solution.py:31
  50.9 2.6 %collective-permute-start.10 = (f32[64,128]{1,0:T(8,128)S(1)}, f32[64,128]{1,0:T(8,128)S(1)}, u32[]{:S(2)}, u32[]{:S(2)}) collective-permute-start(f32[64,128]{1,0:T(8,128)S(1)} %add.30), channel_id=1, source_target_pairs={{0,48},{16,32},{32,16},{48,0},{1,49},{17,33},{33,17},{49,1},{2,50}... | collective-permute-start | bytes 98312 | tf_op jit(solution)/shard_map/ppermute | solution.py:31
  53.6 1.3 %collective-permute-done.10 = f32[64,128]{1,0:T(8,128)S(1)} collective-permute-done((f32[64,128]{1,0:T(8,128)S(1)}, f32[64,128]{1,0:T(8,128)S(1)}, u32[]{:S(2)}, u32[]{:S(2)}) %collective-permute-start.10) | collective-permute-done | bytes 32800 | tf_op jit(solution)/shard_map/ppermute | solution.py:31
  54.9 1.4 %collective-permute-done.9 = f32[64,128]{1,0:T(8,128)S(1)} collective-permute-done((f32[64,128]{1,0:T(8,128)S(1)}, f32[64,128]{1,0:T(8,128)S(1)}, u32[]{:S(2)}, u32[]{:S(2)}) %collective-permute-start.9) | collective-permute-done | bytes 32800 | tf_op jit(solution)/shard_map/ppermute | solution.py:31
  56.4 1.0 collective-permute-start.14
  57.3 5.0 %collective-permute-start.13 = (f32[64,128]{1,0:T(8,128)S(1)}, f32[64,128]{1,0:T(8,128)S(1)}, u32[]{:S(2)}, u32[]{:S(2)}) collective-permute-start(f32[64,128]{1,0:T(8,128)S(1)} %add_add_fusion.2), channel_id=1, source_target_pairs={{0,12},{4,8},{8,4},{12,0},{1,13},{5,9},{9,5},{13,1},{2,14},{6,10},... | collective-permute-start | bytes 98312 | tf_op jit(solution)/shard_map/ppermute | solution.py:31
  62.8 0.8 collective-permute-done.13
  63.6 1.8 %collective-permute-done.12 = f32[64,128]{1,0:T(8,128)S(1)} collective-permute-done((f32[64,128]{1,0:T(8,128)S(1)}, f32[64,128]{1,0:T(8,128)S(1)}, u32[]{:S(2)}, u32[]{:S(2)}) %collective-permute-start.12) | collective-permute-done | bytes 32800 | tf_op jit(solution)/shard_map/ppermute | solution.py:31
  65.4 13.6 %collective-permute-start.17 = (f32[64,128]{1,0:T(8,128)S(1)}, f32[64,128]{1,0:T(8,128)S(1)}, u32[]{:S(2)}, u32[]{:S(2)}) collective-permute-start(f32[64,128]{1,0:T(8,128)S(1)} %add_add_fusion.1), channel_id=1, source_target_pairs={{0,128},{64,192},{128,0},{192,64},{1,129},{65,193},{129,1},{193,65... | collective-permute-start | bytes 98312 | tf_op jit(solution)/shard_map/ppermute | solution.py:31
  79.4 1.0 collective-permute-done.17
  80.3 3.5 %collective-permute-done.16 = f32[64,128]{1,0:T(8,128)S(1)} collective-permute-done((f32[64,128]{1,0:T(8,128)S(1)}, f32[64,128]{1,0:T(8,128)S(1)}, u32[]{:S(2)}, u32[]{:S(2)}) %collective-permute-start.16) | collective-permute-done | bytes 32800 | tf_op jit(solution)/shard_map/ppermute | solution.py:31
  83.9 4.0 %collective-permute-start.20 = (f32[64,128]{1,0:T(8,128)S(1)}, f32[64,128]{1,0:T(8,128)S(1)}, u32[]{:S(2)}, u32[]{:S(2)}) collective-permute-start(f32[64,128]{1,0:T(8,128)S(1)} %add_add_fusion.own), channel_id=1, source_target_pairs={{0,3},{1,2},{2,1},{3,0},{4,7},{5,6},{6,5},{7,4},{8,11},{9,10},{10,... | collective-permute-start | bytes 98312 | tf_op jit(solution)/shard_map/ppermute | solution.py:31
  87.9 1.5 %collective-permute-start.19 = (f32[64,128]{1,0:T(8,128)S(1)}, f32[64,128]{1,0:T(8,128)S(1)}, u32[]{:S(2)}, u32[]{:S(2)}) collective-permute-start(f32[64,128]{1,0:T(8,128)S(1)} %add_add_fusion.own), channel_id=1, source_target_pairs={{0,1},{1,0},{2,3},{3,2},{4,5},{5,4},{6,7},{7,6},{8,9},{9,8},{10,11... | collective-permute-start | bytes 98312 | tf_op jit(solution)/shard_map/ppermute | solution.py:31
  89.5 2.0 %collective-permute-done.19.other_mode = f32[64,128]{1,0:T(8,128)S(1)} collective-permute-done((f32[64,128]{1,0:T(8,128)S(1)}, f32[64,128]{1,0:T(8,128)S(1)}, u32[]{:S(2)}, u32[]{:S(2)}) %collective-permute-start.19) | collective-permute-done | bytes 32800 | tf_op jit(solution)/shard_map/ppermute | solution.py:31
  91.4 7.5 %factor_and_project.1 = (bf16[64,4096]{1,0:T(8,128)(2,1)}, f32[128,128]{1,0:T(8,128)}) custom-call(s32[2]{0:T(128)S(1)} %pad_add_fusion.place, f32[64,128]{1,0:T(8,128)S(1)} %add_add_fusion.own, f32[64,128]{1,0:T(8,128)S(1)} %collective-permute-done.18.other_core, f32[64,128]{1,0:T(8,128)S(1)} %collective-permute-done.19.other_mode, ...), custom_call_target="tpu_custom_call" | custom-call | tf_op jit(solution)/shard_map/factor_and_project/pallas_call | solution.py:546
  (27 shorter events, 2.0 us)
Async XLA Ops:
  2.4 15.4 %collective-permute-start = (bf16[64,1024]{1,0:T(8,128)(2,1)S(1)}, bf16[64,1024]{1,0:T(8,128)(2,1)S(1)}, u32[]{:S(2)}, u32[]{:S(2)}) collective-permute-start(bf16[64,1024]{1,0:T(8,128)(2,1)S(1)} %get-tuple-element.25), channel_id=1, source_target_pairs={{0,2},{2,0},{1,3},{3,1},{4,6},{6,4},{5,7},{7,5},{8,10},{10,8},{9,1... | collective-permute-start | bytes 393224 | tf_op jit(solution)/shard_map/ppermute | solution.py:31
  5.7 12.1 %collective-permute-start.1 = (bf16[64,1024]{1,0:T(8,128)(2,1)S(1)}, bf16[64,1024]{1,0:T(8,128)(2,1)S(1)}, u32[]{:S(2)}, u32[]{:S(2)}) collective-permute-start(bf16[64,1024]{1,0:T(8,128)(2,1)S(1)} %get-tuple-element.26), channel_id=1, source_target_pairs={{2,4},{6,8},{10,12},{14,16},{18,20},{22,24},{26,28},{30,32},{34,36... | collective-permute-start | bytes 393224 | tf_op jit(solution)/shard_map/ppermute | solution.py:37
  19.6 9.2 %collective-permute-start.3 = (bf16[64,1024]{1,0:T(8,128)(2,1)S(1)}, bf16[64,1024]{1,0:T(8,128)(2,1)S(1)}, u32[]{:S(2)}, u32[]{:S(2)}) collective-permute-start(bf16[64,1024]{1,0:T(8,128)(2,1)S(1)} %get-tuple-element.27.new_far), channel_id=1, source_target_pairs={{2,4},{6,8},{10,12},{14,16},{18,20},{22,24},{26,28},{30,32},{34,36... | collective-permute-start | bytes 393224 | tf_op jit(solution)/shard_map/ppermute | solution.py:37
  23.6 5.3 %copy-start = (s32[2,8]{1,0:T(2,128)S(1)}, s32[2,8]{1,0:T(2,128)}, u32[]{:S(2)}) copy-start(s32[2,8]{1,0:T(2,128)} %send.3) | copy-start | bytes 196
  23.6 5.3 %collective-permute-start.2 = (bf16[64,1024]{1,0:T(8,128)(2,1)S(1)}, bf16[64,1024]{1,0:T(8,128)(2,1)S(1)}, u32[]{:S(2)}, u32[]{:S(2)}) collective-permute-start(bf16[64,1024]{1,0:T(8,128)(2,1)S(1)} %get-tuple-element.28.new_near), channel_id=1, source_target_pairs={{0,2},{2,0},{1,3},{3,1},{4,6},{6,4},{5,7},{7,5},{8,10},{10,8},{9,1... | collective-permute-start | bytes 393224 | tf_op jit(solution)/shard_map/ppermute | solution.py:31
  32.0 13.1 %collective-permute-start.4 = (bf16[64,3072]{1,0:T(8,128)(2,1)S(1)}, bf16[64,3072]{1,0:T(8,128)(2,1)S(1)}, u32[]{:S(2)}, u32[]{:S(2)}) collective-permute-start(bf16[64,3072]{1,0:T(8,128)(2,1)S(1)} %get-tuple-element.29.rest_0_.own_first), channel_id=1, source_target_pairs={{0,1},{1,0},{2,3},{3,2},{4,5},{5,4},{6,7},{7,6},{8,9},{9,8},{10,11... | collective-permute-start | bytes 1179656 | tf_op jit(solution)/shard_map/ppermute | solution.py:31
  32.1 7.0 %collective-permute-start.6 = (bf16[64,1024]{1,0:T(8,128)(2,1)S(1)}, bf16[64,1024]{1,0:T(8,128)(2,1)S(1)}, u32[]{:S(2)}, u32[]{:S(2)}) collective-permute-start(bf16[64,1024]{1,0:T(8,128)(2,1)S(1)} %get-tuple-element.31), channel_id=1, source_target_pairs={{0,2},{2,0},{1,3},{3,1},{4,6},{6,4},{5,7},{7,5},{8,10},{10,8},{9,1... | collective-permute-start | bytes 393224 | tf_op jit(solution)/shard_map/ppermute | solution.py:31
  32.8 6.6 %collective-permute-start.7 = (bf16[64,1024]{1,0:T(8,128)(2,1)S(1)}, bf16[64,1024]{1,0:T(8,128)(2,1)S(1)}, u32[]{:S(2)}, u32[]{:S(2)}) collective-permute-start(bf16[64,1024]{1,0:T(8,128)(2,1)S(1)} %get-tuple-element.32), channel_id=1, source_target_pairs={{2,4},{6,8},{10,12},{14,16},{18,20},{22,24},{26,28},{30,32},{34,36... | collective-permute-start | bytes 393224 | tf_op jit(solution)/shard_map/ppermute | solution.py:37
  35.9 9.2 %collective-permute-start.5 = (bf16[64,1024]{1,0:T(8,128)(2,1)S(1)}, bf16[64,1024]{1,0:T(8,128)(2,1)S(1)}, u32[]{:S(2)}, u32[]{:S(2)}) collective-permute-start(bf16[64,1024]{1,0:T(8,128)(2,1)S(1)} %get-tuple-element.30.rest_1_.own_second), channel_id=1, source_target_pairs={{0,1},{1,0},{2,3},{3,2},{4,5},{5,4},{6,7},{7,6},{8,9},{9,8},{10,11... | collective-permute-start | bytes 393224 | tf_op jit(solution)/shard_map/ppermute | solution.py:31
  46.2 2.3 %collective-permute-start.8 = (f32[64,128]{1,0:T(8,128)S(1)}, f32[64,128]{1,0:T(8,128)S(1)}, u32[]{:S(2)}, u32[]{:S(2)}) collective-permute-start(f32[64,128]{1,0:T(8,128)S(1)} %get-tuple-element.34), channel_id=1, source_target_pairs={{0,2},{2,0},{1,3},{3,1},{4,6},{6,4},{5,7},{7,5},{8,10},{10,8},{9,1... | collective-permute-start | bytes 98312 | tf_op jit(solution)/shard_map/ppermute | solution.py:31
  48.5 5.1 %collective-permute-start.11 = (f32[64,128]{1,0:T(8,128)S(1)}, f32[64,128]{1,0:T(8,128)S(1)}, u32[]{:S(2)}, u32[]{:S(2)}) collective-permute-start(f32[64,128]{1,0:T(8,128)S(1)} %add.30), channel_id=1, source_target_pairs={{0,32},{16,48},{32,0},{48,16},{1,33},{17,49},{33,1},{49,17},{2,34}... | collective-permute-start | bytes 98312 | tf_op jit(solution)/shard_map/ppermute | solution.py:31
  50.9 4.0 %collective-permute-start.10 = (f32[64,128]{1,0:T(8,128)S(1)}, f32[64,128]{1,0:T(8,128)S(1)}, u32[]{:S(2)}, u32[]{:S(2)}) collective-permute-start(f32[64,128]{1,0:T(8,128)S(1)} %add.30), channel_id=1, source_target_pairs={{0,48},{16,32},{32,16},{48,0},{1,49},{17,33},{33,17},{49,1},{2,50}... | collective-permute-start | bytes 98312 | tf_op jit(solution)/shard_map/ppermute | solution.py:31
  53.6 2.8 %collective-permute-start.9 = (f32[64,128]{1,0:T(8,128)S(1)}, f32[64,128]{1,0:T(8,128)S(1)}, u32[]{:S(2)}, u32[]{:S(2)}) collective-permute-start(f32[64,128]{1,0:T(8,128)S(1)} %add.30), channel_id=1, source_target_pairs={{0,16},{16,0},{32,48},{48,32},{1,17},{17,1},{33,49},{49,33},{2,18}... | collective-permute-start | bytes 98312 | tf_op jit(solution)/shard_map/ppermute | solution.py:31
  56.4 6.4 %collective-permute-start.14 = (f32[64,128]{1,0:T(8,128)S(1)}, f32[64,128]{1,0:T(8,128)S(1)}, u32[]{:S(2)}, u32[]{:S(2)}) collective-permute-start(f32[64,128]{1,0:T(8,128)S(1)} %add_add_fusion.2), channel_id=1, source_target_pairs={{0,8},{4,12},{8,0},{12,4},{1,9},{5,13},{9,1},{13,5},{2,10},{6,14},... | collective-permute-start | bytes 98312 | tf_op jit(solution)/shard_map/ppermute | solution.py:31
  57.3 6.3 %collective-permute-start.13 = (f32[64,128]{1,0:T(8,128)S(1)}, f32[64,128]{1,0:T(8,128)S(1)}, u32[]{:S(2)}, u32[]{:S(2)}) collective-permute-start(f32[64,128]{1,0:T(8,128)S(1)} %add_add_fusion.2), channel_id=1, source_target_pairs={{0,12},{4,8},{8,4},{12,0},{1,13},{5,9},{9,5},{13,1},{2,14},{6,10},... | collective-permute-start | bytes 98312 | tf_op jit(solution)/shard_map/ppermute | solution.py:31
  62.3 3.1 %collective-permute-start.12 = (f32[64,128]{1,0:T(8,128)S(1)}, f32[64,128]{1,0:T(8,128)S(1)}, u32[]{:S(2)}, u32[]{:S(2)}) collective-permute-start(f32[64,128]{1,0:T(8,128)S(1)} %add_add_fusion.2), channel_id=1, source_target_pairs={{0,4},{4,0},{8,12},{12,8},{1,5},{5,1},{9,13},{13,9},{2,6},{6,2},{1... | collective-permute-start | bytes 98312 | tf_op jit(solution)/shard_map/ppermute | solution.py:31
  65.4 14.9 %collective-permute-start.17 = (f32[64,128]{1,0:T(8,128)S(1)}, f32[64,128]{1,0:T(8,128)S(1)}, u32[]{:S(2)}, u32[]{:S(2)}) collective-permute-start(f32[64,128]{1,0:T(8,128)S(1)} %add_add_fusion.1), channel_id=1, source_target_pairs={{0,128},{64,192},{128,0},{192,64},{1,129},{65,193},{129,1},{193,65... | collective-permute-start | bytes 98312 | tf_op jit(solution)/shard_map/ppermute | solution.py:31
  79.0 4.9 %collective-permute-start.16 = (f32[64,128]{1,0:T(8,128)S(1)}, f32[64,128]{1,0:T(8,128)S(1)}, u32[]{:S(2)}, u32[]{:S(2)}) collective-permute-start(f32[64,128]{1,0:T(8,128)S(1)} %add_add_fusion.1), channel_id=1, source_target_pairs={{0,192},{64,128},{128,64},{192,0},{1,193},{65,129},{129,65},{193,1... | collective-permute-start | bytes 98312 | tf_op jit(solution)/shard_map/ppermute | solution.py:31
  79.0 4.9 %collective-permute-start.15 = (f32[64,128]{1,0:T(8,128)S(1)}, f32[64,128]{1,0:T(8,128)S(1)}, u32[]{:S(2)}, u32[]{:S(2)}) collective-permute-start(f32[64,128]{1,0:T(8,128)S(1)} %add_add_fusion.1), channel_id=1, source_target_pairs={{0,64},{64,0},{128,192},{192,128},{1,65},{65,1},{129,193},{193,129... | collective-permute-start | bytes 98312 | tf_op jit(solution)/shard_map/ppermute | solution.py:31
  83.9 5.6 %collective-permute-start.20 = (f32[64,128]{1,0:T(8,128)S(1)}, f32[64,128]{1,0:T(8,128)S(1)}, u32[]{:S(2)}, u32[]{:S(2)}) collective-permute-start(f32[64,128]{1,0:T(8,128)S(1)} %add_add_fusion.own), channel_id=1, source_target_pairs={{0,3},{1,2},{2,1},{3,0},{4,7},{5,6},{6,5},{7,4},{8,11},{9,10},{10,... | collective-permute-start | bytes 98312 | tf_op jit(solution)/shard_map/ppermute | solution.py:31
  87.9 3.6 %collective-permute-start.19 = (f32[64,128]{1,0:T(8,128)S(1)}, f32[64,128]{1,0:T(8,128)S(1)}, u32[]{:S(2)}, u32[]{:S(2)}) collective-permute-start(f32[64,128]{1,0:T(8,128)S(1)} %add_add_fusion.own), channel_id=1, source_target_pairs={{0,1},{1,0},{2,3},{3,2},{4,5},{5,4},{6,7},{7,6},{8,9},{9,8},{10,11... | collective-permute-start | bytes 98312 | tf_op jit(solution)/shard_map/ppermute | solution.py:31
  89.4 2.0 %collective-permute-start.18 = (f32[64,128]{1,0:T(8,128)S(1)}, f32[64,128]{1,0:T(8,128)S(1)}, u32[]{:S(2)}, u32[]{:S(2)}) collective-permute-start(f32[64,128]{1,0:T(8,128)S(1)} %add_add_fusion.own), channel_id=1, source_target_pairs={{0,2},{2,0},{1,3},{3,1},{4,6},{6,4},{5,7},{7,5},{8,10},{10,8},{9,1... | collective-permute-start | bytes 98312 | tf_op jit(solution)/shard_map/ppermute | solution.py:31

commit v8 on v7

--- a/solution.py
+++ b/solution.py
@@ -1,5 +1,3 @@
-import functools
-
 import jax
 import jax.numpy as jnp
 from jax import lax
@@ -15,7 +13,8 @@
 HBM = pl.BlockSpec(memory_space=pltpu.HBM)
 NT = (((1,), (1,)), ((), ()))
 GROUP = 8
-IMAGE_COST = 10**6
+IMAGE_COST = 10**9
+FIRST_PART = 20
 IN_FLIGHT = 4
 
 
@@ -365,31 +364,31 @@
 def last_level(nnz, place, table, send_rows, bounds, tiles, total, near, far, field, previous):
     modes, width = field.shape
     tile = tiles.shape[1]
-    groups = width // tile // GROUP
+    split = FIRST_PART * tile
 
     def kernel(place, table, send, lower, upper, tiles, total, near, far, field, previous, *rest):
         first, second, new_far, new_near, whole, ghosts, partial = rest
         core = place[1]
         fill_ghosts(core, near, far, ghosts)
 
-        def step(i, carry, out, start):
-            def store(u, row, value):
-                whole[:, columns(row, tile)] = value
-                out[:, columns(row - start * GROUP, tile)] = value
-
+        def store(u, row, value):
+            whole[:, columns(row, tile)] = value
+
+        def step(i, carry):
             rows = ghost_rows(table, None, tiles, ghosts, partial, i * GROUP, nnz)
             level_rows(2, (lower, upper), rows, total, partial, field, previous, store)
             return carry
 
-        for out, start, stop in ((first, 0, groups - 1), (second, groups - 1, groups)):
-            lax.fori_loop(start, stop, functools.partial(step, out=out, start=start), 0)
+        lax.fori_loop(0, width // tile // GROUP, step, 0)
+        first[...] = whole[:, :split]
+        second[...] = whole[:, split:]
         for slot in range(far.shape[1] // tile):
             here = slice(slot * tile, (slot + 1) * tile)
             new_far[:, here] = whole[:, columns(send[core, slot], tile)]
             new_near[:, here] = whole[:, columns(send[1 - core, slot], tile)]
 
     part = shape(far.shape, far.dtype)
-    parts = [shape((modes, count * GROUP * tile), field.dtype) for count in (groups - 1, 1)]
+    parts = [shape((modes, part_width), field.dtype) for part_width in (split, width - split)]
     return pl.pallas_call(
         kernel,
         out_shape=(*parts, part, part),

time: 98.8 us -> 98.1 us (level)
  waiting for transfers between devices: 16 us -> 15 us
    ppermute x18, starting transfers between devices: 37.2 us -> 35.6 us  [flipped(): lax.ppermute(block, axis, [(i, i ^ bits) for i in range(lax.axis_size(axi...]
  transfers between devices with their start and end apart: 21 -> 21, of which waited for: 11 -> 10; matrix products, arithmetic and copies ran while one was open for 0% -> 0% of each run, Pallas kernels for 20% -> 20%
where the time goes in v8:
time: 98.1 us; the launch traced here: 97.8 us
  starting transfers between devices  45.2 us (46%)
  Pallas kernels  35.4 us (36%)
  waiting for transfers between devices  15 us (15%)
  between operations  2.12 us (2%)
    ppermute x18, starting transfers between devices, flipped(): lax.ppermute(block, axis, [(i, i ^ bits) for i in range(lax.axis_size(axi...  35.6 us
    ppermute x18, waiting for transfers between devices, flipped(): lax.ppermute(block, axis, [(i, i ^ bits) for i in range(lax.axis_size(axi...  14.9 us
    ppermute x3, starting transfers between devices, swapped_between_chips(): return lax.ppermute(block, DOF, pairs + [(b, a) for a, b in pairs])  9.57 us
    pallas_call x1, Pallas kernels, stage_and_sum(): pl.pallas_call(kernel, out_shape=(shape(tiles.shape, tiles.dtype), shape(...  8.84 us
    pallas_call x1, Pallas kernels, factor_and_project(): pl.pallas_call(kernel, out_shape=(shape((modes, width), both.dtype), shap...  7.47 us
    pallas_call x2, Pallas kernels, local_sums(): pl.pallas_call(kernel, out_shape=shape((modes, width), jnp.float32), in_s...  5.51 us
    pallas_call x1, Pallas kernels, last_level(): pl.pallas_call(kernel, out_shape=(*parts, part, part), in_specs=[SMEM] *...  3.37 us
    pallas_call x1, Pallas kernels, image_rows(): pl.pallas_call(kernel, out_shape=shape((modes, width), near.dtype), in_sp...  2.98 us
  transfers between devices with their start and end apart: 21, of which 10 were waited for; matrix products, arithmetic and copies ran while one was open for 0% of the time, Pallas kernels for 20%

profile of v8, /device:TPU:1, one launch (start us, length us, event | category | flops | bytes accessed | tf_op | source)
XLA Modules:
  0.0 97.8 jit_solution(35212778747293434)
XLA Ops:
  0.7 1.7 %pick_lists.1 = (bf16[64,4096]{1,0:T(8,128)(2,1)S(1)}, bf16[64,1024]{1,0:T(8,128)(2,1)S(1)}, bf16[64,1024]{1,0:T(8,128)(2,1)S(1)}) custom-call(s32[2]{0:T(128)S(1)} %pad_add_fusion.place, s32[2,8]{1,0:T(2,128)} %send.3, bf16[64,4096]{1,0:T(8,128)(2,1)} %bitcast.7), custom_call_target="tpu_custom_call" | custom-call | tf_op jit(solution)/shard_map/pick_lists/pallas_call | solution.py:63
  2.4 3.3 %collective-permute-start = (bf16[64,1024]{1,0:T(8,128)(2,1)S(1)}, bf16[64,1024]{1,0:T(8,128)(2,1)S(1)}, u32[]{:S(2)}, u32[]{:S(2)}) collective-permute-start(bf16[64,1024]{1,0:T(8,128)(2,1)S(1)} %get-tuple-element.25), channel_id=1, source_target_pairs={{0,2},{2,0},{1,3},{3,1},{4,6},{6,4},{5,7},{7,5},{8,10},{10,8},{9,1... | collective-permute-start | bytes 393224 | tf_op jit(solution)/shard_map/ppermute | solution.py:30
  5.7 1.9 %collective-permute-start.1 = (bf16[64,1024]{1,0:T(8,128)(2,1)S(1)}, bf16[64,1024]{1,0:T(8,128)(2,1)S(1)}, u32[]{:S(2)}, u32[]{:S(2)}) collective-permute-start(bf16[64,1024]{1,0:T(8,128)(2,1)S(1)} %get-tuple-element.26), channel_id=1, source_target_pairs={{2,4},{6,8},{10,12},{14,16},{18,20},{22,24},{26,28},{30,32},{34,36... | collective-permute-start | bytes 393224 | tf_op jit(solution)/shard_map/ppermute | solution.py:36
  8.9 8.8 %stage_and_sum.1 = (bf16[320,128,128]{2,1,0:T(8,128)(2,1)S(1)}, f32[64,4096]{1,0:T(8,128)S(1)}, s32[32,32]{1,0:T(8,128)S(1)}, s32[72]{0:T(128)S(1)}) custom-call(s32[2]{0:T(128)S(1)} %pad_add_fusion.place, s32[2,8]{1,0:T(2,128)} %send.3, s32[10,32]{1,0:T(8,128)} %bitcast.8, bf16[320,128,128]{2,1,0:T(8,128)(2,1)} %bitcast.6, ...), custom_call_target="tpu_custom_call" | custom-call | flops 671088640 | bytes 10485760 | tf_op jit(solution)/shard_map/stage_and_sum/pallas_call | solution.py:195
  17.8 1.8 %next_lists_1.1 = (bf16[64,1024]{1,0:T(8,128)(2,1)S(1)}, bf16[64,1024]{1,0:T(8,128)(2,1)S(1)}) custom-call(s32[2]{0:T(128)S(1)} %pad_add_fusion.place, s32[32,32]{1,0:T(8,128)S(1)} %get-tuple-element.21.table, s32[72]{0:T(128)S(1)} %get-tuple-element.23.order, f32[1]{0:T(128)S(6)} %copy.8.lower, f32[1]{0:T(128)S(6)} %copy.9.upper, ...), custom_call_target="tpu_custom_call" | custom-call | tf_op jit(solution)/shard_map/next_lists_1/pallas_call | solution.py:308
  19.6 4.3 %collective-permute-start.3 = (bf16[64,1024]{1,0:T(8,128)(2,1)S(1)}, bf16[64,1024]{1,0:T(8,128)(2,1)S(1)}, u32[]{:S(2)}, u32[]{:S(2)}) collective-permute-start(bf16[64,1024]{1,0:T(8,128)(2,1)S(1)} %get-tuple-element.27.new_far), channel_id=1, source_target_pairs={{2,4},{6,8},{10,12},{14,16},{18,20},{22,24},{26,28},{30,32},{34,36... | collective-permute-start | bytes 393224 | tf_op jit(solution)/shard_map/ppermute | solution.py:36
  24.0 2.7 %next_level_1.1.rest_0_.field = bf16[64,4096]{1,0:T(8,128)(2,1)S(1)} custom-call(s32[2]{0:T(128)S(1)} %pad_add_fusion.place, s32[32,32]{1,0:T(8,128)S(1)} %get-tuple-element.21.table, s32[72]{0:T(128)S(1)} %get-tuple-element.23.order, f32[1]{0:T(128)S(6)} %copy.8.lower, f32[1]{0:T(128)S(6)} %copy.9.upper, ...), custom_call_target="tpu_custom_call" | custom-call | flops 335544320 | bytes 10485760 | tf_op jit(solution)/shard_map/next_level_1/pallas_call | solution.py:349
  26.7 2.8 %local_sums_2.1.total = f32[64,4096]{1,0:T(8,128)S(1)} custom-call(s32[32,32]{1,0:T(8,128)S(1)} %get-tuple-element.21.table, bf16[320,128,128]{2,1,0:T(8,128)(2,1)S(1)} %get-tuple-element.22.tiles, bf16[64,4096]{1,0:T(8,128)(2,1)S(1)} %next_level_1.1.rest_0_.field), custom_call_target="tpu_custom_call" | custom-call | flops 41943040 | tf_op jit(solution)/shard_map/local_sums_2/pallas_call | solution.py:236
  29.5 3.4 %last_level.1 = (bf16[64,2560]{1,0:T(8,128)(2,1)S(1)}, bf16[64,1536]{1,0:T(8,128)(2,1)S(1)}, bf16[64,1024]{1,0:T(8,128)(2,1)S(1)}, bf16[64,1024]{1,0:T(8,128)(2,1)S(1)}) custom-call(s32[2]{0:T(128)S(1)} %pad_add_fusion.place, s32[32,32]{1,0:T(8,128)S(1)} %get-tuple-element.21.table, s32[2,8]{1,0:T(2,128)S(1)} %copy-done, f32[1]{0:T(128)S(6)} %copy.8.lower, ...), custom_call_target="tpu_custom_call" | custom-call | tf_op jit(solution)/shard_map/last_level/pallas_call | solution.py:392
  33.0 1.0 %collective-permute-start.6 = (bf16[64,1024]{1,0:T(8,128)(2,1)S(1)}, bf16[64,1024]{1,0:T(8,128)(2,1)S(1)}, u32[]{:S(2)}, u32[]{:S(2)}) collective-permute-start(bf16[64,1024]{1,0:T(8,128)(2,1)S(1)} %get-tuple-element.31), channel_id=1, source_target_pairs={{0,2},{2,0},{1,3},{3,1},{4,6},{6,4},{5,7},{7,5},{8,10},{10,8},{9,1... | collective-permute-start | bytes 393224 | tf_op jit(solution)/shard_map/ppermute | solution.py:30
  34.0 3.4 %collective-permute-start.7 = (bf16[64,1024]{1,0:T(8,128)(2,1)S(1)}, bf16[64,1024]{1,0:T(8,128)(2,1)S(1)}, u32[]{:S(2)}, u32[]{:S(2)}) collective-permute-start(bf16[64,1024]{1,0:T(8,128)(2,1)S(1)} %get-tuple-element.32), channel_id=1, source_target_pairs={{2,4},{6,8},{10,12},{14,16},{18,20},{22,24},{26,28},{30,32},{34,36... | collective-permute-start | bytes 393224 | tf_op jit(solution)/shard_map/ppermute | solution.py:36
  37.7 2.8 %local_sums_3.1.total = f32[64,4096]{1,0:T(8,128)S(1)} custom-call(s32[32,32]{1,0:T(8,128)S(1)} %get-tuple-element.21.table, bf16[320,128,128]{2,1,0:T(8,128)(2,1)S(1)} %get-tuple-element.22.tiles, bf16[64,2560]{1,0:T(8,128)(2,1)S(1)} %get-tuple-element.29.rest_0_.own_first, bf16[64,1536]{1,0:T(8,128)(2,1)S(1)} %get-tuple-element.30.rest_1_.own_second), custom_call_target="tpu_custom_call" | custom-call | flops 41943040 | tf_op jit(solution)/shard_map/local_sums_3/pallas_call | solution.py:236
  40.5 3.0 %image_rows.1.image = bf16[64,4096]{1,0:T(8,128)(2,1)S(1)} custom-call(s32[2]{0:T(128)S(1)} %pad_add_fusion.place, s32[32,32]{1,0:T(8,128)S(1)} %get-tuple-element.21.table, bf16[320,128,128]{2,1,0:T(8,128)(2,1)S(1)} %get-tuple-element.22.tiles, f32[64,4096]{1,0:T(8,128)S(1)} %local_sums_3.1.total, bf16[64,1024]{1,0:T(8,128)(2,1)S(1)} %collective-permute-done.6.near, ...), custom_call_target="tpu_custom_call" | custom-call | flops 1000000000 | tf_op jit(solution)/shard_map/image_rows/pallas_call | solution.py:423
  43.5 2.1 %collective-permute-done.5.second = bf16[64,1536]{1,0:T(8,128)(2,1)S(1)} collective-permute-done((bf16[64,1536]{1,0:T(8,128)(2,1)S(1)}, bf16[64,1536]{1,0:T(8,128)(2,1)S(1)}, u32[]{:S(2)}, u32[]{:S(2)}) %collective-permute-start.5) | collective-permute-done | bytes 196640 | tf_op jit(solution)/shard_map/ppermute | solution.py:30
  45.6 1.1 %partial_sums.1 = (f32[64,128]{1,0:T(8,128)S(1)}, f32[64,128]{1,0:T(8,128)S(1)}, bf16[128,4096]{1,0:T(8,128)(2,1)S(1)}) custom-call(s32[2]{0:T(128)S(1)} %pad_add_fusion.place, bf16[64,2560]{1,0:T(8,128)(2,1)S(1)} %get-tuple-element.29.rest_0_.own_first, bf16[64,1536]{1,0:T(8,128)(2,1)S(1)} %get-tuple-element.30.rest_1_.own_second, ...), custom_call_target="tpu_custom_call" | custom-call | tf_op jit(solution)/shard_map/partial_sums/pallas_call | solution.py:457
  46.7 1.8 %collective-permute-start.8 = (f32[64,128]{1,0:T(8,128)S(1)}, f32[64,128]{1,0:T(8,128)S(1)}, u32[]{:S(2)}, u32[]{:S(2)}) collective-permute-start(f32[64,128]{1,0:T(8,128)S(1)} %get-tuple-element.34), channel_id=1, source_target_pairs={{0,2},{2,0},{1,3},{3,1},{4,6},{6,4},{5,7},{7,5},{8,10},{10,8},{9,1... | collective-permute-start | bytes 98312 | tf_op jit(solution)/shard_map/ppermute | solution.py:30
  48.5 0.9 collective-permute-done.8
  49.3 3.0 %collective-permute-start.11 = (f32[64,128]{1,0:T(8,128)S(1)}, f32[64,128]{1,0:T(8,128)S(1)}, u32[]{:S(2)}, u32[]{:S(2)}) collective-permute-start(f32[64,128]{1,0:T(8,128)S(1)} %add.30), channel_id=1, source_target_pairs={{0,32},{16,48},{32,0},{48,16},{1,33},{17,49},{33,1},{49,17},{2,34}... | collective-permute-start | bytes 98312 | tf_op jit(solution)/shard_map/ppermute | solution.py:30
  52.3 0.7 collective-permute-start.10
  53.0 0.6 collective-permute-done.11
  53.6 2.7 %collective-permute-done.10 = f32[64,128]{1,0:T(8,128)S(1)} collective-permute-done((f32[64,128]{1,0:T(8,128)S(1)}, f32[64,128]{1,0:T(8,128)S(1)}, u32[]{:S(2)}, u32[]{:S(2)}) %collective-permute-start.10) | collective-permute-done | bytes 32800 | tf_op jit(solution)/shard_map/ppermute | solution.py:30
  56.3 2.2 %collective-permute-start.14 = (f32[64,128]{1,0:T(8,128)S(1)}, f32[64,128]{1,0:T(8,128)S(1)}, u32[]{:S(2)}, u32[]{:S(2)}) collective-permute-start(f32[64,128]{1,0:T(8,128)S(1)} %add_add_fusion.2), channel_id=1, source_target_pairs={{0,8},{4,12},{8,0},{12,4},{1,9},{5,13},{9,1},{13,5},{2,10},{6,14},... | collective-permute-start | bytes 98312 | tf_op jit(solution)/shard_map/ppermute | solution.py:30
  58.5 6.4 %collective-permute-start.13 = (f32[64,128]{1,0:T(8,128)S(1)}, f32[64,128]{1,0:T(8,128)S(1)}, u32[]{:S(2)}, u32[]{:S(2)}) collective-permute-start(f32[64,128]{1,0:T(8,128)S(1)} %add_add_fusion.2), channel_id=1, source_target_pairs={{0,12},{4,8},{8,4},{12,0},{1,13},{5,9},{9,5},{13,1},{2,14},{6,10},... | collective-permute-start | bytes 98312 | tf_op jit(solution)/shard_map/ppermute | solution.py:30
  65.3 0.8 collective-permute-done.13
  66.2 1.8 %collective-permute-done.12 = f32[64,128]{1,0:T(8,128)S(1)} collective-permute-done((f32[64,128]{1,0:T(8,128)S(1)}, f32[64,128]{1,0:T(8,128)S(1)}, u32[]{:S(2)}, u32[]{:S(2)}) %collective-permute-start.12) | collective-permute-done | bytes 32800 | tf_op jit(solution)/shard_map/ppermute | solution.py:30
  67.9 10.0 %collective-permute-start.17 = (f32[64,128]{1,0:T(8,128)S(1)}, f32[64,128]{1,0:T(8,128)S(1)}, u32[]{:S(2)}, u32[]{:S(2)}) collective-permute-start(f32[64,128]{1,0:T(8,128)S(1)} %add_add_fusion.1), channel_id=1, source_target_pairs={{0,128},{64,192},{128,0},{192,64},{1,129},{65,193},{129,1},{193,65... | collective-permute-start | bytes 98312 | tf_op jit(solution)/shard_map/ppermute | solution.py:30
  77.9 0.8 collective-permute-start.15
  79.2 3.6 %collective-permute-done.16 = f32[64,128]{1,0:T(8,128)S(1)} collective-permute-done((f32[64,128]{1,0:T(8,128)S(1)}, f32[64,128]{1,0:T(8,128)S(1)}, u32[]{:S(2)}, u32[]{:S(2)}) %collective-permute-start.16) | collective-permute-done | bytes 32800 | tf_op jit(solution)/shard_map/ppermute | solution.py:30
  82.8 3.8 %collective-permute-start.20 = (f32[64,128]{1,0:T(8,128)S(1)}, f32[64,128]{1,0:T(8,128)S(1)}, u32[]{:S(2)}, u32[]{:S(2)}) collective-permute-start(f32[64,128]{1,0:T(8,128)S(1)} %add_add_fusion.own), channel_id=1, source_target_pairs={{0,3},{1,2},{2,1},{3,0},{4,7},{5,6},{6,5},{7,4},{8,11},{9,10},{10,... | collective-permute-start | bytes 98312 | tf_op jit(solution)/shard_map/ppermute | solution.py:30
  86.6 1.7 %collective-permute-start.19 = (f32[64,128]{1,0:T(8,128)S(1)}, f32[64,128]{1,0:T(8,128)S(1)}, u32[]{:S(2)}, u32[]{:S(2)}) collective-permute-start(f32[64,128]{1,0:T(8,128)S(1)} %add_add_fusion.own), channel_id=1, source_target_pairs={{0,1},{1,0},{2,3},{3,2},{4,5},{5,4},{6,7},{7,6},{8,9},{9,8},{10,11... | collective-permute-start | bytes 98312 | tf_op jit(solution)/shard_map/ppermute | solution.py:30
  88.3 2.0 %collective-permute-done.19.other_mode = f32[64,128]{1,0:T(8,128)S(1)} collective-permute-done((f32[64,128]{1,0:T(8,128)S(1)}, f32[64,128]{1,0:T(8,128)S(1)}, u32[]{:S(2)}, u32[]{:S(2)}) %collective-permute-start.19) | collective-permute-done | bytes 32800 | tf_op jit(solution)/shard_map/ppermute | solution.py:30
  90.4 7.5 %factor_and_project.1 = (bf16[64,4096]{1,0:T(8,128)(2,1)}, f32[128,128]{1,0:T(8,128)}) custom-call(s32[2]{0:T(128)S(1)} %pad_add_fusion.place, f32[64,128]{1,0:T(8,128)S(1)} %add_add_fusion.own, f32[64,128]{1,0:T(8,128)S(1)} %collective-permute-done.18.other_core, f32[64,128]{1,0:T(8,128)S(1)} %collective-permute-done.19.other_mode, ...), custom_call_target="tpu_custom_call" | custom-call | tf_op jit(solution)/shard_map/factor_and_project/pallas_call | solution.py:545
  (27 shorter events, 1.7 us)
Async XLA Ops:
  2.4 15.4 %collective-permute-start = (bf16[64,1024]{1,0:T(8,128)(2,1)S(1)}, bf16[64,1024]{1,0:T(8,128)(2,1)S(1)}, u32[]{:S(2)}, u32[]{:S(2)}) collective-permute-start(bf16[64,1024]{1,0:T(8,128)(2,1)S(1)} %get-tuple-element.25), channel_id=1, source_target_pairs={{0,2},{2,0},{1,3},{3,1},{4,6},{6,4},{5,7},{7,5},{8,10},{10,8},{9,1... | collective-permute-start | bytes 393224 | tf_op jit(solution)/shard_map/ppermute | solution.py:30
  5.7 12.1 %collective-permute-start.1 = (bf16[64,1024]{1,0:T(8,128)(2,1)S(1)}, bf16[64,1024]{1,0:T(8,128)(2,1)S(1)}, u32[]{:S(2)}, u32[]{:S(2)}) collective-permute-start(bf16[64,1024]{1,0:T(8,128)(2,1)S(1)} %get-tuple-element.26), channel_id=1, source_target_pairs={{2,4},{6,8},{10,12},{14,16},{18,20},{22,24},{26,28},{30,32},{34,36... | collective-permute-start | bytes 393224 | tf_op jit(solution)/shard_map/ppermute | solution.py:36
  19.6 9.8 %collective-permute-start.3 = (bf16[64,1024]{1,0:T(8,128)(2,1)S(1)}, bf16[64,1024]{1,0:T(8,128)(2,1)S(1)}, u32[]{:S(2)}, u32[]{:S(2)}) collective-permute-start(bf16[64,1024]{1,0:T(8,128)(2,1)S(1)} %get-tuple-element.27.new_far), channel_id=1, source_target_pairs={{2,4},{6,8},{10,12},{14,16},{18,20},{22,24},{26,28},{30,32},{34,36... | collective-permute-start | bytes 393224 | tf_op jit(solution)/shard_map/ppermute | solution.py:36
  23.9 5.6 %copy-start = (s32[2,8]{1,0:T(2,128)S(1)}, s32[2,8]{1,0:T(2,128)}, u32[]{:S(2)}) copy-start(s32[2,8]{1,0:T(2,128)} %send.3) | copy-start | bytes 196
  23.9 5.6 %collective-permute-start.2 = (bf16[64,1024]{1,0:T(8,128)(2,1)S(1)}, bf16[64,1024]{1,0:T(8,128)(2,1)S(1)}, u32[]{:S(2)}, u32[]{:S(2)}) collective-permute-start(bf16[64,1024]{1,0:T(8,128)(2,1)S(1)} %get-tuple-element.28.new_near), channel_id=1, source_target_pairs={{0,2},{2,0},{1,3},{3,1},{4,6},{6,4},{5,7},{7,5},{8,10},{10,8},{9,1... | collective-permute-start | bytes 393224 | tf_op jit(solution)/shard_map/ppermute | solution.py:30
  32.9 12.7 %collective-permute-start.4 = (bf16[64,2560]{1,0:T(8,128)(2,1)S(1)}, bf16[64,2560]{1,0:T(8,128)(2,1)S(1)}, u32[]{:S(2)}, u32[]{:S(2)}) collective-permute-start(bf16[64,2560]{1,0:T(8,128)(2,1)S(1)} %get-tuple-element.29.rest_0_.own_first), channel_id=1, source_target_pairs={{0,1},{1,0},{2,3},{3,2},{4,5},{5,4},{6,7},{7,6},{8,9},{9,8},{10,11... | collective-permute-start | bytes 983048 | tf_op jit(solution)/shard_map/ppermute | solution.py:30
  33.0 7.5 %collective-permute-start.6 = (bf16[64,1024]{1,0:T(8,128)(2,1)S(1)}, bf16[64,1024]{1,0:T(8,128)(2,1)S(1)}, u32[]{:S(2)}, u32[]{:S(2)}) collective-permute-start(bf16[64,1024]{1,0:T(8,128)(2,1)S(1)} %get-tuple-element.31), channel_id=1, source_target_pairs={{0,2},{2,0},{1,3},{3,1},{4,6},{6,4},{5,7},{7,5},{8,10},{10,8},{9,1... | collective-permute-start | bytes 393224 | tf_op jit(solution)/shard_map/ppermute | solution.py:30
  34.0 6.6 %collective-permute-start.7 = (bf16[64,1024]{1,0:T(8,128)(2,1)S(1)}, bf16[64,1024]{1,0:T(8,128)(2,1)S(1)}, u32[]{:S(2)}, u32[]{:S(2)}) collective-permute-start(bf16[64,1024]{1,0:T(8,128)(2,1)S(1)} %get-tuple-element.32), channel_id=1, source_target_pairs={{2,4},{6,8},{10,12},{14,16},{18,20},{22,24},{26,28},{30,32},{34,36... | collective-permute-start | bytes 393224 | tf_op jit(solution)/shard_map/ppermute | solution.py:36
  37.4 8.2 %collective-permute-start.5 = (bf16[64,1536]{1,0:T(8,128)(2,1)S(1)}, bf16[64,1536]{1,0:T(8,128)(2,1)S(1)}, u32[]{:S(2)}, u32[]{:S(2)}) collective-permute-start(bf16[64,1536]{1,0:T(8,128)(2,1)S(1)} %get-tuple-element.30.rest_1_.own_second), channel_id=1, source_target_pairs={{0,1},{1,0},{2,3},{3,2},{4,5},{5,4},{6,7},{7,6},{8,9},{9,8},{10,11... | collective-permute-start | bytes 589832 | tf_op jit(solution)/shard_map/ppermute | solution.py:30
  46.7 2.7 %collective-permute-start.8 = (f32[64,128]{1,0:T(8,128)S(1)}, f32[64,128]{1,0:T(8,128)S(1)}, u32[]{:S(2)}, u32[]{:S(2)}) collective-permute-start(f32[64,128]{1,0:T(8,128)S(1)} %get-tuple-element.34), channel_id=1, source_target_pairs={{0,2},{2,0},{1,3},{3,1},{4,6},{6,4},{5,7},{7,5},{8,10},{10,8},{9,1... | collective-permute-start | bytes 98312 | tf_op jit(solution)/shard_map/ppermute | solution.py:30
  49.3 4.3 %collective-permute-start.11 = (f32[64,128]{1,0:T(8,128)S(1)}, f32[64,128]{1,0:T(8,128)S(1)}, u32[]{:S(2)}, u32[]{:S(2)}) collective-permute-start(f32[64,128]{1,0:T(8,128)S(1)} %add.30), channel_id=1, source_target_pairs={{0,32},{16,48},{32,0},{48,16},{1,33},{17,49},{33,1},{49,17},{2,34}... | collective-permute-start | bytes 98312 | tf_op jit(solution)/shard_map/ppermute | solution.py:30
  52.3 4.0 %collective-permute-start.10 = (f32[64,128]{1,0:T(8,128)S(1)}, f32[64,128]{1,0:T(8,128)S(1)}, u32[]{:S(2)}, u32[]{:S(2)}) collective-permute-start(f32[64,128]{1,0:T(8,128)S(1)} %add.30), channel_id=1, source_target_pairs={{0,48},{16,32},{32,16},{48,0},{1,49},{17,33},{33,17},{49,1},{2,50}... | collective-permute-start | bytes 98312 | tf_op jit(solution)/shard_map/ppermute | solution.py:30
  53.0 3.3 %collective-permute-start.9 = (f32[64,128]{1,0:T(8,128)S(1)}, f32[64,128]{1,0:T(8,128)S(1)}, u32[]{:S(2)}, u32[]{:S(2)}) collective-permute-start(f32[64,128]{1,0:T(8,128)S(1)} %add.30), channel_id=1, source_target_pairs={{0,16},{16,0},{32,48},{48,32},{1,17},{17,1},{33,49},{49,33},{2,18}... | collective-permute-start | bytes 98312 | tf_op jit(solution)/shard_map/ppermute | solution.py:30
  56.3 9.0 %collective-permute-start.14 = (f32[64,128]{1,0:T(8,128)S(1)}, f32[64,128]{1,0:T(8,128)S(1)}, u32[]{:S(2)}, u32[]{:S(2)}) collective-permute-start(f32[64,128]{1,0:T(8,128)S(1)} %add_add_fusion.2), channel_id=1, source_target_pairs={{0,8},{4,12},{8,0},{12,4},{1,9},{5,13},{9,1},{13,5},{2,10},{6,14},... | collective-permute-start | bytes 98312 | tf_op jit(solution)/shard_map/ppermute | solution.py:30
  58.5 7.7 %collective-permute-start.13 = (f32[64,128]{1,0:T(8,128)S(1)}, f32[64,128]{1,0:T(8,128)S(1)}, u32[]{:S(2)}, u32[]{:S(2)}) collective-permute-start(f32[64,128]{1,0:T(8,128)S(1)} %add_add_fusion.2), channel_id=1, source_target_pairs={{0,12},{4,8},{8,4},{12,0},{1,13},{5,9},{9,5},{13,1},{2,14},{6,10},... | collective-permute-start | bytes 98312 | tf_op jit(solution)/shard_map/ppermute | solution.py:30
  64.9 3.1 %collective-permute-start.12 = (f32[64,128]{1,0:T(8,128)S(1)}, f32[64,128]{1,0:T(8,128)S(1)}, u32[]{:S(2)}, u32[]{:S(2)}) collective-permute-start(f32[64,128]{1,0:T(8,128)S(1)} %add_add_fusion.2), channel_id=1, source_target_pairs={{0,4},{4,0},{8,12},{12,8},{1,5},{5,1},{9,13},{13,9},{2,6},{6,2},{1... | collective-permute-start | bytes 98312 | tf_op jit(solution)/shard_map/ppermute | solution.py:30
  67.9 11.3 %collective-permute-start.17 = (f32[64,128]{1,0:T(8,128)S(1)}, f32[64,128]{1,0:T(8,128)S(1)}, u32[]{:S(2)}, u32[]{:S(2)}) collective-permute-start(f32[64,128]{1,0:T(8,128)S(1)} %add_add_fusion.1), channel_id=1, source_target_pairs={{0,128},{64,192},{128,0},{192,64},{1,129},{65,193},{129,1},{193,65... | collective-permute-start | bytes 98312 | tf_op jit(solution)/shard_map/ppermute | solution.py:30
  77.9 4.9 %collective-permute-start.16 = (f32[64,128]{1,0:T(8,128)S(1)}, f32[64,128]{1,0:T(8,128)S(1)}, u32[]{:S(2)}, u32[]{:S(2)}) collective-permute-start(f32[64,128]{1,0:T(8,128)S(1)} %add_add_fusion.1), channel_id=1, source_target_pairs={{0,192},{64,128},{128,64},{192,0},{1,193},{65,129},{129,65},{193,1... | collective-permute-start | bytes 98312 | tf_op jit(solution)/shard_map/ppermute | solution.py:30
  77.9 4.9 %collective-permute-start.15 = (f32[64,128]{1,0:T(8,128)S(1)}, f32[64,128]{1,0:T(8,128)S(1)}, u32[]{:S(2)}, u32[]{:S(2)}) collective-permute-start(f32[64,128]{1,0:T(8,128)S(1)} %add_add_fusion.1), channel_id=1, source_target_pairs={{0,64},{64,0},{128,192},{192,128},{1,65},{65,1},{129,193},{193,129... | collective-permute-start | bytes 98312 | tf_op jit(solution)/shard_map/ppermute | solution.py:30
  82.8 5.5 %collective-permute-start.20 = (f32[64,128]{1,0:T(8,128)S(1)}, f32[64,128]{1,0:T(8,128)S(1)}, u32[]{:S(2)}, u32[]{:S(2)}) collective-permute-start(f32[64,128]{1,0:T(8,128)S(1)} %add_add_fusion.own), channel_id=1, source_target_pairs={{0,3},{1,2},{2,1},{3,0},{4,7},{5,6},{6,5},{7,4},{8,11},{9,10},{10,... | collective-permute-start | bytes 98312 | tf_op jit(solution)/shard_map/ppermute | solution.py:30
  86.6 3.7 %collective-permute-start.19 = (f32[64,128]{1,0:T(8,128)S(1)}, f32[64,128]{1,0:T(8,128)S(1)}, u32[]{:S(2)}, u32[]{:S(2)}) collective-permute-start(f32[64,128]{1,0:T(8,128)S(1)} %add_add_fusion.own), channel_id=1, source_target_pairs={{0,1},{1,0},{2,3},{3,2},{4,5},{5,4},{6,7},{7,6},{8,9},{9,8},{10,11... | collective-permute-start | bytes 98312 | tf_op jit(solution)/shard_map/ppermute | solution.py:30
  88.3 2.0 %collective-permute-start.18 = (f32[64,128]{1,0:T(8,128)S(1)}, f32[64,128]{1,0:T(8,128)S(1)}, u32[]{:S(2)}, u32[]{:S(2)}) collective-permute-start(f32[64,128]{1,0:T(8,128)S(1)} %add_add_fusion.own), channel_id=1, source_target_pairs={{0,2},{2,0},{1,3},{3,1},{4,6},{6,4},{5,7},{7,5},{8,10},{10,8},{9,1... | collective-permute-start | bytes 98312 | tf_op jit(solution)/shard_map/ppermute | solution.py:30
